TPU v7x, 32 devices: a whole 2x2x4 slice. The times are simulated.
32 devices in a mesh: groups: 2 (over y), frame: 8 (over z, x), head: 2 (over core).
Axes of the slice: x: 2, y: 2, z: 4, core: 2. Of those that a mesh axis runs over, the one named last changes fastest.
Arguments:
- head_queries: bfloat16 [4096, 1536], P(('groups', 'frame'), 'head'), parts along dimension 0, may hold values from -10 to 10
- head_keys: bfloat16 [4096, 1536], P(('groups', 'frame'), 'head'), parts along dimension 0, may hold values from -10 to 10
- head_values: bfloat16 [4096, 1536], P(('groups', 'frame'), 'head'), parts along dimension 0, may hold values from -18 to 18
- out_weight: bfloat16 [1536, 3072], P('head', 'frame'), may hold values from -0.15625 to 0.15625
- head_class: int32 [12], P('head'), may hold values from 0 to 1, as said below
- block_lists: int32 [12, 16, 4, 2], P('head', ('groups', 'frame')), parts along dimension 1, may hold values from 0 to 3, as said below
- block_counts: int32 [12, 16, 4], P('head', ('groups', 'frame')), parts along dimension 1, may hold values from 1 to 2, as said below
Outputs:
- projected: bfloat16 [4096, 3072], P(('groups', 'frame', 'head')), parts along dimension 0
There are 2 independent parts, one for each index of `groups`. A program takes and returns all parts, laid end to end along the dimension named above; an argument that names none is the same for every part. Nothing has to cross between parts.
Inputs may be any that keep to these rules, and one draw needn't show every extreme that they name: `head_class`: for each j from 0 to 1, exactly half of the heads j * 6 to (j + 1) * 6 - 1 are temporal. block_lists[h, g, b, 0] equals b, and the entries of one list are distinct. `block_counts`: for each head and sequence some query block uses all 2 entries.
All inputs are finite; a program needn't handle non-finite values.
Results may differ from a plain program's by a relative error of at most 0.0062.
Values may be sent and summed in bfloat16 or wider, within the bound.
No kernel may reach another device: no remote copies, remote signals or barrier semaphores. Data moves between devices by JAX's collectives and lax.ppermute only.
A program may use at most 64 MiB of HBM per device.

v0:
```python
import jax
import jax.numpy as jnp
from jax import lax
from jax.sharding import PartitionSpec as P


def dense_head(queries_h, keys_h, values_h, block_ids, counts):
    block_count = block_ids.shape[0]
    listed_most = block_ids.shape[1]
    block_rows = queries_h.shape[0] // block_count
    usable = jnp.arange(listed_most)[None, :] < counts[:, None]
    linked = jnp.any(
        usable[:, :, None] & (block_ids[:, :, None] == jnp.arange(block_count)[None, None, :]),
        axis=1,
    )
    allowed = jnp.repeat(jnp.repeat(linked, block_rows, axis=0), block_rows, axis=1)
    scores = jnp.dot(queries_h, keys_h.T, preferred_element_type=jnp.float32) * queries_h.shape[
        1
    ] ** (-0.5)
    scores = jnp.where(allowed, scores, -jnp.inf)
    row_max = jnp.max(scores, axis=1, keepdims=True)
    weights = jnp.exp(scores - row_max)
    denominator = jnp.sum(weights, axis=1, keepdims=True)
    rounded = weights.astype(jnp.bfloat16)
    result = jnp.dot(rounded, values_h, preferred_element_type=jnp.float32) / denominator
    return result.astype(jnp.bfloat16)


def attend_heads(queries_h, keys_h, values_h, block_ids, counts):

    def single(inputs):
        return dense_head(*inputs)

    stacked = lax.map(
        single,
        (
            queries_h.transpose(1, 0, 2),
            keys_h.transpose(1, 0, 2),
            values_h.transpose(1, 0, 2),
            block_ids,
            counts,
        ),
    )
    return stacked.transpose(1, 0, 2)


def on_device(
    head_queries, head_keys, head_values, out_weight, head_class, block_lists, block_counts
):
    pixels = head_queries.shape[0]
    local_heads = head_class.shape[0]
    half_heads = local_heads // 2
    head_width = head_queries.shape[1] // local_heads
    groups = lax.axis_size("frame")
    head_order = jnp.argsort(head_class, stable=True)
    inverse = jnp.argsort(head_order)
    spatial_ids = head_order[:half_heads]
    temporal_ids = head_order[half_heads:]
    block_ids = block_lists[:, 0]
    counts = block_counts[:, 0]

    def split_heads(tensor, chosen):
        return jnp.take(tensor.reshape(pixels, local_heads, head_width), chosen, axis=1)

    temporal_q = split_heads(head_queries, temporal_ids).reshape(1, pixels, half_heads * head_width)
    temporal_k = split_heads(head_keys, temporal_ids).reshape(1, pixels, half_heads * head_width)
    temporal_v = split_heads(head_values, temporal_ids).reshape(1, pixels, half_heads * head_width)
    arrived = (
        lax.all_to_all(temporal_q, "frame", split_axis=1, concat_axis=0, tiled=True),
        lax.all_to_all(temporal_k, "frame", split_axis=1, concat_axis=0, tiled=True),
        lax.all_to_all(temporal_v, "frame", split_axis=1, concat_axis=0, tiled=True),
    )
    spatial = attend_heads(
        split_heads(head_queries, spatial_ids),
        split_heads(head_keys, spatial_ids),
        split_heads(head_values, spatial_ids),
        block_ids[spatial_ids],
        counts[spatial_ids],
    )
    temporal = attend_heads(
        arrived[0].reshape(pixels, half_heads, head_width),
        arrived[1].reshape(pixels, half_heads, head_width),
        arrived[2].reshape(pixels, half_heads, head_width),
        block_ids[temporal_ids],
        counts[temporal_ids],
    )
    returned = lax.all_to_all(
        temporal.reshape(groups, pixels // groups, half_heads * head_width),
        "frame",
        split_axis=0,
        concat_axis=1,
        tiled=True,
    )
    joined = jnp.concatenate([spatial, returned.reshape(pixels, half_heads, head_width)], axis=1)
    attended = jnp.take(joined, inverse, axis=1).reshape(pixels, local_heads * head_width)
    partial_out = jnp.dot(
        attended,
        lax.all_gather(out_weight, "frame", axis=1, tiled=True),
        preferred_element_type=jnp.float32,
    )
    projected = lax.psum_scatter(
        partial_out.astype(jnp.bfloat16), "head", scatter_dimension=0, tiled=True
    )
    return projected


def solution(mesh):
    placed = (
        P(("groups", "frame"), "head"),
        P(("groups", "frame"), "head"),
        P(("groups", "frame"), "head"),
        P("head", "frame"),
        P("head"),
        P("head", ("groups", "frame"), None, None),
        P("head", ("groups", "frame"), None),
    )
    return jax.shard_map(
        on_device,
        mesh=mesh,
        in_specs=placed,
        out_specs=P(("groups", "frame", "head"), None),
        check_vma=False,
    )
```

profile of v0, /device:TPU:0, one launch (start us, length us, event | category | flops | bytes accessed | tf_op | source)
XLA Modules:
  0.0 125.5 jit_solution(15839549879468988712)
XLA Ops:
  7.3 1.6 %sort.34 = (s32[6]{0:T(128)}, s32[6]{0:T(128)S(1)}) sort(s32[6]{0:T(128)} %param.17, s32[6]{0:T(128)S(1)} %iota.30), dimensions={0}, to_apply=%region_0.0 | sort | flops 18 | bytes 96 | tf_op jit(solution)/shard_map/jit(argsort)/sort | solution.py:55
  9.0 1.2 copy.101
  10.4 1.2 copy.103
  17.2 1.8 %reduce = bf16[256,384]{1,0:T(8,128)(2,1)S(1)} reduce(bf16[256,1,384]{2,1,0:T(2,128)(2,1)S(1)} %bitcast.137, bf16[]{:T(256)} %broadcast.192), dimensions={1}, to_apply=%bitcast.83.reduce_sub_computation | reduce | bytes 393218
  19.0 0.7 reshape.257
  19.7 7.3 %all-to-all-start = ((bf16[8,2,6144]{2,1,0:T(2,128)(2,1)}), bf16[8,2,6144]{2,1,0:T(2,128)(2,1)S(1)}, u32[]{:S(2)}, u32[]{:S(2)}) async-start(bf16[8,2,6144]{2,1,0:T(2,128)(2,1)} %reshape.257), calls=%async_computation | async-start | bytes 393216 | tf_op jit(solution)/shard_map/all_to_all | solution.py:69
  27.6 1.8 %reduce.1 = bf16[256,384]{1,0:T(8,128)(2,1)S(1)} reduce(bf16[256,1,384]{2,1,0:T(2,128)(2,1)S(1)} %bitcast.139, bf16[]{:T(256)} %broadcast.192), dimensions={1}, to_apply=%bitcast.85.reduce_sub_computation | reduce | bytes 393218
  29.5 0.7 reshape.259
  30.2 8.7 %all-to-all-done = bf16[8,2,6144]{2,1,0:T(2,128)(2,1)S(1)} async-done(((bf16[8,2,6144]{2,1,0:T(2,128)(2,1)}), bf16[8,2,6144]{2,1,0:T(2,128)(2,1)S(1)}, u32[]{:S(2)}, u32[]{:S(2)}) %all-to-all-start) | async-done | bytes 196640 | tf_op jit(solution)/shard_map/all_to_all | solution.py:69
  38.9 4.6 %all-to-all-start.1 = ((bf16[8,2,6144]{2,1,0:T(2,128)(2,1)}), bf16[8,2,6144]{2,1,0:T(2,128)(2,1)S(1)}, u32[]{:S(2)}, u32[]{:S(2)}) async-start(bf16[8,2,6144]{2,1,0:T(2,128)(2,1)} %reshape.259), calls=%async_computation.1 | async-start | bytes 393216 | tf_op jit(solution)/shard_map/all_to_all | solution.py:70
  45.5 1.8 %reduce.2 = bf16[256,384]{1,0:T(8,128)(2,1)S(1)} reduce(bf16[256,1,384]{2,1,0:T(2,128)(2,1)S(1)} %bitcast.138, bf16[]{:T(256)} %broadcast.192), dimensions={1}, to_apply=%bitcast.87.reduce_sub_computation | reduce | bytes 393218
  47.3 0.7 reshape.261
  48.1 5.5 %all-to-all-done.1 = bf16[8,2,6144]{2,1,0:T(2,128)(2,1)S(1)} async-done(((bf16[8,2,6144]{2,1,0:T(2,128)(2,1)}), bf16[8,2,6144]{2,1,0:T(2,128)(2,1)S(1)}, u32[]{:S(2)}, u32[]{:S(2)}) %all-to-all-start.1) | async-done | bytes 196640 | tf_op jit(solution)/shard_map/all_to_all | solution.py:70
  53.6 3.4 %all-to-all-start.2 = ((bf16[8,2,6144]{2,1,0:T(2,128)(2,1)}), bf16[8,2,6144]{2,1,0:T(2,128)(2,1)S(1)}, u32[]{:S(2)}, u32[]{:S(2)}) async-start(bf16[8,2,6144]{2,1,0:T(2,128)(2,1)} %reshape.261), calls=%async_computation.2 | async-start | bytes 393216 | tf_op jit(solution)/shard_map/all_to_all | solution.py:71
  57.0 3.0 %while.20 = (s32[]{:T(128)}, bf16[3,256,128]{2,1,0:T(8,128)(2,1)S(1)}, s32[3,4]{1,0:T(4,128)S(1)}, s32[3,4,2]{1,2,0:T(2,128)S(1)}, bf16[3,256,128]{2,1,0:T(8,128...) while((s32[]{:T(128)}, bf16[3,256,128]{2,1,0:T(8,128)(2,1)S(1)}, ...), condition=%wide.region_6.8_spmd, body=%wide.region_2.7_spmd.sunk | while | flops 34078296 | bytes 1191229 | solution.py:34
  61.2 0.9 sort.35
  63.4 7.5 %all-to-all-done.2 = bf16[8,2,6144]{2,1,0:T(2,128)(2,1)S(1)} async-done(((bf16[8,2,6144]{2,1,0:T(2,128)(2,1)}), bf16[8,2,6144]{2,1,0:T(2,128)(2,1)S(1)}, u32[]{:S(2)}, u32[]{:S(2)}) %all-to-all-start.2) | async-done | bytes 196640 | tf_op jit(solution)/shard_map/all_to_all | solution.py:71
  71.5 3.1 %while.21 = (s32[]{:T(128)}, bf16[3,256,128]{2,1,0:T(8,128)(2,1)S(1)}, s32[3,4]{1,0:T(4,128)S(1)}, s32[3,4,2]{1,2,0:T(2,128)S(1)}, bf16[3,256,128]{1,2,0:T(8,128...) while((s32[]{:T(128)}, ...), condition=%wide.region_11.13_spmd, body=%wide.region_7.12_spmd.sunk | while | flops 34078296 | bytes 1191229 | solution.py:34
  74.8 0.8 reshape.144
  75.7 3.4 %all-to-all-start.3 = ((bf16[8,32,384]{2,1,0:T(8,128)(2,1)}), bf16[8,32,384]{2,1,0:T(8,128)(2,1)S(1)}, u32[]{:S(2)}, u32[]{:S(2)}) async-start(bf16[8,32,384]{2,1,0:T(8,128)(2,1)} %reshape.144), calls=%async_computation.3 | async-start | bytes 393216 | tf_op jit(solution)/shard_map/all_to_all | solution.py:87
  79.3 9.9 %all-to-all-done.3 = bf16[8,32,384]{2,1,0:T(8,128)(2,1)S(1)} async-done(((bf16[8,32,384]{2,1,0:T(8,128)(2,1)}), bf16[8,32,384]{2,1,0:T(8,128)(2,1)S(1)}, u32[]{:S(2)}, u32[]{:S(2)}) %all-to-all-start.3) | async-done | bytes 196640 | tf_op jit(solution)/shard_map/all_to_all | solution.py:87
  90.3 14.7 %all-gather.2.cloned.1.call-done = bf16[768,3072]{1,0:T(8,128)(2,1)} async-done(((bf16[768,384]{1,0:T(8,128)(2,1)}), bf16[768,3072]{1,0:T(8,128)(2,1)}) %all-gather.2.cloned.1.call-update) | async-done | bytes 4718608 | tf_op jit(solution)/shard_map/all_gather | solution.py:98
  104.9 4.9 %convolution_convert_fusion = bf16[256,3072]{1,0:T(8,128)(2,1)} fusion(bf16[256,768]{0,1:T(8,128)(2,1)S(1)} %bitcast_select_fusion, bf16[768,3072]{1,0:T(8,128)(2,1)} %all-gather.2.cloned.1.call-done), kind=kOutput, calls=%fused_computation.63 | convolution fusion | flops 1208745984 | bytes 6684672 | tf_op jit(solution)/shard_map/dot_general | solution.py:96
  109.9 8.7 %reduce-scatter.2.cloned.1.call-done = bf16[128,3072]{1,0:T(8,128)(2,1)} async-done(((bf16[256,3072]{1,0:T(8,128)(2,1)}), bf16[128,3072]{1,0:T(8,128)(2,1)}) %reduce-scatter.2.cloned.1.call-update) | async-done | bytes 786448 | tf_op jit(solution)/shard_map/reduce_scatter | solution.py:101
  (125 shorter events, 19.3 us)
Async XLA Ops:
  6.5 7.6 %copy-start = (bf16[256,768]{1,0:T(8,128)(2,1)S(1)}, bf16[256,768]{1,0:T(8,128)(2,1)}, u32[]{:S(2)}) copy-start(bf16[256,768]{1,0:T(8,128)(2,1)} %param.15) | copy-start | bytes 1179652
  6.5 98.4 %all-gather.2.cloned.1.call-start = ((), (), s32[]{:S(2)}) async-start(), calls=%async_computation.5 | async-start | bytes 5308416 | tf_op jit(solution)/shard_map/all_gather | solution.py:98
  14.2 29.4 %copy-start.1 = (s32[6,1,4,2]{0,3,2,1:T(2,128)S(1)}, s32[6,1,4,2]{0,3,2,1:T(2,128)}, u32[]{:S(2)}) copy-start(s32[6,1,4,2]{0,3,2,1:T(2,128)} %param.18) | copy-start | bytes 580
  14.2 30.0 %copy-start.2 = (s32[6,1,4]{0,2,1:T(4,128)S(1)}, s32[6,1,4]{0,2,1:T(4,128)}, u32[]{:S(2)}) copy-start(s32[6,1,4]{0,2,1:T(4,128)} %param.19) | copy-start | bytes 292
  19.7 19.2 %all-to-all-start = ((bf16[8,2,6144]{2,1,0:T(2,128)(2,1)}), bf16[8,2,6144]{2,1,0:T(2,128)(2,1)S(1)}, u32[]{:S(2)}, u32[]{:S(2)}) async-start(bf16[8,2,6144]{2,1,0:T(2,128)(2,1)} %reshape.257), calls=%async_computation | async-start | bytes 393216 | tf_op jit(solution)/shard_map/all_to_all | solution.py:69
  38.9 14.7 %all-to-all-start.1 = ((bf16[8,2,6144]{2,1,0:T(2,128)(2,1)}), bf16[8,2,6144]{2,1,0:T(2,128)(2,1)S(1)}, u32[]{:S(2)}, u32[]{:S(2)}) async-start(bf16[8,2,6144]{2,1,0:T(2,128)(2,1)} %reshape.259), calls=%async_computation.1 | async-start | bytes 393216 | tf_op jit(solution)/shard_map/all_to_all | solution.py:70
  53.6 17.3 %all-to-all-start.2 = ((bf16[8,2,6144]{2,1,0:T(2,128)(2,1)}), bf16[8,2,6144]{2,1,0:T(2,128)(2,1)S(1)}, u32[]{:S(2)}, u32[]{:S(2)}) async-start(bf16[8,2,6144]{2,1,0:T(2,128)(2,1)} %reshape.261), calls=%async_computation.2 | async-start | bytes 393216 | tf_op jit(solution)/shard_map/all_to_all | solution.py:71
  75.7 13.5 %all-to-all-start.3 = ((bf16[8,32,384]{2,1,0:T(8,128)(2,1)}), bf16[8,32,384]{2,1,0:T(8,128)(2,1)S(1)}, u32[]{:S(2)}, u32[]{:S(2)}) async-start(bf16[8,32,384]{2,1,0:T(8,128)(2,1)} %reshape.144), calls=%async_computation.3 | async-start | bytes 393216 | tf_op jit(solution)/shard_map/all_to_all | solution.py:87
  79.1 39.5 %reduce-scatter.2.cloned.1.call-start = ((), (), s32[]{:S(2)}) async-start(), calls=%async_computation.6 | async-start | bytes 2359296 | tf_op jit(solution)/shard_map/reduce_scatter | solution.py:101
Sparse Core Ops, SparseCore 0:
  9.4 95.4 all-gather.1
  110.0 8.5 reduce-scatter.1
where the time goes:
time: 126 us; the launch traced here: 125 us
  waiting for transfers between devices  55.8 us (44%)
  local copies, waits for them, and re-layouts  19.5 us (15%)
  starting transfers between devices  18.7 us (15%)
  between operations  13.7 us (11%)
  other arithmetic  9.56 us (8%)
  matrix products  7.91 us (6%)
    all_gather x1, waiting for transfers between devices, on_device(): lax.all_gather(out_weight, 'frame', axis=1, tiled=True)  14.7 us
    all_to_all x1, waiting for transfers between devices, on_device(): lax.all_to_all(temporal.reshape(groups, pixels // groups, half_heads * he...  9.88 us
    reduce_scatter x1, waiting for transfers between devices, on_device(): lax.psum_scatter(partial_out.astype(jnp.bfloat16), 'head', scatter_dimens...  8.74 us
    all_to_all x1, waiting for transfers between devices, on_device(): lax.all_to_all(temporal_q, 'frame', split_axis=1, concat_axis=0, tiled=True)  8.72 us
    all_to_all x1, waiting for transfers between devices, on_device(): lax.all_to_all(temporal_v, 'frame', split_axis=1, concat_axis=0, tiled=True)  7.5 us
    all_to_all x1, starting transfers between devices, on_device(): lax.all_to_all(temporal_q, 'frame', split_axis=1, concat_axis=0, tiled=True)  7.25 us
    unnamed x17, local copies, waits for them, and re-layouts  5.83 us
    unnamed x3, other arithmetic  5.54 us
  transfers between devices with their start and end apart: 6, of which 6 were waited for; matrix products, arithmetic and copies ran while one was open for 25% of the time, Pallas kernels for 0%

commit v1 on v0

v1 whole, which is shorter than its diff:
```python
import functools

import jax
import jax.numpy as jnp
from jax import lax
from jax.experimental import pallas as pl
from jax.experimental.pallas import tpu as pltpu
from jax.sharding import PartitionSpec as P

VMEM = pl.BlockSpec(memory_space=pltpu.VMEM)
SMEM = pl.BlockSpec(memory_space=pltpu.SMEM)
PARAMS = pltpu.CompilerParams(vmem_limit_bytes=40 * 1024 * 1024)


def head_of_rank(class_ref, kind, rank, heads):
    found = jnp.int32(0)
    seen = jnp.int32(0)
    for head in range(heads):
        is_kind = class_ref[head] == kind
        found = jnp.where(is_kind & (seen == rank), head, found)
        seen = seen + is_kind.astype(jnp.int32)
    return found


def columns(index, width):
    return pl.ds(pl.multiple_of(index * width, width), width)


def pack_kernel(heads, width, class_ref, q_ref, k_ref, v_ref, packed_ref):
    half = heads // 2
    for rank in range(half):
        head = head_of_rank(class_ref, 1, rank, heads)
        for place, ref in enumerate((q_ref, k_ref, v_ref)):
            at = (place * half + rank) * width
            packed_ref[:, at : at + width] = ref[:, columns(head, width)]


def attend(queries, keys, values, listed, blocks):
    rows = queries.shape[0] // blocks
    scores = lax.dot_general(
        queries, keys, (((1,), (1,)), ((), ())), preferred_element_type=jnp.float32
    ) * (queries.shape[1] ** -0.5)
    key_block = lax.broadcasted_iota(jnp.int32, (rows, keys.shape[0]), 1) // rows
    masked = []
    for block in range(blocks):
        first, second = listed[block]
        allowed = (key_block == first) | (key_block == second)
        masked.append(
            jnp.where(allowed, scores[block * rows : (block + 1) * rows], -jnp.inf)
        )
    scores = jnp.concatenate(masked, axis=0)
    weights = jnp.exp(scores - jnp.max(scores, axis=1, keepdims=True))
    denominator = jnp.sum(weights, axis=1, keepdims=True)
    total = jnp.dot(
        weights.astype(jnp.bfloat16), values, preferred_element_type=jnp.float32
    )
    return (total / denominator).astype(jnp.bfloat16)


def listed_blocks(lists_ref, counts_ref, head, blocks):
    listed = []
    for block in range(blocks):
        first = lists_ref[head * 2 * blocks + 2 * block]
        second = lists_ref[head * 2 * blocks + 2 * block + 1]
        listed.append(
            (first, jnp.where(counts_ref[head * blocks + block] > 1, second, first))
        )
    return listed


def spatial_kernel(
    heads, width, blocks, class_ref, lists_ref, counts_ref, q_ref, k_ref, v_ref, out_ref
):
    for rank in range(heads // 2):
        head = head_of_rank(class_ref, 0, rank, heads)
        at = columns(head, width)
        out_ref[:, rank * width : (rank + 1) * width] = attend(
            q_ref[:, at],
            k_ref[:, at],
            v_ref[:, at],
            listed_blocks(lists_ref, counts_ref, head, blocks),
            blocks,
        )


def temporal_kernel(
    heads, width, blocks, class_ref, lists_ref, counts_ref, packed_ref, out_ref
):
    half = heads // 2
    for rank in range(half):
        head = head_of_rank(class_ref, 1, rank, heads)
        q, k, v = (
            packed_ref[:, (place * half + rank) * width : (place * half + rank + 1) * width]
            for place in range(3)
        )
        out_ref[:, rank * width : (rank + 1) * width] = attend(
            q, k, v, listed_blocks(lists_ref, counts_ref, head, blocks), blocks
        )


def place_heads(heads, width, class_ref, spatial_ref, temporal_ref, att_ref):
    for kind, ref in ((0, spatial_ref), (1, temporal_ref)):
        for rank in range(heads // 2):
            head = head_of_rank(class_ref, kind, rank, heads)
            att_ref[:, columns(head, width)] = ref[:, rank * width : (rank + 1) * width]


def project_pieces_kernel(
    heads, width, count, class_ref, at_ref, spatial_ref, temporal_ref, *refs
):
    pieces, (peer_ref, mine_ref, att_ref) = refs[: 2 * count], refs[2 * count :]
    place_heads(heads, width, class_ref, spatial_ref, temporal_ref, att_ref)
    depth, cols = pieces[0].shape
    rows = peer_ref.shape[0]
    half = at_ref[count]
    side = at_ref[count + 1]
    for out_ref, part in ((peer_ref, 1 - side), (mine_ref, side)):
        take = pl.ds(pl.multiple_of(part * rows, rows), rows)
        left = att_ref[take, columns(half, depth)]
        right = att_ref[take, columns(1 - half, depth)]
        for index in range(count):
            total = jnp.dot(
                left, pieces[2 * index][...], preferred_element_type=jnp.float32
            ) + jnp.dot(
                right, pieces[2 * index + 1][...], preferred_element_type=jnp.float32
            )
            out_ref[:, columns(at_ref[index], cols)] = total.astype(out_ref.dtype)


def project_whole_kernel(
    heads, width, class_ref, at_ref, spatial_ref, temporal_ref, weight_ref, peer_ref, mine_ref, att_ref
):
    place_heads(heads, width, class_ref, spatial_ref, temporal_ref, att_ref)
    rows = peer_ref.shape[0]
    side = at_ref[0]
    for out_ref, part in ((peer_ref, 1 - side), (mine_ref, side)):
        take = pl.ds(pl.multiple_of(part * rows, rows), rows)
        out_ref[...] = jnp.dot(
            att_ref[take, :], weight_ref[...], preferred_element_type=jnp.float32
        ).astype(out_ref.dtype)


def gather_pieces(shard):
    rows = shard.shape[0] // 2
    group = lax.axis_index("groups")
    index = lax.axis_index("frame")
    line, pair = index // 2, index % 2

    def swap_pair(piece):
        return lax.ppermute(piece, "frame", [(i, i ^ 1) for i in range(8)])

    def swap_group(piece):
        return lax.ppermute(piece, "groups", [(0, 1), (1, 0)])

    def next_line(piece):
        return lax.ppermute(piece, "frame", [(i, (i + 2) % 8) for i in range(8)])

    mine = lax.dynamic_slice_in_dim(shard, group * rows, rows, 0)
    other = lax.dynamic_slice_in_dim(shard, (1 - group) * rows, rows, 0)
    across = swap_pair(shard)
    pieces = [
        (mine, other, index),
        (
            lax.dynamic_slice_in_dim(across, group * rows, rows, 0),
            lax.dynamic_slice_in_dim(across, (1 - group) * rows, rows, 0),
            index ^ 1,
        ),
    ]
    held = mine
    for step in (1, 2, 3):
        held = next_line(held)
        source = ((line - step) % 4) * 2
        held_pair = swap_pair(held)
        held_group = swap_group(held)
        last = swap_pair(held_group) if step == 3 else swap_group(held_pair)
        pieces.append((held, held_group, source + pair))
        pieces.append((held_pair, last, source + 1 - pair))
    return pieces


def on_device(
    head_queries, head_keys, head_values, out_weight, head_class, block_lists, block_counts
):
    pixels = head_queries.shape[0]
    heads = head_class.shape[0]
    half = heads // 2
    width = head_queries.shape[1] // heads
    blocks = block_counts.shape[2]
    frames = lax.axis_size("frame")
    groups = lax.axis_size("groups")
    model = out_weight.shape[1] * frames
    side = lax.axis_index("head")
    bf16 = functools.partial(jax.ShapeDtypeStruct, dtype=jnp.bfloat16)
    lists = block_lists.reshape(-1)
    counts = block_counts.reshape(-1)

    packed = pl.pallas_call(
        functools.partial(pack_kernel, heads, width),
        out_shape=bf16((pixels, 3 * half * width)),
        in_specs=[SMEM, VMEM, VMEM, VMEM],
        out_specs=VMEM,
        compiler_params=PARAMS,
    )(head_class, head_queries, head_keys, head_values)
    arrived = lax.all_to_all(
        packed.reshape(frames, pixels // frames, 3 * half * width),
        "frame",
        split_axis=0,
        concat_axis=0,
        tiled=True,
    ).reshape(pixels, 3 * half * width)
    spatial = pl.pallas_call(
        functools.partial(spatial_kernel, heads, width, blocks),
        out_shape=bf16((pixels, half * width)),
        in_specs=[SMEM, SMEM, SMEM, VMEM, VMEM, VMEM],
        out_specs=VMEM,
        compiler_params=PARAMS,
    )(head_class, lists, counts, head_queries, head_keys, head_values)
    temporal = pl.pallas_call(
        functools.partial(temporal_kernel, heads, width, blocks),
        out_shape=bf16((pixels, half * width)),
        in_specs=[SMEM, SMEM, SMEM, VMEM],
        out_specs=VMEM,
        compiler_params=PARAMS,
    )(head_class, lists, counts, arrived)
    returned = lax.all_to_all(
        temporal.reshape(frames, pixels // frames, half * width),
        "frame",
        split_axis=0,
        concat_axis=0,
        tiled=True,
    ).reshape(pixels, half * width)

    portion_shapes = [bf16((pixels // 2, model))] * 2
    scratch = [pltpu.VMEM((pixels, heads * width), jnp.bfloat16)]
    if frames == 8 and groups == 2:
        pieces = gather_pieces(out_weight)
        at = jnp.stack(
            [piece[2] for piece in pieces] + [lax.axis_index("groups"), side]
        ).astype(jnp.int32)
        operands = [ref for piece in pieces for ref in piece[:2]]
        peer, mine = pl.pallas_call(
            functools.partial(project_pieces_kernel, heads, width, len(pieces)),
            out_shape=portion_shapes,
            in_specs=[SMEM, SMEM] + [VMEM] * (2 + len(operands)),
            out_specs=[VMEM, VMEM],
            scratch_shapes=scratch,
            compiler_params=PARAMS,
        )(head_class, at, spatial, returned, *operands)
    else:
        weight = lax.all_gather(out_weight, "frame", axis=1, tiled=True)
        peer, mine = pl.pallas_call(
            functools.partial(project_whole_kernel, heads, width),
            out_shape=portion_shapes,
            in_specs=[SMEM, SMEM] + [VMEM] * 3,
            out_specs=[VMEM, VMEM],
            scratch_shapes=scratch,
            compiler_params=PARAMS,
        )(head_class, side.reshape(1).astype(jnp.int32), spatial, returned, weight)
    received = lax.ppermute(peer, "head", [(0, 1), (1, 0)])
    return (mine.astype(jnp.float32) + received.astype(jnp.float32)).astype(jnp.bfloat16)


def solution(mesh):
    placed = (
        P(("groups", "frame"), "head"),
        P(("groups", "frame"), "head"),
        P(("groups", "frame"), "head"),
        P("head", "frame"),
        P("head"),
        P("head", ("groups", "frame"), None, None),
        P("head", ("groups", "frame"), None),
    )
    return jax.shard_map(
        on_device,
        mesh=mesh,
        in_specs=placed,
        out_specs=P(("groups", "frame", "head"), None),
        check_vma=False,
    )
```

time: 126 us -> 76.9 us (0.61)
  waiting for transfers between devices: 55.8 us -> 38.7 us
  local copies, waits for them, and re-layouts: 19.5 us -> 2.82 us
  between operations: 13.7 us -> 0.08 us
  Pallas kernels: 0 us -> 8.9 us
  other arithmetic: 9.56 us -> 1.07 us
  matrix products: 7.91 us -> 0 us
  starting transfers between devices: 18.7 us -> 24.9 us
    ppermute x0 -> x14, waiting for transfers between devices: none -> 38.7 us  [the longest x3 23.2 us: next_line(): return lax.ppermute(piece, 'frame', [(i, (i + 2) % 8) for i in range(8)])]
    all_to_all x4 -> x2, waiting for transfers between devices: 31.6 us -> 0.01 us  [the longest x1 0.01 us: on_device(): lax.all_to_all(packed.reshape(frames, pixels // frames, 3 * half * width)...]
    ppermute x0 -> x14, starting transfers between devices: none -> 15 us  [the longest x5 5.64 us: swap_group(): return lax.ppermute(piece, 'groups', [(0, 1), (1, 0)])]
    all_gather x1 -> x0, waiting for transfers between devices: 14.7 us -> none  [on_device(): lax.all_gather(out_weight, 'frame', axis=1, tiled=True)]
    pallas_call x0 -> x4, Pallas kernels: none -> 8.9 us  [the longest x1 4.09 us: on_device(): pl.pallas_call(functools.partial(project_pieces_kernel, heads, width, len...]
    all_to_all x4 -> x2, starting transfers between devices: 18.7 us -> 9.87 us  [the longest x1 4.95 us: on_device(): lax.all_to_all(temporal.reshape(frames, pixels // frames, half * width),...]
    reduce_scatter x1 -> x0, waiting for transfers between devices: 8.74 us -> none  [on_device(): lax.psum_scatter(partial_out.astype(jnp.bfloat16), 'head', scatter_dimens...]
    dot_general x13 -> x0, matrix products: 7.91 us -> none  [the longest x1 4.93 us: on_device(): jnp.dot(attended, lax.all_gather(out_weight, 'frame', axis=1, tiled=True)...]
  transfers between devices with their start and end apart: 6 -> 16, of which waited for: 6 -> 7; matrix products, arithmetic and copies ran while one was open for 25% -> 2% of each run, Pallas kernels for 0% -> 6%
where the time goes in v1:
time: 76.9 us; the launch traced here: 76.5 us
  waiting for transfers between devices  38.7 us (50%)
  starting transfers between devices  24.9 us (32%)
  Pallas kernels  8.9 us (12%)
  local copies, waits for them, and re-layouts  2.82 us (4%)
  other arithmetic  1.07 us (1%)
    ppermute x3, waiting for transfers between devices, next_line(): return lax.ppermute(piece, 'frame', [(i, (i + 2) % 8) for i in range(8)])  23.2 us
    ppermute x5, waiting for transfers between devices, swap_group(): return lax.ppermute(piece, 'groups', [(0, 1), (1, 0)])  13.3 us
    ppermute x5, starting transfers between devices, swap_group(): return lax.ppermute(piece, 'groups', [(0, 1), (1, 0)])  5.64 us
    ppermute x5, starting transfers between devices, swap_pair(): return lax.ppermute(piece, 'frame', [(i, i ^ 1) for i in range(8)])  5.55 us
    all_to_all x1, starting transfers between devices, on_device(): lax.all_to_all(temporal.reshape(frames, pixels // frames, half * width),...  4.95 us
    all_to_all x1, starting transfers between devices, on_device(): lax.all_to_all(packed.reshape(frames, pixels // frames, 3 * half * width)...  4.92 us
    pallas_call x1, Pallas kernels, on_device(): pl.pallas_call(functools.partial(project_pieces_kernel, heads, width, len...  4.09 us
    ppermute x3, starting transfers between devices, next_line(): return lax.ppermute(piece, 'frame', [(i, (i + 2) % 8) for i in range(8)])  3.76 us
  transfers between devices with their start and end apart: 16, of which 7 were waited for; matrix products, arithmetic and copies ran while one was open for 2% of the time, Pallas kernels for 6%

profile of v1, /device:TPU:0, one launch (start us, length us, event | category | flops | bytes accessed | tf_op | source)
XLA Modules:
  0.0 76.5 jit_solution(918909857679095248)
XLA Ops:
  0.0 1.2 %constant_dynamic-slice_fusion.2 = (bf16[384,384]{1,0:T(8,128)(2,1)S(1)}, bf16[384,384]{1,0:T(8,128)(2,1)S(1)}) fusion(bf16[768,384]{1,0:T(8,128)(2,1)} %param.10, s32[]{:T(128)S(6)} %select_n.37, s32[]{:T(128)S(6)} %select_n.36), kind=kLoop, calls=%fused_computation.3 | loop fusion | bytes 1179656 | tf_op jit(solution)/shard_map/dynamic_slice | solution.py:159
  1.2 3.1 %collective-permute-start.1 = (bf16[384,384]{1,0:T(8,128)(2,1)S(1)}, bf16[384,384]{1,0:T(8,128)(2,1)S(1)}, u32[]{:S(2)}, u32[]{:S(2)}) collective-permute-start(bf16[384,384]{1,0:T(8,128)(2,1)S(1)} %get-tuple-element.12.refs_0_), channel_id=1, source_target_pairs={{0,4},{2,6},{4,8},{6,10},{8,12},{10,14},{12,0},{14,2},{1,5},{3,7},... | collective-permute-start | bytes 884744 | tf_op jit(solution)/shard_map/ppermute | solution.py:156
  4.3 1.5 %shard_map.74 = bf16[256,1152]{1,0:T(8,128)(2,1)} custom-call(s32[6]{0:T(128)S(1)} %copy-done.3, bf16[256,768]{1,0:T(8,128)(2,1)S(1)} %copy-done, bf16[256,768]{1,0:T(8,128)(2,1)S(1)} %copy-done.1, bf16[256,768]{1,0:T(8,128)(2,1)S(1)} %copy-done.2), custom_call_target="tpu_custom_call" | custom-call | tf_op jit(solution)/shard_map/pallas_call | solution.py:197
  5.8 4.9 %all-to-all-start = ((bf16[8,32,1152]{2,1,0:T(8,128)(2,1)}), bf16[8,32,1152]{2,1,0:T(8,128)(2,1)S(1)}, u32[]{:S(2)}, u32[]{:S(2)}) async-start(bf16[8,32,1152]{2,1,0:T(8,128)(2,1)} %bitcast.10), calls=%async_computation | async-start | bytes 1179648 | tf_op jit(solution)/shard_map/all_to_all | solution.py:204
  10.7 2.7 %collective-permute-done.1.refs_4_ = bf16[384,384]{1,0:T(8,128)(2,1)S(1)} collective-permute-done((bf16[384,384]{1,0:T(8,128)(2,1)S(1)}, bf16[384,384]{1,0:T(8,128)(2,1)S(1)}, u32[]{:S(2)}, u32[]{:S(2)}) %collective-permute-start.1) | collective-permute-done | bytes 294944 | tf_op jit(solution)/shard_map/ppermute | solution.py:156
  13.4 1.5 %collective-permute-start = (bf16[768,384]{1,0:T(8,128)(2,1)}, bf16[768,384]{1,0:T(8,128)(2,1)}, u32[]{:S(2)}, u32[]{:S(2)}) collective-permute-start(bf16[768,384]{1,0:T(8,128)(2,1)} %param.10), channel_id=1, source_target_pairs={{0,2},{2,0},{4,6},{6,4},{8,10},{10,8},{12,14},{14,12},{1,3},{3,1},... | collective-permute-start | bytes 1769480 | tf_op jit(solution)/shard_map/ppermute | solution.py:150
  14.9 15.6 %collective-permute-done.5.refs_8_ = bf16[384,384]{1,0:T(8,128)(2,1)S(1)} collective-permute-done((bf16[384,384]{1,0:T(8,128)(2,1)S(1)}, bf16[384,384]{1,0:T(8,128)(2,1)S(1)}, u32[]{:S(2)}, u32[]{:S(2)}) %collective-permute-start.5) | collective-permute-done | bytes 294944 | tf_op jit(solution)/shard_map/ppermute | solution.py:156
  30.5 0.7 collective-permute-start.9
  31.1 1.7 %collective-permute-start.3 = (bf16[384,384]{1,0:T(8,128)(2,1)S(1)}, bf16[384,384]{1,0:T(8,128)(2,1)}, u32[]{:S(2)}, u32[]{:S(2)}) collective-permute-start(bf16[384,384]{1,0:T(8,128)(2,1)S(1)} %collective-permute-done.1.refs_4_), channel_id=1, source_target_pairs={{0,2},{2,0},{4,6},{6,4},{8,10},{10,8},{12,14},{14,12},{1,3},{3,1},... | collective-permute-start | bytes 884744 | tf_op jit(solution)/shard_map/ppermute | solution.py:150
  32.8 1.5 %collective-permute-start.2 = (bf16[384,384]{1,0:T(8,128)(2,1)S(1)}, bf16[384,384]{1,0:T(8,128)(2,1)}, u32[]{:S(2)}, u32[]{:S(2)}) collective-permute-start(bf16[384,384]{1,0:T(8,128)(2,1)S(1)} %collective-permute-done.1.refs_4_), channel_id=1, source_target_pairs={{0,16},{16,0},{1,17},{17,1},{2,18},{18,2},{3,19},{19,3},{4,20},{20... | collective-permute-start | bytes 884744 | tf_op jit(solution)/shard_map/ppermute | solution.py:153
  34.7 5.0 %collective-permute-done.9.refs_12_ = bf16[384,384]{1,0:T(8,128)(2,1)} collective-permute-done((bf16[384,384]{1,0:T(8,128)(2,1)S(1)}, bf16[384,384]{1,0:T(8,128)(2,1)}, u32[]{:S(2)}, u32[]{:S(2)}) %collective-permute-start.9) | collective-permute-done | bytes 294944 | tf_op jit(solution)/shard_map/ppermute | solution.py:156
  39.6 1.5 %collective-permute-start.10 = (bf16[384,384]{1,0:T(8,128)(2,1)}, bf16[384,384]{1,0:T(8,128)(2,1)}, u32[]{:S(2)}, u32[]{:S(2)}) collective-permute-start(bf16[384,384]{1,0:T(8,128)(2,1)} %collective-permute-done.9.refs_12_), channel_id=1, source_target_pairs={{0,16},{16,0},{1,17},{17,1},{2,18},{18,2},{3,19},{19,3},{4,20},{20... | collective-permute-start | bytes 884744 | tf_op jit(solution)/shard_map/ppermute | solution.py:153
  41.6 2.0 %shard_map.75 = bf16[256,384]{1,0:T(8,128)(2,1)} custom-call(s32[6]{0:T(128)S(1)} %copy-done.3, s32[48]{0:T(128)S(1)} %reshape.18.lists_ref, s32[24]{0:T(128)S(1)} %reshape.19.counts_ref, bf16[256,1152]{1,0:T(8,128)(2,1)S(1)} %bitcast.18), custom_call_target="tpu_custom_call" | custom-call | tf_op jit(solution)/shard_map/pallas_call | solution.py:218
  43.5 5.0 %all-to-all-start.1 = ((bf16[8,32,384]{2,1,0:T(8,128)(2,1)}), bf16[8,32,384]{2,1,0:T(8,128)(2,1)S(1)}, u32[]{:S(2)}, u32[]{:S(2)}) async-start(bf16[8,32,384]{2,1,0:T(8,128)(2,1)} %bitcast.12), calls=%async_computation.1 | async-start | bytes 393216 | tf_op jit(solution)/shard_map/all_to_all | solution.py:225
  49.1 1.5 %collective-permute-start.4 = (bf16[384,384]{1,0:T(8,128)(2,1)}, bf16[384,384]{1,0:T(8,128)(2,1)}, u32[]{:S(2)}, u32[]{:S(2)}) collective-permute-start(bf16[384,384]{1,0:T(8,128)(2,1)} %collective-permute-done.3.refs_6_), channel_id=1, source_target_pairs={{0,16},{16,0},{1,17},{17,1},{2,18},{18,2},{3,19},{19,3},{4,20},{20... | collective-permute-start | bytes 884744 | tf_op jit(solution)/shard_map/ppermute | solution.py:153
  50.6 2.0 %collective-permute-start.11 = (bf16[384,384]{1,0:T(8,128)(2,1)}, bf16[384,384]{1,0:T(8,128)(2,1)}, u32[]{:S(2)}, u32[]{:S(2)}) collective-permute-start(bf16[384,384]{1,0:T(8,128)(2,1)} %collective-permute-done.9.refs_12_), channel_id=1, source_target_pairs={{0,2},{2,0},{4,6},{6,4},{8,10},{10,8},{12,14},{14,12},{1,3},{3,1},... | collective-permute-start | bytes 884744 | tf_op jit(solution)/shard_map/ppermute | solution.py:150
  53.1 1.3 %shard_map.73.spatial_ref = bf16[256,384]{1,0:T(8,128)(2,1)S(1)} custom-call(s32[6]{0:T(128)S(1)} %copy-done.3, s32[48]{0:T(128)S(1)} %reshape.18.lists_ref, s32[24]{0:T(128)S(1)} %reshape.19.counts_ref, bf16[256,768]{1,0:T(8,128)(2,1)S(1)} %copy-done, bf16[256,768]{1,0:T(8,128)(2,1)S(1)} %copy-done.1, bf16[256,768]{1,0:T(8,128)(2,1)S(1)} %copy-done.2), custom_call_target="tpu_custom_call" | custom-call | tf_op jit(solution)/shard_map/pallas_call | solution.py:211
  54.6 1.1 %constant_dynamic-slice_fusion = (bf16[384,384]{1,0:T(8,128)(2,1)S(1)}, bf16[384,384]{1,0:T(8,128)(2,1)S(1)}) fusion(bf16[768,384]{1,0:T(8,128)(2,1)} %collective-permute-done, s32[]{:T(128)S(6)} %select_n.37, s32[]{:T(128)S(6)} %select_n.36), kind=kLoop, calls=%fused_computation.1 | loop fusion | bytes 1179656 | tf_op jit(solution)/shard_map/dynamic_slice | solution.py:165
  55.7 2.9 %collective-permute-done.6.refs_9_ = bf16[384,384]{1,0:T(8,128)(2,1)} collective-permute-done((bf16[384,384]{1,0:T(8,128)(2,1)S(1)}, bf16[384,384]{1,0:T(8,128)(2,1)}, u32[]{:S(2)}, u32[]{:S(2)}) %collective-permute-start.6) | collective-permute-done | bytes 294944 | tf_op jit(solution)/shard_map/ppermute | solution.py:153
  58.6 6.3 %collective-permute-done.4.refs_7_ = bf16[384,384]{1,0:T(8,128)(2,1)} collective-permute-done((bf16[384,384]{1,0:T(8,128)(2,1)}, bf16[384,384]{1,0:T(8,128)(2,1)}, u32[]{:S(2)}, u32[]{:S(2)}) %collective-permute-start.4) | collective-permute-done | bytes 294944 | tf_op jit(solution)/shard_map/ppermute | solution.py:153
  64.9 4.0 %collective-permute-done.8.refs_11_ = bf16[384,384]{1,0:T(8,128)(2,1)} collective-permute-done((bf16[384,384]{1,0:T(8,128)(2,1)}, bf16[384,384]{1,0:T(8,128)(2,1)}, u32[]{:S(2)}, u32[]{:S(2)}) %collective-permute-start.8) | collective-permute-done | bytes 294944 | tf_op jit(solution)/shard_map/ppermute | solution.py:153
  69.0 4.1 %shard_map.76 = (bf16[128,3072]{1,0:T(8,128)(2,1)S(1)}, bf16[128,3072]{1,0:T(8,128)(2,1)S(1)}) custom-call(s32[6]{0:T(128)S(1)} %copy-done.3, s32[10]{0:T(128)S(1)} %stack.43.at_ref, bf16[256,384]{1,0:T(8,128)(2,1)S(1)} %shard_map.73.spatial_ref, bf16[256,384]{1,0:T(8,128)(2,1)S(1)} %bitcast.19, bf16[384,384]{1,0:T(8,128)(2,1)S(1)} %get-tuple-element.12.refs_0_, ...), custom_call_target="tpu_custom_call" | custom-call | tf_op jit(solution)/shard_map/pallas_call | solution.py:241
  73.2 2.3 %collective-permute-done.13 = bf16[128,3072]{1,0:T(8,128)(2,1)S(1)} collective-permute-done((bf16[128,3072]{1,0:T(8,128)(2,1)S(1)}, bf16[128,3072]{1,0:T(8,128)(2,1)S(1)}, u32[]{:S(2)}, u32[]{:S(2)}) %collective-permute-start.13) | collective-permute-done | bytes 786464 | tf_op jit(solution)/shard_map/ppermute | solution.py:259
  75.4 1.1 %add_convert_fusion = bf16[128,3072]{1,0:T(8,128)(2,1)} fusion(bf16[128,3072]{1,0:T(8,128)(2,1)S(1)} %collective-permute-done.13, bf16[128,3072]{1,0:T(8,128)(2,1)S(1)} %get-tuple-element.7), kind=kLoop, calls=%fused_computation | loop fusion | flops 1572864 | bytes 2359296 | tf_op jit(solution)/shard_map/convert_element_type | solution.py:260
  (32 shorter events, 2.1 us)
Async XLA Ops:
  0.0 4.3 %copy-start.3 = (s32[6]{0:T(128)S(1)}, s32[6]{0:T(128)}, u32[]{:S(2)}) copy-start(s32[6]{0:T(128)} %class_ref.7) | copy-start | bytes 76
  0.0 4.3 %copy-start.2 = (bf16[256,768]{1,0:T(8,128)(2,1)S(1)}, bf16[256,768]{1,0:T(8,128)(2,1)}, u32[]{:S(2)}) copy-start(bf16[256,768]{1,0:T(8,128)(2,1)} %v_ref.3) | copy-start | bytes 1179652
  0.0 4.3 %copy-start.1 = (bf16[256,768]{1,0:T(8,128)(2,1)S(1)}, bf16[256,768]{1,0:T(8,128)(2,1)}, u32[]{:S(2)}) copy-start(bf16[256,768]{1,0:T(8,128)(2,1)} %k_ref.3) | copy-start | bytes 1179652
  0.0 4.3 %copy-start = (bf16[256,768]{1,0:T(8,128)(2,1)S(1)}, bf16[256,768]{1,0:T(8,128)(2,1)}, u32[]{:S(2)}) copy-start(bf16[256,768]{1,0:T(8,128)(2,1)} %q_ref.3) | copy-start | bytes 1179652
  1.2 12.2 %collective-permute-start.1 = (bf16[384,384]{1,0:T(8,128)(2,1)S(1)}, bf16[384,384]{1,0:T(8,128)(2,1)S(1)}, u32[]{:S(2)}, u32[]{:S(2)}) collective-permute-start(bf16[384,384]{1,0:T(8,128)(2,1)S(1)} %get-tuple-element.12.refs_0_), channel_id=1, source_target_pairs={{0,4},{2,6},{4,8},{6,10},{8,12},{10,14},{12,0},{14,2},{1,5},{3,7},... | collective-permute-start | bytes 884744 | tf_op jit(solution)/shard_map/ppermute | solution.py:156
  5.8 35.3 %copy-start.5 = (s32[6,1,4]{0,2,1:T(4,128)S(1)}, s32[6,1,4]{0,2,1:T(4,128)}, u32[]{:S(2)}) copy-start(s32[6,1,4]{0,2,1:T(4,128)} %param.13) | copy-start | bytes 292
  5.8 35.5 %copy-start.4 = (s32[6,1,4,2]{0,3,2,1:T(2,128)S(1)}, s32[6,1,4,2]{0,3,2,1:T(2,128)}, u32[]{:S(2)}) copy-start(s32[6,1,4,2]{0,3,2,1:T(2,128)} %param.12) | copy-start | bytes 580
  5.8 35.7 %all-to-all-start = ((bf16[8,32,1152]{2,1,0:T(8,128)(2,1)}), bf16[8,32,1152]{2,1,0:T(8,128)(2,1)S(1)}, u32[]{:S(2)}, u32[]{:S(2)}) async-start(bf16[8,32,1152]{2,1,0:T(8,128)(2,1)} %bitcast.10), calls=%async_computation | async-start | bytes 1179648 | tf_op jit(solution)/shard_map/all_to_all | solution.py:204
  13.4 17.1 %collective-permute-start.5 = (bf16[384,384]{1,0:T(8,128)(2,1)S(1)}, bf16[384,384]{1,0:T(8,128)(2,1)S(1)}, u32[]{:S(2)}, u32[]{:S(2)}) collective-permute-start(bf16[384,384]{1,0:T(8,128)(2,1)S(1)} %collective-permute-done.1.refs_4_), channel_id=1, source_target_pairs={{0,4},{2,6},{4,8},{6,10},{8,12},{10,14},{12,0},{14,2},{1,5},{3,7},... | collective-permute-start | bytes 884744 | tf_op jit(solution)/shard_map/ppermute | solution.py:156
  13.4 37.2 %collective-permute-start = (bf16[768,384]{1,0:T(8,128)(2,1)}, bf16[768,384]{1,0:T(8,128)(2,1)}, u32[]{:S(2)}, u32[]{:S(2)}) collective-permute-start(bf16[768,384]{1,0:T(8,128)(2,1)} %param.10), channel_id=1, source_target_pairs={{0,2},{2,0},{4,6},{6,4},{8,10},{10,8},{12,14},{14,12},{1,3},{3,1},... | collective-permute-start | bytes 1769480 | tf_op jit(solution)/shard_map/ppermute | solution.py:150
  30.5 9.2 %collective-permute-start.9 = (bf16[384,384]{1,0:T(8,128)(2,1)S(1)}, bf16[384,384]{1,0:T(8,128)(2,1)}, u32[]{:S(2)}, u32[]{:S(2)}) collective-permute-start(bf16[384,384]{1,0:T(8,128)(2,1)S(1)} %collective-permute-done.5.refs_8_), channel_id=1, source_target_pairs={{0,4},{2,6},{4,8},{6,10},{8,12},{10,14},{12,0},{14,2},{1,5},{3,7},... | collective-permute-start | bytes 884744 | tf_op jit(solution)/shard_map/ppermute | solution.py:156
  31.1 17.4 %collective-permute-start.3 = (bf16[384,384]{1,0:T(8,128)(2,1)S(1)}, bf16[384,384]{1,0:T(8,128)(2,1)}, u32[]{:S(2)}, u32[]{:S(2)}) collective-permute-start(bf16[384,384]{1,0:T(8,128)(2,1)S(1)} %collective-permute-done.1.refs_4_), channel_id=1, source_target_pairs={{0,2},{2,0},{4,6},{6,4},{8,10},{10,8},{12,14},{14,12},{1,3},{3,1},... | collective-permute-start | bytes 884744 | tf_op jit(solution)/shard_map/ppermute | solution.py:150
  32.8 16.3 %collective-permute-start.2 = (bf16[384,384]{1,0:T(8,128)(2,1)S(1)}, bf16[384,384]{1,0:T(8,128)(2,1)}, u32[]{:S(2)}, u32[]{:S(2)}) collective-permute-start(bf16[384,384]{1,0:T(8,128)(2,1)S(1)} %collective-permute-done.1.refs_4_), channel_id=1, source_target_pairs={{0,16},{16,0},{1,17},{17,1},{2,18},{18,2},{3,19},{19,3},{4,20},{20... | collective-permute-start | bytes 884744 | tf_op jit(solution)/shard_map/ppermute | solution.py:153
  34.3 18.2 %collective-permute-start.7 = (bf16[384,384]{1,0:T(8,128)(2,1)S(1)}, bf16[384,384]{1,0:T(8,128)(2,1)}, u32[]{:S(2)}, u32[]{:S(2)}) collective-permute-start(bf16[384,384]{1,0:T(8,128)(2,1)S(1)} %collective-permute-done.5.refs_8_), channel_id=1, source_target_pairs={{0,2},{2,0},{4,6},{6,4},{8,10},{10,8},{12,14},{14,12},{1,3},{3,1},... | collective-permute-start | bytes 884744 | tf_op jit(solution)/shard_map/ppermute | solution.py:150
  39.6 13.4 %collective-permute-start.10 = (bf16[384,384]{1,0:T(8,128)(2,1)}, bf16[384,384]{1,0:T(8,128)(2,1)}, u32[]{:S(2)}, u32[]{:S(2)}) collective-permute-start(bf16[384,384]{1,0:T(8,128)(2,1)} %collective-permute-done.9.refs_12_), channel_id=1, source_target_pairs={{0,16},{16,0},{1,17},{17,1},{2,18},{18,2},{3,19},{19,3},{4,20},{20... | collective-permute-start | bytes 884744 | tf_op jit(solution)/shard_map/ppermute | solution.py:153
  43.5 25.4 %all-to-all-start.1 = ((bf16[8,32,384]{2,1,0:T(8,128)(2,1)}), bf16[8,32,384]{2,1,0:T(8,128)(2,1)S(1)}, u32[]{:S(2)}, u32[]{:S(2)}) async-start(bf16[8,32,384]{2,1,0:T(8,128)(2,1)} %bitcast.12), calls=%async_computation.1 | async-start | bytes 393216 | tf_op jit(solution)/shard_map/all_to_all | solution.py:225
  48.5 10.1 %collective-permute-start.6 = (bf16[384,384]{1,0:T(8,128)(2,1)S(1)}, bf16[384,384]{1,0:T(8,128)(2,1)}, u32[]{:S(2)}, u32[]{:S(2)}) collective-permute-start(bf16[384,384]{1,0:T(8,128)(2,1)S(1)} %collective-permute-done.5.refs_8_), channel_id=1, source_target_pairs={{0,16},{16,0},{1,17},{17,1},{2,18},{18,2},{3,19},{19,3},{4,20},{20... | collective-permute-start | bytes 884744 | tf_op jit(solution)/shard_map/ppermute | solution.py:153
  49.1 15.9 %collective-permute-start.4 = (bf16[384,384]{1,0:T(8,128)(2,1)}, bf16[384,384]{1,0:T(8,128)(2,1)}, u32[]{:S(2)}, u32[]{:S(2)}) collective-permute-start(bf16[384,384]{1,0:T(8,128)(2,1)} %collective-permute-done.3.refs_6_), channel_id=1, source_target_pairs={{0,16},{16,0},{1,17},{17,1},{2,18},{18,2},{3,19},{19,3},{4,20},{20... | collective-permute-start | bytes 884744 | tf_op jit(solution)/shard_map/ppermute | solution.py:153
  50.6 14.3 %collective-permute-start.11 = (bf16[384,384]{1,0:T(8,128)(2,1)}, bf16[384,384]{1,0:T(8,128)(2,1)}, u32[]{:S(2)}, u32[]{:S(2)}) collective-permute-start(bf16[384,384]{1,0:T(8,128)(2,1)} %collective-permute-done.9.refs_12_), channel_id=1, source_target_pairs={{0,2},{2,0},{4,6},{6,4},{8,10},{10,8},{12,14},{14,12},{1,3},{3,1},... | collective-permute-start | bytes 884744 | tf_op jit(solution)/shard_map/ppermute | solution.py:150
  52.6 16.4 %collective-permute-start.8 = (bf16[384,384]{1,0:T(8,128)(2,1)}, bf16[384,384]{1,0:T(8,128)(2,1)}, u32[]{:S(2)}, u32[]{:S(2)}) collective-permute-start(bf16[384,384]{1,0:T(8,128)(2,1)} %collective-permute-done.7.refs_10_), channel_id=1, source_target_pairs={{0,16},{16,0},{1,17},{17,1},{2,18},{18,2},{3,19},{19,3},{4,20},{20... | collective-permute-start | bytes 884744 | tf_op jit(solution)/shard_map/ppermute | solution.py:153
  53.1 15.9 %collective-permute-start.12 = (bf16[384,384]{1,0:T(8,128)(2,1)}, bf16[384,384]{1,0:T(8,128)(2,1)}, u32[]{:S(2)}, u32[]{:S(2)}) collective-permute-start(bf16[384,384]{1,0:T(8,128)(2,1)} %collective-permute-done.10.refs_13_), channel_id=1, source_target_pairs={{0,2},{2,0},{4,6},{6,4},{8,10},{10,8},{12,14},{14,12},{1,3},{3,1},... | collective-permute-start | bytes 884744 | tf_op jit(solution)/shard_map/ppermute | solution.py:150
  73.1 2.4 %collective-permute-start.13 = (bf16[128,3072]{1,0:T(8,128)(2,1)S(1)}, bf16[128,3072]{1,0:T(8,128)(2,1)S(1)}, u32[]{:S(2)}, u32[]{:S(2)}) collective-permute-start(bf16[128,3072]{1,0:T(8,128)(2,1)S(1)} %get-tuple-element.8), channel_id=1, source_target_pairs={{0,1},{1,0},{2,3},{3,2},{4,5},{5,4},{6,7},{7,6},{8,9},{9,8},{10,11... | collective-permute-start | bytes 2359304 | tf_op jit(solution)/shard_map/ppermute | solution.py:259

commit v2 on v1

v2 whole, which is shorter than its diff:
```python
import functools

import jax
import jax.numpy as jnp
from jax import lax
from jax.experimental import pallas as pl
from jax.experimental.pallas import tpu as pltpu
from jax.sharding import PartitionSpec as P

VMEM = pl.BlockSpec(memory_space=pltpu.VMEM)
SMEM = pl.BlockSpec(memory_space=pltpu.SMEM)
ANY = pl.BlockSpec(memory_space=pl.ANY)
PARAMS = pltpu.CompilerParams(vmem_limit_bytes=40 * 1024 * 1024)


def head_of_rank(class_ref, kind, rank, heads):
    found = jnp.int32(0)
    seen = jnp.int32(0)
    for head in range(heads):
        is_kind = class_ref[head] == kind
        found = jnp.where(is_kind & (seen == rank), head, found)
        seen = seen + is_kind.astype(jnp.int32)
    return found


def columns(index, width):
    return pl.ds(pl.multiple_of(index * width, width), width)


def head_copies(heads, width, kind, class_ref, sources, place, sems):
    copies = []
    for rank in range(heads // 2):
        head = head_of_rank(class_ref, kind, rank, heads)
        for index, source in enumerate(sources):
            copies.append(
                pltpu.make_async_copy(
                    source.at[:, columns(head, width)],
                    place(index, rank),
                    sems.at[index, rank],
                )
            )
    for copy in copies:
        copy.start()
    return copies


def pack_kernel(heads, width, class_ref, q_ref, k_ref, v_ref, packed_ref, sems):
    def place(index, rank):
        at = (index * (heads // 2) + rank) * width
        return packed_ref.at[:, at : at + width]

    for copy in head_copies(heads, width, 1, class_ref, (q_ref, k_ref, v_ref), place, sems):
        copy.wait()


def attend(queries, keys, values, listed, blocks):
    rows = queries.shape[0] // blocks
    scores = lax.dot_general(
        queries, keys, (((1,), (1,)), ((), ())), preferred_element_type=jnp.float32
    ) * (queries.shape[1] ** -0.5)
    key_block = lax.broadcasted_iota(jnp.int32, (rows, keys.shape[0]), 1) // rows
    masked = []
    for block in range(blocks):
        first, second = listed[block]
        allowed = (key_block == first) | (key_block == second)
        masked.append(
            jnp.where(allowed, scores[block * rows : (block + 1) * rows], -jnp.inf)
        )
    scores = jnp.concatenate(masked, axis=0)
    weights = jnp.exp(scores - jnp.max(scores, axis=1, keepdims=True))
    denominator = jnp.sum(weights, axis=1, keepdims=True)
    total = jnp.dot(
        weights.astype(jnp.bfloat16), values, preferred_element_type=jnp.float32
    )
    return (total / denominator).astype(jnp.bfloat16)


def listed_blocks(lists_ref, head, blocks):
    listed = []
    for block in range(blocks):
        both = lists_ref[head * blocks + block]
        listed.append((both >> 8, both & 255))
    return listed


def spatial_kernel(
    heads, width, blocks, class_ref, lists_ref, q_ref, k_ref, v_ref, out_ref, held_ref, sems
):
    copies = head_copies(
        heads,
        width,
        0,
        class_ref,
        (q_ref, k_ref, v_ref),
        lambda index, rank: held_ref.at[index, rank],
        sems,
    )
    for rank in range(heads // 2):
        head = head_of_rank(class_ref, 0, rank, heads)
        for copy in copies[3 * rank : 3 * rank + 3]:
            copy.wait()
        out_ref[:, rank * width : (rank + 1) * width] = attend(
            held_ref[0, rank],
            held_ref[1, rank],
            held_ref[2, rank],
            listed_blocks(lists_ref, head, blocks),
            blocks,
        )


def temporal_kernel(
    heads, width, blocks, class_ref, lists_ref, packed_ref, out_ref
):
    half = heads // 2
    for rank in range(half):
        head = head_of_rank(class_ref, 1, rank, heads)
        q, k, v = (
            packed_ref[:, (place * half + rank) * width : (place * half + rank + 1) * width]
            for place in range(3)
        )
        out_ref[:, rank * width : (rank + 1) * width] = attend(
            q, k, v, listed_blocks(lists_ref, head, blocks), blocks
        )


def place_heads(heads, width, class_ref, spatial_ref, temporal_ref, att_ref):
    for kind, ref in ((0, spatial_ref), (1, temporal_ref)):
        for rank in range(heads // 2):
            head = head_of_rank(class_ref, kind, rank, heads)
            att_ref[:, columns(head, width)] = ref[:, rank * width : (rank + 1) * width]


def project_pieces_kernel(heads, width, count, class_ref, spatial_ref, temporal_ref, *refs):
    pieces, (peer_ref, mine_ref, att_ref, held_ref, sems) = refs[: 2 * count], refs[2 * count :]
    copies = [
        pltpu.make_async_copy(piece, held_ref.at[index], sems.at[index])
        for index, piece in enumerate(pieces)
    ]
    for copy in copies:
        copy.start()
    place_heads(heads, width, class_ref, spatial_ref, temporal_ref, att_ref)
    depth, cols = pieces[0].shape
    rows = peer_ref.shape[0]
    half = lax.axis_index("groups")
    side = lax.axis_index("head")
    for index in range(count):
        take = slice(index * cols, (index + 1) * cols)
        copies[2 * index].wait()
        total = jnp.dot(
            att_ref[:, columns(half, depth)],
            held_ref[2 * index],
            preferred_element_type=jnp.float32,
        )
        copies[2 * index + 1].wait()
        total += jnp.dot(
            att_ref[:, columns(1 - half, depth)],
            held_ref[2 * index + 1],
            preferred_element_type=jnp.float32,
        )
        total = total.astype(peer_ref.dtype)

        @pl.when(side == 0)
        def _():
            mine_ref[:, take] = total[:rows]
            peer_ref[:, take] = total[rows:]

        @pl.when(side != 0)
        def _():
            mine_ref[:, take] = total[rows:]
            peer_ref[:, take] = total[:rows]


def project_whole_kernel(
    heads, width, class_ref, spatial_ref, temporal_ref, weight_ref, peer_ref, mine_ref, att_ref
):
    place_heads(heads, width, class_ref, spatial_ref, temporal_ref, att_ref)
    rows = peer_ref.shape[0]
    side = lax.axis_index("head")
    for out_ref, part in ((peer_ref, 1 - side), (mine_ref, side)):
        take = pl.ds(pl.multiple_of(part * rows, rows), rows)
        out_ref[...] = jnp.dot(
            att_ref[take, :], weight_ref[...], preferred_element_type=jnp.float32
        ).astype(out_ref.dtype)


def join_kernel(shards, *refs):
    parts, out_ref = refs[:-1], refs[-1]
    index = lax.axis_index("frame")
    line, pair = index // 2, index % 2
    cols = out_ref.shape[1] // 8
    order = iter(shards)
    for mine_ref, received_ref in zip(parts[0::2], parts[1::2]):
        for at in range(mine_ref.shape[1] // cols):
            step, crossed = next(order)
            source = lax.rem(line - step + 4, 4) * 2 + (1 - pair if crossed else pair)
            take = slice(at * cols, (at + 1) * cols)
            total = mine_ref[:, take].astype(jnp.float32) + received_ref[:, take].astype(
                jnp.float32
            )
            out_ref[:, columns(source, cols)] = total.astype(out_ref.dtype)


def swap_pair(piece):
    return lax.ppermute(piece, "frame", [(i, i ^ 1) for i in range(8)])


def swap_group(piece):
    return lax.ppermute(piece, "groups", [(0, 1), (1, 0)])


def next_line(piece):
    return lax.ppermute(piece, "frame", [(i, (i + 2) % 8) for i in range(8)])


def swap_side(portion):
    return lax.ppermute(portion, "head", [(0, 1), (1, 0)])


def tied(*values):
    return lax.optimization_barrier(values)


def on_device(
    head_queries, head_keys, head_values, out_weight, head_class, block_lists, block_counts
):
    pixels = head_queries.shape[0]
    heads = head_class.shape[0]
    half = heads // 2
    width = head_queries.shape[1] // heads
    blocks = block_counts.shape[2]
    frames = lax.axis_size("frame")
    groups = lax.axis_size("groups")
    model = out_weight.shape[1] * frames
    bf16 = functools.partial(jax.ShapeDtypeStruct, dtype=jnp.bfloat16)
    first, second = block_lists[:, 0, :, 0], block_lists[:, 0, :, 1]
    lists = (first * 256 + jnp.where(block_counts[:, 0] > 1, second, first)).reshape(-1)

    def call(kernel, ins, outs, *operands, scratch=()):
        return pl.pallas_call(
            kernel,
            out_shape=outs,
            in_specs=ins,
            out_specs=jax.tree.map(lambda _: VMEM, outs),
            scratch_shapes=scratch,
            compiler_params=PARAMS,
            cost_estimate=pl.CostEstimate(flops=2000000000, bytes_accessed=8000000, transcendentals=0),
        )(*operands)

    def exchange(rows):
        split = rows.reshape(frames, pixels // frames, rows.shape[1])
        return lax.all_to_all(
            split, "frame", split_axis=0, concat_axis=0, tiled=True
        ).reshape(rows.shape)

    packed = call(
        functools.partial(pack_kernel, heads, width),
        [SMEM, ANY, ANY, ANY],
        bf16((pixels, 3 * half * width)),
        head_class,
        head_queries,
        head_keys,
        head_values,
        scratch=[pltpu.SemaphoreType.DMA((3, half))],
    )

    def spatial_heads():
        return call(
            functools.partial(spatial_kernel, heads, width, blocks),
            [SMEM, SMEM, ANY, ANY, ANY],
            bf16((pixels, half * width)),
            head_class,
            lists,
            head_queries,
            head_keys,
            head_values,
            scratch=[
                pltpu.VMEM((3, half, pixels, width), jnp.bfloat16),
                pltpu.SemaphoreType.DMA((3, half)),
            ],
        )

    def temporal_heads(arrived):
        return call(
            functools.partial(temporal_kernel, heads, width, blocks),
            [SMEM, SMEM, VMEM],
            bf16((pixels, half * width)),
            head_class,
            lists,
            arrived,
        )

    att_scratch = [pltpu.VMEM((pixels, heads * width), jnp.bfloat16)]
    if frames != 8 or groups != 2:
        spatial = spatial_heads()
        returned = exchange(temporal_heads(exchange(packed)))
        weight = lax.all_gather(out_weight, "frame", axis=1, tiled=True)
        peer, mine = call(
            functools.partial(project_whole_kernel, heads, width),
            [SMEM, VMEM, VMEM, VMEM],
            [bf16((pixels // 2, model))] * 2,
            head_class,
            spatial,
            returned,
            weight,
            scratch=att_scratch,
        )
        received = swap_side(peer)
        return (mine.astype(jnp.float32) + received.astype(jnp.float32)).astype(jnp.bfloat16)

    depth, cols = out_weight.shape[0] // 2, out_weight.shape[1]
    group = lax.axis_index("groups")
    own = lax.dynamic_slice_in_dim(out_weight, group * depth, depth, 0)
    rest = lax.dynamic_slice_in_dim(out_weight, (1 - group) * depth, depth, 0)

    def project(pieces):
        count = len(pieces) // 2
        return call(
            functools.partial(project_pieces_kernel, heads, width, count),
            [SMEM, VMEM, VMEM] + [ANY] * len(pieces),
            [bf16((pixels // 2, count * cols))] * 2,
            head_class,
            spatial,
            returned,
            *pieces,
            scratch=att_scratch
            + [
                pltpu.VMEM((len(pieces), depth, cols), jnp.bfloat16),
                pltpu.SemaphoreType.DMA((len(pieces),)),
            ],
        )

    arrived = exchange(packed)
    held_1, pair_0, spatial = tied(next_line(own), swap_pair(out_weight), spatial_heads())
    held_2, pair_1, rest_1, arrived = tied(
        next_line(held_1), swap_pair(held_1), swap_group(held_1), arrived
    )
    temporal, held_2, pair_1, rest_1 = tied(temporal_heads(arrived), held_2, pair_1, rest_1)
    returned = exchange(temporal)
    held_3, pair_2, pair_rest_1, rest_1 = tied(
        next_line(held_2), swap_pair(held_2), swap_group(pair_1), rest_1
    )
    rest_2, pair_3, rest_3, returned = tied(
        next_line(rest_1), swap_pair(held_3), swap_group(held_3), returned
    )
    pair_rest_2, pair_rest_3 = swap_group(pair_2), swap_pair(rest_3)
    across = [
        lax.dynamic_slice_in_dim(pair_0, start * depth, depth, 0) for start in (group, 1 - group)
    ]
    peer, mine = project(
        [own, rest, *across, held_1, rest_1, pair_1, pair_rest_1, held_2, rest_2, held_3, rest_3]
    )
    received = swap_side(peer)
    last_peer, last_mine = project([pair_2, pair_rest_2, pair_3, pair_rest_3])
    last_received = swap_side(last_peer)
    order = ((0, 0), (0, 1), (1, 0), (1, 1), (2, 0), (3, 0), (2, 1), (3, 1))
    return call(
        functools.partial(join_kernel, order),
        [VMEM] * 4,
        bf16((pixels // 2, model)),
        mine,
        received,
        last_mine,
        last_received,
    )


def solution(mesh):
    placed = (
        P(("groups", "frame"), "head"),
        P(("groups", "frame"), "head"),
        P(("groups", "frame"), "head"),
        P("head", "frame"),
        P("head"),
        P("head", ("groups", "frame"), None, None),
        P("head", ("groups", "frame"), None),
    )
    return jax.shard_map(
        on_device,
        mesh=mesh,
        in_specs=placed,
        out_specs=P(("groups", "frame", "head"), None),
        check_vma=False,
    )
```

time: 76.9 us -> 69.7 us (0.906)
  waiting for transfers between devices: 38.7 us -> 21.5 us
  Pallas kernels: 8.9 us -> 14 us
  starting transfers between devices: 24.9 us -> 29.2 us
  local copies, waits for them, and re-layouts: 2.82 us -> 4.43 us
  other arithmetic: 1.07 us -> 0.01 us
    ppermute x3 -> x4, waiting for transfers between devices: 23.2 us -> 6.01 us  [next_line(): return lax.ppermute(piece, 'frame', [(i, (i + 2) % 8) for i in range(8)])]
    ppermute x5 -> x4, waiting for transfers between devices: 13.3 us -> 0.19 us  [swap_group(): return lax.ppermute(piece, 'groups', [(0, 1), (1, 0)])]
    all_to_all x2, waiting for transfers between devices: 0.01 us -> 8.28 us  [exchange(): lax.all_to_all(split, 'frame', split_axis=0, concat_axis=0, tiled=True)]
    ppermute x5, waiting for transfers between devices: 0.01 us -> 5.95 us  [swap_pair(): return lax.ppermute(piece, 'frame', [(i, i ^ 1) for i in range(8)])]
    pallas_call x4 -> x6, Pallas kernels: 8.9 us -> 14 us  [call(): pl.pallas_call(kernel, out_shape=outs, in_specs=ins, out_specs=jax.tree.m...]
    ppermute x5, starting transfers between devices: 5.55 us -> 9.41 us  [swap_pair(): return lax.ppermute(piece, 'frame', [(i, i ^ 1) for i in range(8)])]
    unnamed x14 -> x18, local copies, waits for them, and re-layouts: 0.22 us -> 1.56 us
    ppermute x1 -> x2, waiting for transfers between devices: 2.27 us -> 1.07 us  [swap_side(): return lax.ppermute(portion, 'head', [(0, 1), (1, 0)])]
  transfers between devices with their start and end apart: 16 -> 17, of which waited for: 7 -> 7; matrix products, arithmetic and copies ran while one was open for 2% -> 4% of each run, Pallas kernels for 6% -> 16%
where the time goes in v2:
time: 69.7 us; the launch traced here: 69.3 us
  starting transfers between devices  29.2 us (42%)
  waiting for transfers between devices  21.5 us (31%)
  Pallas kernels  14 us (20%)
  local copies, waits for them, and re-layouts  4.43 us (6%)
    pallas_call x6, Pallas kernels, call(): pl.pallas_call(kernel, out_shape=outs, in_specs=ins, out_specs=jax.tree.m...  14 us
    ppermute x5, starting transfers between devices, swap_pair(): return lax.ppermute(piece, 'frame', [(i, i ^ 1) for i in range(8)])  9.41 us
    all_to_all x2, starting transfers between devices, exchange(): lax.all_to_all(split, 'frame', split_axis=0, concat_axis=0, tiled=True)  9.19 us
    all_to_all x2, waiting for transfers between devices, exchange(): lax.all_to_all(split, 'frame', split_axis=0, concat_axis=0, tiled=True)  8.28 us
    ppermute x4, waiting for transfers between devices, next_line(): return lax.ppermute(piece, 'frame', [(i, (i + 2) % 8) for i in range(8)])  6.01 us
    ppermute x5, waiting for transfers between devices, swap_pair(): return lax.ppermute(piece, 'frame', [(i, i ^ 1) for i in range(8)])  5.95 us
    ppermute x4, starting transfers between devices, swap_group(): return lax.ppermute(piece, 'groups', [(0, 1), (1, 0)])  5.43 us
    ppermute x4, starting transfers between devices, next_line(): return lax.ppermute(piece, 'frame', [(i, (i + 2) % 8) for i in range(8)])  4.59 us
  transfers between devices with their start and end apart: 17, of which 7 were waited for; matrix products, arithmetic and copies ran while one was open for 4% of the time, Pallas kernels for 16%

profile of v2, /device:TPU:0, one launch (start us, length us, event | category | flops | bytes accessed | tf_op | source)
XLA Modules:
  0.0 69.3 jit_solution(16498445528819454790)
XLA Ops:
  0.0 2.9 %collective-permute-start.1 = (bf16[768,384]{1,0:T(8,128)(2,1)}, bf16[768,384]{1,0:T(8,128)(2,1)S(1)}, u32[]{:S(2)}, u32[]{:S(2)}) collective-permute-start(bf16[768,384]{1,0:T(8,128)(2,1)} %param.10), channel_id=1, source_target_pairs={{0,2},{2,0},{4,6},{6,4},{8,10},{10,8},{12,14},{14,12},{1,3},{3,1},... | collective-permute-start | bytes 1769480 | tf_op jit(solution)/shard_map/ppermute | solution.py:204
  2.9 1.2 %constant_dynamic-slice_fusion.2 = (bf16[384,384]{1,0:T(8,128)(2,1)S(1)}, bf16[384,384]{1,0:T(8,128)(2,1)S(1)}) fusion(bf16[768,384]{1,0:T(8,128)(2,1)} %param.10, s32[]{:T(128)S(6)} %select_n.15, s32[]{:T(128)S(6)} %select_n.13), kind=kLoop, calls=%fused_computation.3 | loop fusion | bytes 1179656 | tf_op jit(solution)/shard_map/dynamic_slice | solution.py:313
  4.2 1.6 %collective-permute-start = (bf16[384,384]{1,0:T(8,128)(2,1)S(1)}, bf16[384,384]{1,0:T(8,128)(2,1)S(1)}, u32[]{:S(2)}, u32[]{:S(2)}) collective-permute-start(bf16[384,384]{1,0:T(8,128)(2,1)S(1)} %get-tuple-element.54.refs_0_), channel_id=1, source_target_pairs={{0,4},{2,6},{4,8},{6,10},{8,12},{10,14},{12,0},{14,2},{1,5},{3,7},... | collective-permute-start | bytes 884744 | tf_op jit(solution)/shard_map/ppermute | solution.py:212
  5.8 1.6 %shard_map.74 = bf16[256,1152]{1,0:T(8,128)(2,1)} custom-call(s32[6]{0:T(128)S(1)} %copy-done.3, bf16[256,768]{1,0:T(8,128)(2,1)S(1)} %copy-done, bf16[256,768]{1,0:T(8,128)(2,1)S(1)} %copy-done.1, bf16[256,768]{1,0:T(8,128)(2,1)S(1)} %copy-done.2), custom_call_target="tpu_custom_call" | custom-call | flops 2000000000 | bytes 8000000 | tf_op jit(solution)/shard_map/pallas_call | solution.py:239
  7.4 3.9 %all-to-all-start = ((bf16[8,32,1152]{2,1,0:T(8,128)(2,1)}), bf16[8,32,1152]{2,1,0:T(8,128)(2,1)S(1)}, u32[]{:S(2)}, u32[]{:S(2)}) async-start(bf16[8,32,1152]{2,1,0:T(8,128)(2,1)} %bitcast), calls=%async_computation | async-start | bytes 1179648 | tf_op jit(solution)/shard_map/all_to_all | solution.py:251
  12.5 2.1 %shard_map.73.spatial_ref = bf16[256,384]{1,0:T(8,128)(2,1)S(1)} custom-call(s32[6]{0:T(128)S(1)} %copy-done.3, s32[24]{0:T(128)S(1)} %select_add_fusion.lists_ref, bf16[256,768]{1,0:T(8,128)(2,1)S(1)} %copy-done, bf16[256,768]{1,0:T(8,128)(2,1)S(1)} %copy-done.1, bf16[256,768]{1,0:T(8,128)(2,1)S(1)} %copy-done.2), custom_call_target="tpu_custom_call" | custom-call | flops 2000000000 | bytes 8000000 | tf_op jit(solution)/shard_map/pallas_call | solution.py:239
  14.6 5.9 %collective-permute-done.1 = bf16[768,384]{1,0:T(8,128)(2,1)S(1)} collective-permute-done((bf16[768,384]{1,0:T(8,128)(2,1)}, bf16[768,384]{1,0:T(8,128)(2,1)S(1)}, u32[]{:S(2)}, u32[]{:S(2)}) %collective-permute-start.1) | collective-permute-done | bytes 589856 | tf_op jit(solution)/shard_map/ppermute | solution.py:204
  20.6 1.6 %collective-permute-start.2 = (bf16[384,384]{1,0:T(8,128)(2,1)S(1)}, bf16[384,384]{1,0:T(8,128)(2,1)S(1)}, u32[]{:S(2)}, u32[]{:S(2)}) collective-permute-start(bf16[384,384]{1,0:T(8,128)(2,1)S(1)} %collective-permute-done.refs_4_), channel_id=1, source_target_pairs={{0,4},{2,6},{4,8},{6,10},{8,12},{10,14},{12,0},{14,2},{1,5},{3,7},... | collective-permute-start | bytes 884744 | tf_op jit(solution)/shard_map/ppermute | solution.py:212
  22.2 2.4 %collective-permute-start.3 = (bf16[384,384]{1,0:T(8,128)(2,1)S(1)}, bf16[384,384]{1,0:T(8,128)(2,1)S(1)}, u32[]{:S(2)}, u32[]{:S(2)}) collective-permute-start(bf16[384,384]{1,0:T(8,128)(2,1)S(1)} %collective-permute-done.refs_4_), channel_id=1, source_target_pairs={{0,2},{2,0},{4,6},{6,4},{8,10},{10,8},{12,14},{14,12},{1,3},{3,1},... | collective-permute-start | bytes 884744 | tf_op jit(solution)/shard_map/ppermute | solution.py:204
  24.5 1.5 %collective-permute-start.4 = (bf16[384,384]{1,0:T(8,128)(2,1)S(1)}, bf16[384,384]{1,0:T(8,128)(2,1)S(1)}, u32[]{:S(2)}, u32[]{:S(2)}) collective-permute-start(bf16[384,384]{1,0:T(8,128)(2,1)S(1)} %collective-permute-done.refs_4_), channel_id=1, source_target_pairs={{0,16},{16,0},{1,17},{17,1},{2,18},{18,2},{3,19},{19,3},{4,20},{20... | collective-permute-start | bytes 884744 | tf_op jit(solution)/shard_map/ppermute | solution.py:208
  26.1 5.0 %collective-permute-done.2.refs_8_ = bf16[384,384]{1,0:T(8,128)(2,1)S(1)} collective-permute-done((bf16[384,384]{1,0:T(8,128)(2,1)S(1)}, bf16[384,384]{1,0:T(8,128)(2,1)S(1)}, u32[]{:S(2)}, u32[]{:S(2)}) %collective-permute-start.2) | collective-permute-done | bytes 294944 | tf_op jit(solution)/shard_map/ppermute | solution.py:212
  31.3 2.2 %all-to-all-done = bf16[8,32,1152]{2,1,0:T(8,128)(2,1)S(1)} async-done(((bf16[8,32,1152]{2,1,0:T(8,128)(2,1)}), bf16[8,32,1152]{2,1,0:T(8,128)(2,1)S(1)}, u32[]{:S(2)}, u32[]{:S(2)}) %all-to-all-start) | async-done | bytes 589856 | tf_op jit(solution)/shard_map/all_to_all | solution.py:251
  33.5 2.0 %shard_map.75 = bf16[256,384]{1,0:T(8,128)(2,1)} custom-call(s32[6]{0:T(128)S(1)} %copy-done.3, s32[24]{0:T(128)S(1)} %select_add_fusion.lists_ref, bf16[256,1152]{1,0:T(8,128)(2,1)S(1)} %bitcast.10), custom_call_target="tpu_custom_call" | custom-call | flops 2000000000 | bytes 8000000 | tf_op jit(solution)/shard_map/pallas_call | solution.py:239
  36.8 1.5 %collective-permute-start.7 = (bf16[384,384]{1,0:T(8,128)(2,1)S(1)}, bf16[384,384]{1,0:T(8,128)(2,1)S(1)}, u32[]{:S(2)}, u32[]{:S(2)}) collective-permute-start(bf16[384,384]{1,0:T(8,128)(2,1)S(1)} %collective-permute-done.3.refs_6_), channel_id=1, source_target_pairs={{0,16},{16,0},{1,17},{17,1},{2,18},{18,2},{3,19},{19,3},{4,20},{20... | collective-permute-start | bytes 884744 | tf_op jit(solution)/shard_map/ppermute | solution.py:208
  38.3 5.3 %all-to-all-start.1 = ((bf16[8,32,384]{2,1,0:T(8,128)(2,1)}), bf16[8,32,384]{2,1,0:T(8,128)(2,1)S(1)}, u32[]{:S(2)}, u32[]{:S(2)}) async-start(bf16[8,32,384]{2,1,0:T(8,128)(2,1)} %bitcast.2), calls=%async_computation.1 | async-start | bytes 393216 | tf_op jit(solution)/shard_map/all_to_all | solution.py:251
  44.5 1.6 %collective-permute-start.10 = (bf16[384,384]{1,0:T(8,128)(2,1)S(1)}, bf16[384,384]{1,0:T(8,128)(2,1)}, u32[]{:S(2)}, u32[]{:S(2)}) collective-permute-start(bf16[384,384]{1,0:T(8,128)(2,1)S(1)} %collective-permute-done.5.refs_10_), channel_id=1, source_target_pairs={{0,16},{16,0},{1,17},{17,1},{2,18},{18,2},{3,19},{19,3},{4,20},{20... | collective-permute-start | bytes 884744 | tf_op jit(solution)/shard_map/ppermute | solution.py:208
  47.1 1.4 %collective-permute-start.9 = (bf16[384,384]{1,0:T(8,128)(2,1)S(1)}, bf16[384,384]{1,0:T(8,128)(2,1)}, u32[]{:S(2)}, u32[]{:S(2)}) collective-permute-start(bf16[384,384]{1,0:T(8,128)(2,1)S(1)} %collective-permute-done.5.refs_10_), channel_id=1, source_target_pairs={{0,2},{2,0},{4,6},{6,4},{8,10},{10,8},{12,14},{14,12},{1,3},{3,1},... | collective-permute-start | bytes 884744 | tf_op jit(solution)/shard_map/ppermute | solution.py:204
  48.4 1.1 %constant_dynamic-slice_fusion = (bf16[384,384]{1,0:T(8,128)(2,1)S(1)}, bf16[384,384]{1,0:T(8,128)(2,1)S(1)}) fusion(bf16[768,384]{1,0:T(8,128)(2,1)} %copy-done.6, s32[]{:T(128)S(6)} %select_n.15, s32[]{:T(128)S(6)} %select_n.13), kind=kLoop, calls=%fused_computation.1 | loop fusion | bytes 1179656 | tf_op jit(solution)/shard_map/dynamic_slice | solution.py:347
  50.4 6.0 %all-to-all-done.1 = bf16[8,32,384]{2,1,0:T(8,128)(2,1)S(1)} async-done(((bf16[8,32,384]{2,1,0:T(8,128)(2,1)}), bf16[8,32,384]{2,1,0:T(8,128)(2,1)S(1)}, u32[]{:S(2)}, u32[]{:S(2)}) %all-to-all-start.1) | async-done | bytes 196640 | tf_op jit(solution)/shard_map/all_to_all | solution.py:251
  56.4 1.9 %collective-permute-start.13 = (bf16[384,384]{1,0:T(8,128)(2,1)}, bf16[384,384]{1,0:T(8,128)(2,1)S(1)}, u32[]{:S(2)}, u32[]{:S(2)}) collective-permute-start(bf16[384,384]{1,0:T(8,128)(2,1)} %collective-permute-done.10.refs_11_), channel_id=1, source_target_pairs={{0,2},{2,0},{4,6},{6,4},{8,10},{10,8},{12,14},{14,12},{1,3},{3,1},... | collective-permute-start | bytes 884744 | tf_op jit(solution)/shard_map/ppermute | solution.py:204
  59.2 4.6 %shard_map.76 = (bf16[128,2304]{1,0:T(8,128)(2,1)S(1)}, bf16[128,2304]{1,0:T(8,128)(2,1)S(1)}) custom-call(s32[6]{0:T(128)S(1)} %copy-done.3, bf16[256,384]{1,0:T(8,128)(2,1)S(1)} %copy-done.5, bf16[256,384]{1,0:T(8,128)(2,1)S(1)} %bitcast.11, bf16[384,384]{1,0:T(8,128)(2,1)S(1)} %get-tuple-element.54.refs_0_, ...), custom_call_target="tpu_custom_call" | custom-call | flops 2000000000 | bytes 8000000 | tf_op jit(solution)/shard_map/pallas_call | solution.py:239
  63.9 2.7 %shard_map.77 = (bf16[128,768]{1,0:T(8,128)(2,1)S(1)}, bf16[128,768]{1,0:T(8,128)(2,1)S(1)}) custom-call(s32[6]{0:T(128)S(1)} %copy-done.3, bf16[256,384]{1,0:T(8,128)(2,1)S(1)} %copy-done.5, bf16[256,384]{1,0:T(8,128)(2,1)S(1)} %bitcast.12, bf16[384,384]{1,0:T(8,128)(2,1)S(1)} %collective-permute-done.6.refs_0_, ...), custom_call_target="tpu_custom_call" | custom-call | flops 2000000000 | bytes 8000000 | tf_op jit(solution)/shard_map/pallas_call | solution.py:239
  67.1 1.1 %collective-permute-done.14.refs_3_ = bf16[128,768]{1,0:T(8,128)(2,1)S(1)} collective-permute-done((bf16[128,768]{1,0:T(8,128)(2,1)S(1)}, bf16[128,768]{1,0:T(8,128)(2,1)S(1)}, u32[]{:S(2)}, u32[]{:S(2)}) %collective-permute-start.14) | collective-permute-done | bytes 196640 | tf_op jit(solution)/shard_map/ppermute | solution.py:216
  68.2 1.1 %shard_map.78 = bf16[128,3072]{1,0:T(8,128)(2,1)} custom-call(bf16[128,2304]{1,0:T(8,128)(2,1)S(1)} %get-tuple-element.45.refs_0_, bf16[128,2304]{1,0:T(8,128)(2,1)S(1)} %collective-permute-done.11.refs_1_, bf16[128,768]{1,0:T(8,128)(2,1)S(1)} %get-tuple-element.49.refs_2_, bf16[128,768]{1,0:T(8,128)(2,1)S(1)} %collective-permute-done.14.refs_3_), custom_call_target="tpu_custom_call" | custom-call | flops 2000000000 | bytes 8000000 | tf_op jit(solution)/shard_map/pallas_call | solution.py:239
  (45 shorter events, 7.0 us)
Async XLA Ops:
  0.0 20.6 %collective-permute-start.1 = (bf16[768,384]{1,0:T(8,128)(2,1)}, bf16[768,384]{1,0:T(8,128)(2,1)S(1)}, u32[]{:S(2)}, u32[]{:S(2)}) collective-permute-start(bf16[768,384]{1,0:T(8,128)(2,1)} %param.10), channel_id=1, source_target_pairs={{0,2},{2,0},{4,6},{6,4},{8,10},{10,8},{12,14},{14,12},{1,3},{3,1},... | collective-permute-start | bytes 1769480 | tf_op jit(solution)/shard_map/ppermute | solution.py:204
  2.9 2.9 %copy-start = (bf16[256,768]{1,0:T(8,128)(2,1)S(1)}, bf16[256,768]{1,0:T(8,128)(2,1)}, u32[]{:S(2)}) copy-start(bf16[256,768]{1,0:T(8,128)(2,1)} %q_ref.3) | copy-start | bytes 1179652
  2.9 2.9 %copy-start.1 = (bf16[256,768]{1,0:T(8,128)(2,1)S(1)}, bf16[256,768]{1,0:T(8,128)(2,1)}, u32[]{:S(2)}) copy-start(bf16[256,768]{1,0:T(8,128)(2,1)} %k_ref.3) | copy-start | bytes 1179652
  2.9 2.9 %copy-start.2 = (bf16[256,768]{1,0:T(8,128)(2,1)S(1)}, bf16[256,768]{1,0:T(8,128)(2,1)}, u32[]{:S(2)}) copy-start(bf16[256,768]{1,0:T(8,128)(2,1)} %v_ref.3) | copy-start | bytes 1179652
  4.2 1.7 %copy-start.3 = (s32[6]{0:T(128)S(1)}, s32[6]{0:T(128)}, u32[]{:S(2)}) copy-start(s32[6]{0:T(128)} %class_ref.9) | copy-start | bytes 76
  4.2 10.5 %collective-permute-start = (bf16[384,384]{1,0:T(8,128)(2,1)S(1)}, bf16[384,384]{1,0:T(8,128)(2,1)S(1)}, u32[]{:S(2)}, u32[]{:S(2)}) collective-permute-start(bf16[384,384]{1,0:T(8,128)(2,1)S(1)} %get-tuple-element.54.refs_0_), channel_id=1, source_target_pairs={{0,4},{2,6},{4,8},{6,10},{8,12},{10,14},{12,0},{14,2},{1,5},{3,7},... | collective-permute-start | bytes 884744 | tf_op jit(solution)/shard_map/ppermute | solution.py:212
  7.4 4.0 %copy-start.7 = (s32[6,1,4,2]{0,3,2,1:T(2,128)S(1)}, s32[6,1,4,2]{0,3,2,1:T(2,128)}, u32[]{:S(2)}) copy-start(s32[6,1,4,2]{0,3,2,1:T(2,128)} %param.12) | copy-start | bytes 580
  7.4 26.1 %all-to-all-start = ((bf16[8,32,1152]{2,1,0:T(8,128)(2,1)}), bf16[8,32,1152]{2,1,0:T(8,128)(2,1)S(1)}, u32[]{:S(2)}, u32[]{:S(2)}) async-start(bf16[8,32,1152]{2,1,0:T(8,128)(2,1)} %bitcast), calls=%async_computation | async-start | bytes 1179648 | tf_op jit(solution)/shard_map/all_to_all | solution.py:251
  14.6 20.9 %copy-start.4 = (bf16[256,384]{1,0:T(8,128)(2,1)}, bf16[256,384]{1,0:T(8,128)(2,1)S(1)}, u32[]{:S(2)}) copy-start(bf16[256,384]{1,0:T(8,128)(2,1)S(1)} %shard_map.73.spatial_ref) | copy-start | bytes 589828
  20.6 14.9 %copy-start.6 = (bf16[768,384]{1,0:T(8,128)(2,1)}, bf16[768,384]{1,0:T(8,128)(2,1)S(1)}, u32[]{:S(2)}) copy-start(bf16[768,384]{1,0:T(8,128)(2,1)S(1)} %collective-permute-done.1) | copy-start | bytes 1769476
  20.6 10.5 %collective-permute-start.2 = (bf16[384,384]{1,0:T(8,128)(2,1)S(1)}, bf16[384,384]{1,0:T(8,128)(2,1)S(1)}, u32[]{:S(2)}, u32[]{:S(2)}) collective-permute-start(bf16[384,384]{1,0:T(8,128)(2,1)S(1)} %collective-permute-done.refs_4_), channel_id=1, source_target_pairs={{0,4},{2,6},{4,8},{6,10},{8,12},{10,14},{12,0},{14,2},{1,5},{3,7},... | collective-permute-start | bytes 884744 | tf_op jit(solution)/shard_map/ppermute | solution.py:212
  22.2 8.9 %collective-permute-start.3 = (bf16[384,384]{1,0:T(8,128)(2,1)S(1)}, bf16[384,384]{1,0:T(8,128)(2,1)S(1)}, u32[]{:S(2)}, u32[]{:S(2)}) collective-permute-start(bf16[384,384]{1,0:T(8,128)(2,1)S(1)} %collective-permute-done.refs_4_), channel_id=1, source_target_pairs={{0,2},{2,0},{4,6},{6,4},{8,10},{10,8},{12,14},{14,12},{1,3},{3,1},... | collective-permute-start | bytes 884744 | tf_op jit(solution)/shard_map/ppermute | solution.py:204
  24.5 6.7 %collective-permute-start.4 = (bf16[384,384]{1,0:T(8,128)(2,1)S(1)}, bf16[384,384]{1,0:T(8,128)(2,1)S(1)}, u32[]{:S(2)}, u32[]{:S(2)}) collective-permute-start(bf16[384,384]{1,0:T(8,128)(2,1)S(1)} %collective-permute-done.refs_4_), channel_id=1, source_target_pairs={{0,16},{16,0},{1,17},{17,1},{2,18},{18,2},{3,19},{19,3},{4,20},{20... | collective-permute-start | bytes 884744 | tf_op jit(solution)/shard_map/ppermute | solution.py:208
  35.5 9.0 %collective-permute-start.5 = (bf16[384,384]{1,0:T(8,128)(2,1)S(1)}, bf16[384,384]{1,0:T(8,128)(2,1)S(1)}, u32[]{:S(2)}, u32[]{:S(2)}) collective-permute-start(bf16[384,384]{1,0:T(8,128)(2,1)S(1)} %collective-permute-done.2.refs_8_), channel_id=1, source_target_pairs={{0,4},{2,6},{4,8},{6,10},{8,12},{10,14},{12,0},{14,2},{1,5},{3,7},... | collective-permute-start | bytes 884744 | tf_op jit(solution)/shard_map/ppermute | solution.py:212
  36.0 8.6 %collective-permute-start.6 = (bf16[384,384]{1,0:T(8,128)(2,1)S(1)}, bf16[384,384]{1,0:T(8,128)(2,1)S(1)}, u32[]{:S(2)}, u32[]{:S(2)}) collective-permute-start(bf16[384,384]{1,0:T(8,128)(2,1)S(1)} %collective-permute-done.2.refs_8_), channel_id=1, source_target_pairs={{0,2},{2,0},{4,6},{6,4},{8,10},{10,8},{12,14},{14,12},{1,3},{3,1},... | collective-permute-start | bytes 884744 | tf_op jit(solution)/shard_map/ppermute | solution.py:204
  36.8 7.7 %collective-permute-start.7 = (bf16[384,384]{1,0:T(8,128)(2,1)S(1)}, bf16[384,384]{1,0:T(8,128)(2,1)S(1)}, u32[]{:S(2)}, u32[]{:S(2)}) collective-permute-start(bf16[384,384]{1,0:T(8,128)(2,1)S(1)} %collective-permute-done.3.refs_6_), channel_id=1, source_target_pairs={{0,16},{16,0},{1,17},{17,1},{2,18},{18,2},{3,19},{19,3},{4,20},{20... | collective-permute-start | bytes 884744 | tf_op jit(solution)/shard_map/ppermute | solution.py:208
  38.3 18.1 %all-to-all-start.1 = ((bf16[8,32,384]{2,1,0:T(8,128)(2,1)}), bf16[8,32,384]{2,1,0:T(8,128)(2,1)S(1)}, u32[]{:S(2)}, u32[]{:S(2)}) async-start(bf16[8,32,384]{2,1,0:T(8,128)(2,1)} %bitcast.2), calls=%async_computation.1 | async-start | bytes 393216 | tf_op jit(solution)/shard_map/all_to_all | solution.py:251
  44.5 11.9 %collective-permute-start.10 = (bf16[384,384]{1,0:T(8,128)(2,1)S(1)}, bf16[384,384]{1,0:T(8,128)(2,1)}, u32[]{:S(2)}, u32[]{:S(2)}) collective-permute-start(bf16[384,384]{1,0:T(8,128)(2,1)S(1)} %collective-permute-done.5.refs_10_), channel_id=1, source_target_pairs={{0,16},{16,0},{1,17},{17,1},{2,18},{18,2},{3,19},{19,3},{4,20},{20... | collective-permute-start | bytes 884744 | tf_op jit(solution)/shard_map/ppermute | solution.py:208
  46.1 10.3 %collective-permute-start.8 = (bf16[384,384]{1,0:T(8,128)(2,1)S(1)}, bf16[384,384]{1,0:T(8,128)(2,1)}, u32[]{:S(2)}, u32[]{:S(2)}) collective-permute-start(bf16[384,384]{1,0:T(8,128)(2,1)S(1)} %collective-permute-done.4.refs_5_), channel_id=1, source_target_pairs={{0,4},{2,6},{4,8},{6,10},{8,12},{10,14},{12,0},{14,2},{1,5},{3,7},... | collective-permute-start | bytes 884744 | tf_op jit(solution)/shard_map/ppermute | solution.py:212
  47.1 9.3 %collective-permute-start.9 = (bf16[384,384]{1,0:T(8,128)(2,1)S(1)}, bf16[384,384]{1,0:T(8,128)(2,1)}, u32[]{:S(2)}, u32[]{:S(2)}) collective-permute-start(bf16[384,384]{1,0:T(8,128)(2,1)S(1)} %collective-permute-done.5.refs_10_), channel_id=1, source_target_pairs={{0,2},{2,0},{4,6},{6,4},{8,10},{10,8},{12,14},{14,12},{1,3},{3,1},... | collective-permute-start | bytes 884744 | tf_op jit(solution)/shard_map/ppermute | solution.py:204
  49.5 14.4 %collective-permute-start.12 = (bf16[384,384]{1,0:T(8,128)(2,1)S(1)}, bf16[384,384]{1,0:T(8,128)(2,1)}, u32[]{:S(2)}, u32[]{:S(2)}) collective-permute-start(bf16[384,384]{1,0:T(8,128)(2,1)S(1)} %collective-permute-done.6.refs_0_), channel_id=1, source_target_pairs={{0,16},{16,0},{1,17},{17,1},{2,18},{18,2},{3,19},{19,3},{4,20},{20... | collective-permute-start | bytes 884744 | tf_op jit(solution)/shard_map/ppermute | solution.py:208
  56.4 7.5 %collective-permute-start.13 = (bf16[384,384]{1,0:T(8,128)(2,1)}, bf16[384,384]{1,0:T(8,128)(2,1)S(1)}, u32[]{:S(2)}, u32[]{:S(2)}) collective-permute-start(bf16[384,384]{1,0:T(8,128)(2,1)} %collective-permute-done.10.refs_11_), channel_id=1, source_target_pairs={{0,2},{2,0},{4,6},{6,4},{8,10},{10,8},{12,14},{14,12},{1,3},{3,1},... | collective-permute-start | bytes 884744 | tf_op jit(solution)/shard_map/ppermute | solution.py:204
  63.8 4.4 %collective-permute-start.11 = (bf16[128,2304]{1,0:T(8,128)(2,1)S(1)}, bf16[128,2304]{1,0:T(8,128)(2,1)S(1)}, u32[]{:S(2)}, u32[]{:S(2)}) collective-permute-start(bf16[128,2304]{1,0:T(8,128)(2,1)S(1)} %get-tuple-element.46), channel_id=1, source_target_pairs={{0,1},{1,0},{2,3},{3,2},{4,5},{5,4},{6,7},{7,6},{8,9},{9,8},{10,11... | collective-permute-start | bytes 1769480 | tf_op jit(solution)/shard_map/ppermute | solution.py:216
  66.6 1.6 %collective-permute-start.14 = (bf16[128,768]{1,0:T(8,128)(2,1)S(1)}, bf16[128,768]{1,0:T(8,128)(2,1)S(1)}, u32[]{:S(2)}, u32[]{:S(2)}) collective-permute-start(bf16[128,768]{1,0:T(8,128)(2,1)S(1)} %get-tuple-element.50), channel_id=1, source_target_pairs={{0,1},{1,0},{2,3},{3,2},{4,5},{5,4},{6,7},{7,6},{8,9},{9,8},{10,11... | collective-permute-start | bytes 589832 | tf_op jit(solution)/shard_map/ppermute | solution.py:216
  (2 other events, 1.6 us)

commit v3 on v2

--- a/solution.py
+++ b/solution.py
@@ -10,7 +10,8 @@
 VMEM = pl.BlockSpec(memory_space=pltpu.VMEM)
 SMEM = pl.BlockSpec(memory_space=pltpu.SMEM)
 ANY = pl.BlockSpec(memory_space=pl.ANY)
-PARAMS = pltpu.CompilerParams(vmem_limit_bytes=40 * 1024 * 1024)
+COSTS = {"pack": 1, "lists": 10000, "spatial": 2000, "temporal": 10000, "join": 10000, "add": 5000, "project": 20000}
+PARAMS = pltpu.CompilerParams(vmem_limit_bytes=16 * 1024 * 1024)
 
 
 def head_of_rank(class_ref, kind, rank, heads):
@@ -75,6 +76,14 @@
     return (total / denominator).astype(jnp.bfloat16)
 
 
+def lists_kernel(heads, blocks, lists_ref, counts_ref, out_ref):
+    for head in range(heads):
+        for block in range(blocks):
+            first = lists_ref[head, 2 * block]
+            second = jnp.where(counts_ref[head, block] > 1, lists_ref[head, 2 * block + 1], first)
+            out_ref[head * blocks + block] = first * 256 + second
+
+
 def listed_blocks(lists_ref, head, blocks):
     listed = []
     for block in range(blocks):
@@ -124,50 +133,41 @@
 
 
 def place_heads(heads, width, class_ref, spatial_ref, temporal_ref, att_ref):
+    rows = att_ref.shape[0] // 2
+    side = lax.axis_index("head")
     for kind, ref in ((0, spatial_ref), (1, temporal_ref)):
         for rank in range(heads // 2):
             head = head_of_rank(class_ref, kind, rank, heads)
-            att_ref[:, columns(head, width)] = ref[:, rank * width : (rank + 1) * width]
+            for place, part in ((0, 1 - side), (1, side)):
+                take = pl.ds(pl.multiple_of(part * rows, rows), rows)
+                att_ref[place * rows : (place + 1) * rows, columns(head, width)] = ref[
+                    take, rank * width : (rank + 1) * width
+                ]
 
 
 def project_pieces_kernel(heads, width, count, class_ref, spatial_ref, temporal_ref, *refs):
-    pieces, (peer_ref, mine_ref, att_ref, held_ref, sems) = refs[: 2 * count], refs[2 * count :]
-    copies = [
-        pltpu.make_async_copy(piece, held_ref.at[index], sems.at[index])
-        for index, piece in enumerate(pieces)
-    ]
-    for copy in copies:
-        copy.start()
+    pieces, (peer_ref, mine_ref, att_ref) = refs[: 2 * count], refs[2 * count :]
     place_heads(heads, width, class_ref, spatial_ref, temporal_ref, att_ref)
     depth, cols = pieces[0].shape
     rows = peer_ref.shape[0]
     half = lax.axis_index("groups")
-    side = lax.axis_index("head")
-    for index in range(count):
-        take = slice(index * cols, (index + 1) * cols)
-        copies[2 * index].wait()
-        total = jnp.dot(
-            att_ref[:, columns(half, depth)],
-            held_ref[2 * index],
-            preferred_element_type=jnp.float32,
-        )
-        copies[2 * index + 1].wait()
-        total += jnp.dot(
-            att_ref[:, columns(1 - half, depth)],
-            held_ref[2 * index + 1],
-            preferred_element_type=jnp.float32,
-        )
+    attended = jnp.concatenate(
+        [att_ref[:, columns(half, depth)], att_ref[:, columns(1 - half, depth)]], axis=1
+    )
+    for index in range(0, count, 2):
+        shards = range(index, min(index + 2, count))
+        weight = jnp.concatenate(
+            [
+                jnp.concatenate([pieces[2 * at][...], pieces[2 * at + 1][...]], axis=0)
+                for at in shards
+            ],
+            axis=1,
+        )
+        total = jnp.dot(attended, weight, preferred_element_type=jnp.float32)
         total = total.astype(peer_ref.dtype)
-
-        @pl.when(side == 0)
-        def _():
-            mine_ref[:, take] = total[:rows]
-            peer_ref[:, take] = total[rows:]
-
-        @pl.when(side != 0)
-        def _():
-            mine_ref[:, take] = total[rows:]
-            peer_ref[:, take] = total[:rows]
+        take = slice(index * cols, (index + len(shards)) * cols)
+        peer_ref[:, take] = total[:rows]
+        mine_ref[:, take] = total[rows:]
 
 
 def project_whole_kernel(
@@ -175,11 +175,11 @@
 ):
     place_heads(heads, width, class_ref, spatial_ref, temporal_ref, att_ref)
     rows = peer_ref.shape[0]
-    side = lax.axis_index("head")
-    for out_ref, part in ((peer_ref, 1 - side), (mine_ref, side)):
-        take = pl.ds(pl.multiple_of(part * rows, rows), rows)
+    for place, out_ref in enumerate((peer_ref, mine_ref)):
         out_ref[...] = jnp.dot(
-            att_ref[take, :], weight_ref[...], preferred_element_type=jnp.float32
+            att_ref[place * rows : (place + 1) * rows, :],
+            weight_ref[...],
+            preferred_element_type=jnp.float32,
         ).astype(out_ref.dtype)
 
 
@@ -232,18 +232,15 @@
     groups = lax.axis_size("groups")
     model = out_weight.shape[1] * frames
     bf16 = functools.partial(jax.ShapeDtypeStruct, dtype=jnp.bfloat16)
-    first, second = block_lists[:, 0, :, 0], block_lists[:, 0, :, 1]
-    lists = (first * 256 + jnp.where(block_counts[:, 0] > 1, second, first)).reshape(-1)
-
-    def call(kernel, ins, outs, *operands, scratch=()):
+    def call(kernel, ins, outs, *operands, scratch=(), out_spec=VMEM):
         return pl.pallas_call(
             kernel,
             out_shape=outs,
             in_specs=ins,
-            out_specs=jax.tree.map(lambda _: VMEM, outs),
+            out_specs=jax.tree.map(lambda _: out_spec, outs),
             scratch_shapes=scratch,
             compiler_params=PARAMS,
-            cost_estimate=pl.CostEstimate(flops=2000000000, bytes_accessed=8000000, transcendentals=0),
+            cost_estimate=pl.CostEstimate(flops=next(v for k, v in COSTS.items() if k in str(kernel)) * 10**6, bytes_accessed=1000, transcendentals=0),
         )(*operands)
 
     def exchange(rows):
@@ -252,6 +249,14 @@
             split, "frame", split_axis=0, concat_axis=0, tiled=True
         ).reshape(rows.shape)
 
+    lists = call(
+        functools.partial(lists_kernel, heads, blocks),
+        [SMEM, SMEM],
+        jax.ShapeDtypeStruct((heads * blocks,), jnp.int32),
+        block_lists.reshape(heads, -1),
+        block_counts.reshape(heads, -1),
+        out_spec=SMEM,
+    )
     packed = call(
         functools.partial(pack_kernel, heads, width),
         [SMEM, ANY, ANY, ANY],
@@ -316,38 +321,33 @@
         count = len(pieces) // 2
         return call(
             functools.partial(project_pieces_kernel, heads, width, count),
-            [SMEM, VMEM, VMEM] + [ANY] * len(pieces),
+            [SMEM] + [VMEM] * (2 + len(pieces)),
             [bf16((pixels // 2, count * cols))] * 2,
             head_class,
             spatial,
             returned,
             *pieces,
-            scratch=att_scratch
-            + [
-                pltpu.VMEM((len(pieces), depth, cols), jnp.bfloat16),
-                pltpu.SemaphoreType.DMA((len(pieces),)),
-            ],
+            scratch=att_scratch,
         )
 
     arrived = exchange(packed)
-    held_1, pair_0, spatial = tied(next_line(own), swap_pair(out_weight), spatial_heads())
-    held_2, pair_1, rest_1, arrived = tied(
-        next_line(held_1), swap_pair(held_1), swap_group(held_1), arrived
-    )
-    temporal, held_2, pair_1, rest_1 = tied(temporal_heads(arrived), held_2, pair_1, rest_1)
-    returned = exchange(temporal)
-    held_3, pair_2, pair_rest_1, rest_1 = tied(
-        next_line(held_2), swap_pair(held_2), swap_group(pair_1), rest_1
-    )
-    rest_2, pair_3, rest_3, returned = tied(
-        next_line(rest_1), swap_pair(held_3), swap_group(held_3), returned
+    held_1, pair_0, lists = tied(next_line(own), swap_pair(own), lists)
+    pair_1, rest_1, pair_rest_0, spatial = tied(
+        swap_pair(held_1), swap_group(held_1), swap_group(pair_0), spatial_heads()
+    )
+    pair_rest_1 = swap_group(pair_1)
+    held_2, arrived = tied(next_line(held_1), arrived)
+    returned = exchange(temporal_heads(arrived))
+    held_3, pair_2, rest_2, pair_rest_1 = tied(
+        next_line(held_2), swap_pair(held_2), swap_group(held_2), pair_rest_1
+    )
+    pair_3, rest_3, returned, pair_2 = tied(
+        swap_pair(held_3), swap_group(held_3), returned, pair_2
     )
     pair_rest_2, pair_rest_3 = swap_group(pair_2), swap_pair(rest_3)
-    across = [
-        lax.dynamic_slice_in_dim(pair_0, start * depth, depth, 0) for start in (group, 1 - group)
-    ]
     peer, mine = project(
-        [own, rest, *across, held_1, rest_1, pair_1, pair_rest_1, held_2, rest_2, held_3, rest_3]
+        [own, rest, pair_0, pair_rest_0, held_1, rest_1, pair_1, pair_rest_1, held_2, rest_2]
+        + [held_3, rest_3]
     )
     received = swap_side(peer)
     last_peer, last_mine = project([pair_2, pair_rest_2, pair_3, pair_rest_3])

time: 69.7 us -> 64.5 us (0.925)
  waiting for transfers between devices: 21.5 us -> 18.7 us
  Pallas kernels: 14 us -> 11.8 us
  local copies, waits for them, and re-layouts: 4.43 us -> 3.73 us
    ppermute x4 -> x3, waiting for transfers between devices: 6.01 us -> 0.56 us  [next_line(): return lax.ppermute(piece, 'frame', [(i, (i + 2) % 8) for i in range(8)])]
    ppermute x4 -> x6, waiting for transfers between devices: 0.19 us -> 3.3 us  [swap_group(): return lax.ppermute(piece, 'groups', [(0, 1), (1, 0)])]
    pallas_call x6 -> x7, Pallas kernels: 14 us -> 11.8 us  [call(): pl.pallas_call(kernel, out_shape=outs, in_specs=ins, out_specs=jax.tree.m...]
    ppermute x4 -> x3, starting transfers between devices: 4.59 us -> 5.91 us  [next_line(): return lax.ppermute(piece, 'frame', [(i, (i + 2) % 8) for i in range(8)])]
    ppermute x5, starting transfers between devices: 9.41 us -> 8.23 us  [swap_pair(): return lax.ppermute(piece, 'frame', [(i, i ^ 1) for i in range(8)])]
    dynamic_slice x1 -> x0, local copies, waits for them, and re-layouts: 1.11 us -> none  [on_device(): lax.dynamic_slice_in_dim(pair_0, start * depth, depth, 0)]
    all_to_all x2, waiting for transfers between devices: 8.28 us -> 7.25 us  [exchange(): lax.all_to_all(split, 'frame', split_axis=0, concat_axis=0, tiled=True)]
    ppermute x4 -> x6, starting transfers between devices: 5.43 us -> 6.26 us  [swap_group(): return lax.ppermute(piece, 'groups', [(0, 1), (1, 0)])]
  transfers between devices with their start and end apart: 17 -> 18, of which waited for: 7 -> 9; matrix products, arithmetic and copies ran while one was open for 4% -> 0% of each run, Pallas kernels for 16% -> 17%
where the time goes in v3:
time: 64.5 us; the launch traced here: 64.1 us
  starting transfers between devices  29.7 us (46%)
  waiting for transfers between devices  18.7 us (29%)
  Pallas kernels  11.8 us (18%)
  local copies, waits for them, and re-layouts  3.73 us (6%)
    pallas_call x7, Pallas kernels, call(): pl.pallas_call(kernel, out_shape=outs, in_specs=ins, out_specs=jax.tree.m...  11.8 us
    all_to_all x2, starting transfers between devices, exchange(): lax.all_to_all(split, 'frame', split_axis=0, concat_axis=0, tiled=True)  9.15 us
    ppermute x5, starting transfers between devices, swap_pair(): return lax.ppermute(piece, 'frame', [(i, i ^ 1) for i in range(8)])  8.23 us
    all_to_all x2, waiting for transfers between devices, exchange(): lax.all_to_all(split, 'frame', split_axis=0, concat_axis=0, tiled=True)  7.25 us
    ppermute x6, starting transfers between devices, swap_group(): return lax.ppermute(piece, 'groups', [(0, 1), (1, 0)])  6.26 us
    ppermute x5, waiting for transfers between devices, swap_pair(): return lax.ppermute(piece, 'frame', [(i, i ^ 1) for i in range(8)])  6.2 us
    ppermute x3, starting transfers between devices, next_line(): return lax.ppermute(piece, 'frame', [(i, (i + 2) % 8) for i in range(8)])  5.91 us
    ppermute x6, waiting for transfers between devices, swap_group(): return lax.ppermute(piece, 'groups', [(0, 1), (1, 0)])  3.3 us
  transfers between devices with their start and end apart: 18, of which 9 were waited for; matrix products, arithmetic and copies ran while one was open for 0% of the time, Pallas kernels for 17%

profile of v3, /device:TPU:0, one launch (start us, length us, event | category | flops | bytes accessed | tf_op | source)
XLA Modules:
  0.0 64.1 jit_solution(8472218471627244660)
XLA Ops:
  0.0 1.2 %constant_dynamic-slice_fusion = (bf16[384,384]{1,0:T(8,128)(2,1)S(1)}, bf16[384,384]{1,0:T(8,128)(2,1)S(1)}) fusion(bf16[768,384]{1,0:T(8,128)(2,1)} %param.10, s32[]{:T(128)S(6)} %select_n.7, s32[]{:T(128)S(6)} %select_n.6), kind=kLoop, calls=%fused_computation | loop fusion | bytes 1179656 | tf_op jit(solution)/shard_map/dynamic_slice | solution.py:318
  1.2 3.1 %collective-permute-start = (bf16[384,384]{1,0:T(8,128)(2,1)S(1)}, bf16[384,384]{1,0:T(8,128)(2,1)S(1)}, u32[]{:S(2)}, u32[]{:S(2)}) collective-permute-start(bf16[384,384]{1,0:T(8,128)(2,1)S(1)} %get-tuple-element.48.refs_0_), channel_id=1, source_target_pairs={{0,4},{2,6},{4,8},{6,10},{8,12},{10,14},{12,0},{14,2},{1,5},{3,7},... | collective-permute-start | bytes 884744 | tf_op jit(solution)/shard_map/ppermute | solution.py:212
  4.3 1.5 %collective-permute-start.1 = (bf16[384,384]{1,0:T(8,128)(2,1)S(1)}, bf16[384,384]{1,0:T(8,128)(2,1)S(1)}, u32[]{:S(2)}, u32[]{:S(2)}) collective-permute-start(bf16[384,384]{1,0:T(8,128)(2,1)S(1)} %get-tuple-element.48.refs_0_), channel_id=1, source_target_pairs={{0,2},{2,0},{4,6},{6,4},{8,10},{10,8},{12,14},{14,12},{1,3},{3,1},... | collective-permute-start | bytes 884744 | tf_op jit(solution)/shard_map/ppermute | solution.py:204
  5.8 1.6 %shard_map.75 = bf16[256,1152]{1,0:T(8,128)(2,1)} custom-call(s32[6]{0:T(128)S(1)} %copy-done.3, bf16[256,768]{1,0:T(8,128)(2,1)S(1)} %copy-done, bf16[256,768]{1,0:T(8,128)(2,1)S(1)} %copy-done.1, bf16[256,768]{1,0:T(8,128)(2,1)S(1)} %copy-done.2), custom_call_target="tpu_custom_call" | custom-call | flops 1000000 | bytes 1000 | tf_op jit(solution)/shard_map/pallas_call | solution.py:236
  7.4 3.9 %all-to-all-start = ((bf16[8,32,1152]{2,1,0:T(8,128)(2,1)}), bf16[8,32,1152]{2,1,0:T(8,128)(2,1)S(1)}, u32[]{:S(2)}, u32[]{:S(2)}) async-start(bf16[8,32,1152]{2,1,0:T(8,128)(2,1)} %bitcast.2), calls=%async_computation | async-start | bytes 1179648 | tf_op jit(solution)/shard_map/all_to_all | solution.py:248
  11.5 1.3 %shard_map.73.lists_ref = s32[24]{0:T(128)S(1)} custom-call(s32[6,8]{1,0:T(8,128)S(1)} %copy.8.lists_ref, s32[6,4]{1,0:T(8,128)S(1)} %copy.9.counts_ref), custom_call_target="tpu_custom_call" | custom-call | flops 10000000000 | bytes 1000 | tf_op jit(solution)/shard_map/pallas_call | solution.py:236
  13.4 2.5 %collective-permute-start.2 = (bf16[384,384]{1,0:T(8,128)(2,1)S(1)}, bf16[384,384]{1,0:T(8,128)(2,1)S(1)}, u32[]{:S(2)}, u32[]{:S(2)}) collective-permute-start(bf16[384,384]{1,0:T(8,128)(2,1)S(1)} %collective-permute-done.refs_4_), channel_id=1, source_target_pairs={{0,2},{2,0},{4,6},{6,4},{8,10},{10,8},{12,14},{14,12},{1,3},{3,1},... | collective-permute-start | bytes 884744 | tf_op jit(solution)/shard_map/ppermute | solution.py:204
  15.8 1.5 %collective-permute-start.3 = (bf16[384,384]{1,0:T(8,128)(2,1)S(1)}, bf16[384,384]{1,0:T(8,128)(2,1)S(1)}, u32[]{:S(2)}, u32[]{:S(2)}) collective-permute-start(bf16[384,384]{1,0:T(8,128)(2,1)S(1)} %collective-permute-done.refs_4_), channel_id=1, source_target_pairs={{0,16},{16,0},{1,17},{17,1},{2,18},{18,2},{3,19},{19,3},{4,20},{20... | collective-permute-start | bytes 884744 | tf_op jit(solution)/shard_map/ppermute | solution.py:208
  17.8 2.2 %collective-permute-start.5 = (bf16[384,384]{1,0:T(8,128)(2,1)S(1)}, bf16[384,384]{1,0:T(8,128)(2,1)}, u32[]{:S(2)}, u32[]{:S(2)}) collective-permute-start(bf16[384,384]{1,0:T(8,128)(2,1)S(1)} %collective-permute-done.refs_4_), channel_id=1, source_target_pairs={{0,4},{2,6},{4,8},{6,10},{8,12},{10,14},{12,0},{14,2},{1,5},{3,7},... | collective-permute-start | bytes 884744 | tf_op jit(solution)/shard_map/ppermute | solution.py:212
  20.0 2.1 %shard_map.74.spatial_ref = bf16[256,384]{1,0:T(8,128)(2,1)S(1)} custom-call(s32[6]{0:T(128)S(1)} %copy-done.3, s32[24]{0:T(128)S(1)} %shard_map.73.lists_ref, bf16[256,768]{1,0:T(8,128)(2,1)S(1)} %copy-done, bf16[256,768]{1,0:T(8,128)(2,1)S(1)} %copy-done.1, bf16[256,768]{1,0:T(8,128)(2,1)S(1)} %copy-done.2), custom_call_target="tpu_custom_call" | custom-call | flops 2000000000 | bytes 1000 | tf_op jit(solution)/shard_map/pallas_call | solution.py:236
  22.8 4.1 %collective-permute-done.2.refs_6_ = bf16[384,384]{1,0:T(8,128)(2,1)S(1)} collective-permute-done((bf16[384,384]{1,0:T(8,128)(2,1)S(1)}, bf16[384,384]{1,0:T(8,128)(2,1)S(1)}, u32[]{:S(2)}, u32[]{:S(2)}) %collective-permute-start.2) | collective-permute-done | bytes 294944 | tf_op jit(solution)/shard_map/ppermute | solution.py:204
  26.9 1.9 %collective-permute-done.4.refs_3_ = bf16[384,384]{1,0:T(8,128)(2,1)S(1)} collective-permute-done((bf16[384,384]{1,0:T(8,128)(2,1)S(1)}, bf16[384,384]{1,0:T(8,128)(2,1)S(1)}, u32[]{:S(2)}, u32[]{:S(2)}) %collective-permute-start.4) | collective-permute-done | bytes 294944 | tf_op jit(solution)/shard_map/ppermute | solution.py:208
  29.5 1.5 %collective-permute-start.9 = (bf16[384,384]{1,0:T(8,128)(2,1)S(1)}, bf16[384,384]{1,0:T(8,128)(2,1)S(1)}, u32[]{:S(2)}, u32[]{:S(2)}) collective-permute-start(bf16[384,384]{1,0:T(8,128)(2,1)S(1)} %collective-permute-done.2.refs_6_), channel_id=1, source_target_pairs={{0,16},{16,0},{1,17},{17,1},{2,18},{18,2},{3,19},{19,3},{4,20},{20... | collective-permute-start | bytes 884744 | tf_op jit(solution)/shard_map/ppermute | solution.py:208
  31.1 2.0 %all-to-all-done = bf16[8,32,1152]{2,1,0:T(8,128)(2,1)S(1)} async-done(((bf16[8,32,1152]{2,1,0:T(8,128)(2,1)}), bf16[8,32,1152]{2,1,0:T(8,128)(2,1)S(1)}, u32[]{:S(2)}, u32[]{:S(2)}) %all-to-all-start) | async-done | bytes 589856 | tf_op jit(solution)/shard_map/all_to_all | solution.py:248
  34.5 1.5 %collective-permute-start.8 = (bf16[384,384]{1,0:T(8,128)(2,1)}, bf16[384,384]{1,0:T(8,128)(2,1)S(1)}, u32[]{:S(2)}, u32[]{:S(2)}) collective-permute-start(bf16[384,384]{1,0:T(8,128)(2,1)} %collective-permute-done.5.refs_8_), channel_id=1, source_target_pairs={{0,16},{16,0},{1,17},{17,1},{2,18},{18,2},{3,19},{19,3},{4,20},{20... | collective-permute-start | bytes 884744 | tf_op jit(solution)/shard_map/ppermute | solution.py:208
  36.0 2.0 %shard_map.76 = bf16[256,384]{1,0:T(8,128)(2,1)} custom-call(s32[6]{0:T(128)S(1)} %copy-done.3, s32[24]{0:T(128)S(1)} %shard_map.73.lists_ref, bf16[256,1152]{1,0:T(8,128)(2,1)S(1)} %bitcast.6), custom_call_target="tpu_custom_call" | custom-call | flops 10000000000 | bytes 1000 | tf_op jit(solution)/shard_map/pallas_call | solution.py:236
  38.0 5.3 %all-to-all-start.1 = ((bf16[8,32,384]{2,1,0:T(8,128)(2,1)}), bf16[8,32,384]{2,1,0:T(8,128)(2,1)S(1)}, u32[]{:S(2)}, u32[]{:S(2)}) async-start(bf16[8,32,384]{2,1,0:T(8,128)(2,1)} %bitcast.4), calls=%async_computation.1 | async-start | bytes 393216 | tf_op jit(solution)/shard_map/all_to_all | solution.py:248
  43.3 2.1 %collective-permute-start.10 = (bf16[384,384]{1,0:T(8,128)(2,1)S(1)}, bf16[384,384]{1,0:T(8,128)(2,1)}, u32[]{:S(2)}, u32[]{:S(2)}) collective-permute-start(bf16[384,384]{1,0:T(8,128)(2,1)S(1)} %collective-permute-done.6.refs_10_), channel_id=1, source_target_pairs={{0,2},{2,0},{4,6},{6,4},{8,10},{10,8},{12,14},{14,12},{1,3},{3,1},... | collective-permute-start | bytes 884744 | tf_op jit(solution)/shard_map/ppermute | solution.py:204
  45.9 5.3 %all-to-all-done.1 = bf16[8,32,384]{2,1,0:T(8,128)(2,1)S(1)} async-done(((bf16[8,32,384]{2,1,0:T(8,128)(2,1)}), bf16[8,32,384]{2,1,0:T(8,128)(2,1)S(1)}, u32[]{:S(2)}, u32[]{:S(2)}) %all-to-all-start.1) | async-done | bytes 196640 | tf_op jit(solution)/shard_map/all_to_all | solution.py:248
  53.0 1.4 %collective-permute-start.14 = (bf16[384,384]{1,0:T(8,128)(2,1)}, bf16[384,384]{1,0:T(8,128)(2,1)S(1)}, u32[]{:S(2)}, u32[]{:S(2)}) collective-permute-start(bf16[384,384]{1,0:T(8,128)(2,1)} %collective-permute-done.11.refs_11_), channel_id=1, source_target_pairs={{0,2},{2,0},{4,6},{6,4},{8,10},{10,8},{12,14},{14,12},{1,3},{3,1},... | collective-permute-start | bytes 884744 | tf_op jit(solution)/shard_map/ppermute | solution.py:204
  55.4 2.2 %shard_map.77 = (bf16[128,2304]{1,0:T(8,128)(2,1)S(1)}, bf16[128,2304]{1,0:T(8,128)(2,1)S(1)}) custom-call(s32[6]{0:T(128)S(1)} %copy-done.3, bf16[256,384]{1,0:T(8,128)(2,1)S(1)} %copy-done.7, bf16[256,384]{1,0:T(8,128)(2,1)S(1)} %bitcast.7, bf16[384,384]{1,0:T(8,128)(2,1)S(1)} %get-tuple-element.48.refs_0_, ...), custom_call_target="tpu_custom_call" | custom-call | flops 20000000000 | bytes 1000 | tf_op jit(solution)/shard_map/pallas_call | solution.py:236
  57.7 1.4 %collective-permute-done.13.refs_1_ = bf16[384,384]{1,0:T(8,128)(2,1)S(1)} collective-permute-done((bf16[384,384]{1,0:T(8,128)(2,1)S(1)}, bf16[384,384]{1,0:T(8,128)(2,1)S(1)}, u32[]{:S(2)}, u32[]{:S(2)}) %collective-permute-start.13) | collective-permute-done | bytes 294944 | tf_op jit(solution)/shard_map/ppermute | solution.py:208
  60.0 1.5 %shard_map.78 = (bf16[128,768]{1,0:T(8,128)(2,1)S(1)}, bf16[128,768]{1,0:T(8,128)(2,1)S(1)}) custom-call(s32[6]{0:T(128)S(1)} %copy-done.3, bf16[256,384]{1,0:T(8,128)(2,1)S(1)} %copy-done.7, bf16[256,384]{1,0:T(8,128)(2,1)S(1)} %bitcast.8, bf16[384,384]{1,0:T(8,128)(2,1)S(1)} %collective-permute-done.7.refs_0_, ...), custom_call_target="tpu_custom_call" | custom-call | flops 20000000000 | bytes 1000 | tf_op jit(solution)/shard_map/pallas_call | solution.py:236
  61.6 1.4 %collective-permute-done.15.refs_3_ = bf16[128,768]{1,0:T(8,128)(2,1)S(1)} collective-permute-done((bf16[128,768]{1,0:T(8,128)(2,1)S(1)}, bf16[128,768]{1,0:T(8,128)(2,1)S(1)}, u32[]{:S(2)}, u32[]{:S(2)}) %collective-permute-start.15) | collective-permute-done | bytes 196640 | tf_op jit(solution)/shard_map/ppermute | solution.py:216
  (42 shorter events, 9.5 us)
Async XLA Ops:
  0.0 5.8 %copy-start = (bf16[256,768]{1,0:T(8,128)(2,1)S(1)}, bf16[256,768]{1,0:T(8,128)(2,1)}, u32[]{:S(2)}) copy-start(bf16[256,768]{1,0:T(8,128)(2,1)} %q_ref.3) | copy-start | bytes 1179652
  0.0 5.8 %copy-start.1 = (bf16[256,768]{1,0:T(8,128)(2,1)S(1)}, bf16[256,768]{1,0:T(8,128)(2,1)}, u32[]{:S(2)}) copy-start(bf16[256,768]{1,0:T(8,128)(2,1)} %k_ref.3) | copy-start | bytes 1179652
  0.0 5.8 %copy-start.2 = (bf16[256,768]{1,0:T(8,128)(2,1)S(1)}, bf16[256,768]{1,0:T(8,128)(2,1)}, u32[]{:S(2)}) copy-start(bf16[256,768]{1,0:T(8,128)(2,1)} %v_ref.3) | copy-start | bytes 1179652
  1.2 4.6 %copy-start.3 = (s32[6]{0:T(128)S(1)}, s32[6]{0:T(128)}, u32[]{:S(2)}) copy-start(s32[6]{0:T(128)} %class_ref.9) | copy-start | bytes 76
  1.2 12.1 %collective-permute-start = (bf16[384,384]{1,0:T(8,128)(2,1)S(1)}, bf16[384,384]{1,0:T(8,128)(2,1)S(1)}, u32[]{:S(2)}, u32[]{:S(2)}) collective-permute-start(bf16[384,384]{1,0:T(8,128)(2,1)S(1)} %get-tuple-element.48.refs_0_), channel_id=1, source_target_pairs={{0,4},{2,6},{4,8},{6,10},{8,12},{10,14},{12,0},{14,2},{1,5},{3,7},... | collective-permute-start | bytes 884744 | tf_op jit(solution)/shard_map/ppermute | solution.py:212
  4.3 9.1 %collective-permute-start.1 = (bf16[384,384]{1,0:T(8,128)(2,1)S(1)}, bf16[384,384]{1,0:T(8,128)(2,1)S(1)}, u32[]{:S(2)}, u32[]{:S(2)}) collective-permute-start(bf16[384,384]{1,0:T(8,128)(2,1)S(1)} %get-tuple-element.48.refs_0_), channel_id=1, source_target_pairs={{0,2},{2,0},{4,6},{6,4},{8,10},{10,8},{12,14},{14,12},{1,3},{3,1},... | collective-permute-start | bytes 884744 | tf_op jit(solution)/shard_map/ppermute | solution.py:204
  7.4 4.0 %copy-start.9 = (s32[6,1,4]{0,2,1:T(4,128)S(1)}, s32[6,1,4]{0,2,1:T(4,128)}, u32[]{:S(2)}) copy-start(s32[6,1,4]{0,2,1:T(4,128)} %param.13) | copy-start | bytes 292
  7.4 25.6 %all-to-all-start = ((bf16[8,32,1152]{2,1,0:T(8,128)(2,1)}), bf16[8,32,1152]{2,1,0:T(8,128)(2,1)S(1)}, u32[]{:S(2)}, u32[]{:S(2)}) async-start(bf16[8,32,1152]{2,1,0:T(8,128)(2,1)} %bitcast.2), calls=%async_computation | async-start | bytes 1179648 | tf_op jit(solution)/shard_map/all_to_all | solution.py:248
  13.4 13.5 %collective-permute-start.2 = (bf16[384,384]{1,0:T(8,128)(2,1)S(1)}, bf16[384,384]{1,0:T(8,128)(2,1)S(1)}, u32[]{:S(2)}, u32[]{:S(2)}) collective-permute-start(bf16[384,384]{1,0:T(8,128)(2,1)S(1)} %collective-permute-done.refs_4_), channel_id=1, source_target_pairs={{0,2},{2,0},{4,6},{6,4},{8,10},{10,8},{12,14},{14,12},{1,3},{3,1},... | collective-permute-start | bytes 884744 | tf_op jit(solution)/shard_map/ppermute | solution.py:204
  15.8 11.1 %collective-permute-start.3 = (bf16[384,384]{1,0:T(8,128)(2,1)S(1)}, bf16[384,384]{1,0:T(8,128)(2,1)S(1)}, u32[]{:S(2)}, u32[]{:S(2)}) collective-permute-start(bf16[384,384]{1,0:T(8,128)(2,1)S(1)} %collective-permute-done.refs_4_), channel_id=1, source_target_pairs={{0,16},{16,0},{1,17},{17,1},{2,18},{18,2},{3,19},{19,3},{4,20},{20... | collective-permute-start | bytes 884744 | tf_op jit(solution)/shard_map/ppermute | solution.py:208
  17.3 11.5 %collective-permute-start.4 = (bf16[384,384]{1,0:T(8,128)(2,1)S(1)}, bf16[384,384]{1,0:T(8,128)(2,1)S(1)}, u32[]{:S(2)}, u32[]{:S(2)}) collective-permute-start(bf16[384,384]{1,0:T(8,128)(2,1)S(1)} %collective-permute-done.1.refs_2_), channel_id=1, source_target_pairs={{0,16},{16,0},{1,17},{17,1},{2,18},{18,2},{3,19},{19,3},{4,20},{20... | collective-permute-start | bytes 884744 | tf_op jit(solution)/shard_map/ppermute | solution.py:208
  17.8 13.2 %collective-permute-start.5 = (bf16[384,384]{1,0:T(8,128)(2,1)S(1)}, bf16[384,384]{1,0:T(8,128)(2,1)}, u32[]{:S(2)}, u32[]{:S(2)}) collective-permute-start(bf16[384,384]{1,0:T(8,128)(2,1)S(1)} %collective-permute-done.refs_4_), channel_id=1, source_target_pairs={{0,4},{2,6},{4,8},{6,10},{8,12},{10,14},{12,0},{14,2},{1,5},{3,7},... | collective-permute-start | bytes 884744 | tf_op jit(solution)/shard_map/ppermute | solution.py:212
  29.5 13.7 %collective-permute-start.9 = (bf16[384,384]{1,0:T(8,128)(2,1)S(1)}, bf16[384,384]{1,0:T(8,128)(2,1)S(1)}, u32[]{:S(2)}, u32[]{:S(2)}) collective-permute-start(bf16[384,384]{1,0:T(8,128)(2,1)S(1)} %collective-permute-done.2.refs_6_), channel_id=1, source_target_pairs={{0,16},{16,0},{1,17},{17,1},{2,18},{18,2},{3,19},{19,3},{4,20},{20... | collective-permute-start | bytes 884744 | tf_op jit(solution)/shard_map/ppermute | solution.py:208
  33.1 10.2 %collective-permute-start.6 = (bf16[384,384]{1,0:T(8,128)(2,1)}, bf16[384,384]{1,0:T(8,128)(2,1)S(1)}, u32[]{:S(2)}, u32[]{:S(2)}) collective-permute-start(bf16[384,384]{1,0:T(8,128)(2,1)} %collective-permute-done.5.refs_8_), channel_id=1, source_target_pairs={{0,4},{2,6},{4,8},{6,10},{8,12},{10,14},{12,0},{14,2},{1,5},{3,7},... | collective-permute-start | bytes 884744 | tf_op jit(solution)/shard_map/ppermute | solution.py:212
  33.7 9.6 %collective-permute-start.7 = (bf16[384,384]{1,0:T(8,128)(2,1)}, bf16[384,384]{1,0:T(8,128)(2,1)S(1)}, u32[]{:S(2)}, u32[]{:S(2)}) collective-permute-start(bf16[384,384]{1,0:T(8,128)(2,1)} %collective-permute-done.5.refs_8_), channel_id=1, source_target_pairs={{0,2},{2,0},{4,6},{6,4},{8,10},{10,8},{12,14},{14,12},{1,3},{3,1},... | collective-permute-start | bytes 884744 | tf_op jit(solution)/shard_map/ppermute | solution.py:204
  34.5 8.8 %collective-permute-start.8 = (bf16[384,384]{1,0:T(8,128)(2,1)}, bf16[384,384]{1,0:T(8,128)(2,1)S(1)}, u32[]{:S(2)}, u32[]{:S(2)}) collective-permute-start(bf16[384,384]{1,0:T(8,128)(2,1)} %collective-permute-done.5.refs_8_), channel_id=1, source_target_pairs={{0,16},{16,0},{1,17},{17,1},{2,18},{18,2},{3,19},{19,3},{4,20},{20... | collective-permute-start | bytes 884744 | tf_op jit(solution)/shard_map/ppermute | solution.py:208
  38.0 16.5 %copy-start.5 = (bf16[384,384]{1,0:T(8,128)(2,1)S(1)}, bf16[384,384]{1,0:T(8,128)(2,1)}, u32[]{:S(2)}) copy-start(bf16[384,384]{1,0:T(8,128)(2,1)} %copy-done.4) | copy-start | bytes 884740
  38.0 13.2 %all-to-all-start.1 = ((bf16[8,32,384]{2,1,0:T(8,128)(2,1)}), bf16[8,32,384]{2,1,0:T(8,128)(2,1)S(1)}, u32[]{:S(2)}, u32[]{:S(2)}) async-start(bf16[8,32,384]{2,1,0:T(8,128)(2,1)} %bitcast.4), calls=%async_computation.1 | async-start | bytes 393216 | tf_op jit(solution)/shard_map/all_to_all | solution.py:248
  43.3 9.0 %collective-permute-start.10 = (bf16[384,384]{1,0:T(8,128)(2,1)S(1)}, bf16[384,384]{1,0:T(8,128)(2,1)}, u32[]{:S(2)}, u32[]{:S(2)}) collective-permute-start(bf16[384,384]{1,0:T(8,128)(2,1)S(1)} %collective-permute-done.6.refs_10_), channel_id=1, source_target_pairs={{0,2},{2,0},{4,6},{6,4},{8,10},{10,8},{12,14},{14,12},{1,3},{3,1},... | collective-permute-start | bytes 884744 | tf_op jit(solution)/shard_map/ppermute | solution.py:204
  45.4 7.0 %collective-permute-start.11 = (bf16[384,384]{1,0:T(8,128)(2,1)S(1)}, bf16[384,384]{1,0:T(8,128)(2,1)}, u32[]{:S(2)}, u32[]{:S(2)}) collective-permute-start(bf16[384,384]{1,0:T(8,128)(2,1)S(1)} %collective-permute-done.6.refs_10_), channel_id=1, source_target_pairs={{0,16},{16,0},{1,17},{17,1},{2,18},{18,2},{3,19},{19,3},{4,20},{20... | collective-permute-start | bytes 884744 | tf_op jit(solution)/shard_map/ppermute | solution.py:208
  52.4 6.7 %collective-permute-start.13 = (bf16[384,384]{1,0:T(8,128)(2,1)S(1)}, bf16[384,384]{1,0:T(8,128)(2,1)S(1)}, u32[]{:S(2)}, u32[]{:S(2)}) collective-permute-start(bf16[384,384]{1,0:T(8,128)(2,1)S(1)} %collective-permute-done.7.refs_0_), channel_id=1, source_target_pairs={{0,16},{16,0},{1,17},{17,1},{2,18},{18,2},{3,19},{19,3},{4,20},{20... | collective-permute-start | bytes 884744 | tf_op jit(solution)/shard_map/ppermute | solution.py:208
  53.0 6.9 %collective-permute-start.14 = (bf16[384,384]{1,0:T(8,128)(2,1)}, bf16[384,384]{1,0:T(8,128)(2,1)S(1)}, u32[]{:S(2)}, u32[]{:S(2)}) collective-permute-start(bf16[384,384]{1,0:T(8,128)(2,1)} %collective-permute-done.11.refs_11_), channel_id=1, source_target_pairs={{0,2},{2,0},{4,6},{6,4},{8,10},{10,8},{12,14},{14,12},{1,3},{3,1},... | collective-permute-start | bytes 884744 | tf_op jit(solution)/shard_map/ppermute | solution.py:204
  57.6 5.4 %collective-permute-start.12 = (bf16[128,2304]{1,0:T(8,128)(2,1)S(1)}, bf16[128,2304]{1,0:T(8,128)(2,1)S(1)}, u32[]{:S(2)}, u32[]{:S(2)}) collective-permute-start(bf16[128,2304]{1,0:T(8,128)(2,1)S(1)} %get-tuple-element.42), channel_id=1, source_target_pairs={{0,1},{1,0},{2,3},{3,2},{4,5},{5,4},{6,7},{7,6},{8,9},{9,8},{10,11... | collective-permute-start | bytes 1769480 | tf_op jit(solution)/shard_map/ppermute | solution.py:216
  61.5 1.5 %collective-permute-start.15 = (bf16[128,768]{1,0:T(8,128)(2,1)S(1)}, bf16[128,768]{1,0:T(8,128)(2,1)S(1)}, u32[]{:S(2)}, u32[]{:S(2)}) collective-permute-start(bf16[128,768]{1,0:T(8,128)(2,1)S(1)} %get-tuple-element.46), channel_id=1, source_target_pairs={{0,1},{1,0},{2,3},{3,2},{4,5},{5,4},{6,7},{7,6},{8,9},{9,8},{10,11... | collective-permute-start | bytes 589832 | tf_op jit(solution)/shard_map/ppermute | solution.py:216
  (4 other events, 6.2 us)

commit v4 on v3

--- a/solution.py
+++ b/solution.py
@@ -10,7 +10,8 @@
 VMEM = pl.BlockSpec(memory_space=pltpu.VMEM)
 SMEM = pl.BlockSpec(memory_space=pltpu.SMEM)
 ANY = pl.BlockSpec(memory_space=pl.ANY)
-COSTS = {"pack": 1, "lists": 10000, "spatial": 2000, "temporal": 10000, "join": 10000, "add": 5000, "project": 20000}
+HBM = pl.BlockSpec(memory_space=pltpu.HBM)
+COSTS = {"pack": 5000, "spatial": 10000, "temporal": 5000, "join_first": 1, "join_last": 1, "project_first": 3000, "project_last": 5000, "project_whole": 20000}
 PARAMS = pltpu.CompilerParams(vmem_limit_bytes=16 * 1024 * 1024)
 
 
@@ -54,7 +55,8 @@
         copy.wait()
 
 
-def attend(queries, keys, values, listed, blocks):
+def attend(load, head, lists_ref, counts_ref, blocks):
+    queries, keys, values = (load(place) for place in range(3))
     rows = queries.shape[0] // blocks
     scores = lax.dot_general(
         queries, keys, (((1,), (1,)), ((), ())), preferred_element_type=jnp.float32
@@ -62,7 +64,9 @@
     key_block = lax.broadcasted_iota(jnp.int32, (rows, keys.shape[0]), 1) // rows
     masked = []
     for block in range(blocks):
-        first, second = listed[block]
+        first = lists_ref[head, 2 * block]
+        second = lists_ref[head, 2 * block + 1]
+        second = jnp.where(counts_ref[head, block] > 1, second, first)
         allowed = (key_block == first) | (key_block == second)
         masked.append(
             jnp.where(allowed, scores[block * rows : (block + 1) * rows], -jnp.inf)
@@ -76,24 +80,19 @@
     return (total / denominator).astype(jnp.bfloat16)
 
 
-def lists_kernel(heads, blocks, lists_ref, counts_ref, out_ref):
-    for head in range(heads):
-        for block in range(blocks):
-            first = lists_ref[head, 2 * block]
-            second = jnp.where(counts_ref[head, block] > 1, lists_ref[head, 2 * block + 1], first)
-            out_ref[head * blocks + block] = first * 256 + second
-
-
-def listed_blocks(lists_ref, head, blocks):
-    listed = []
-    for block in range(blocks):
-        both = lists_ref[head * blocks + block]
-        listed.append((both >> 8, both & 255))
-    return listed
-
-
 def spatial_kernel(
-    heads, width, blocks, class_ref, lists_ref, q_ref, k_ref, v_ref, out_ref, held_ref, sems
+    heads,
+    width,
+    blocks,
+    class_ref,
+    lists_ref,
+    counts_ref,
+    q_ref,
+    k_ref,
+    v_ref,
+    out_ref,
+    held_ref,
+    sems,
 ):
     copies = head_copies(
         heads,
@@ -109,26 +108,27 @@
         for copy in copies[3 * rank : 3 * rank + 3]:
             copy.wait()
         out_ref[:, rank * width : (rank + 1) * width] = attend(
-            held_ref[0, rank],
-            held_ref[1, rank],
-            held_ref[2, rank],
-            listed_blocks(lists_ref, head, blocks),
+            lambda place: held_ref[place, rank],
+            head,
+            lists_ref,
+            counts_ref,
             blocks,
         )
 
 
 def temporal_kernel(
-    heads, width, blocks, class_ref, lists_ref, packed_ref, out_ref
+    heads, width, blocks, class_ref, lists_ref, counts_ref, packed_ref, out_ref
 ):
     half = heads // 2
     for rank in range(half):
         head = head_of_rank(class_ref, 1, rank, heads)
-        q, k, v = (
-            packed_ref[:, (place * half + rank) * width : (place * half + rank + 1) * width]
-            for place in range(3)
-        )
+
+        def load(place):
+            at = (place * half + rank) * width
+            return packed_ref[:, at : at + width]
+
         out_ref[:, rank * width : (rank + 1) * width] = attend(
-            q, k, v, listed_blocks(lists_ref, head, blocks), blocks
+            load, head, lists_ref, counts_ref, blocks
         )
 
 
@@ -145,29 +145,37 @@
                 ]
 
 
-def project_pieces_kernel(heads, width, count, class_ref, spatial_ref, temporal_ref, *refs):
-    pieces, (peer_ref, mine_ref, att_ref) = refs[: 2 * count], refs[2 * count :]
-    place_heads(heads, width, class_ref, spatial_ref, temporal_ref, att_ref)
-    depth, cols = pieces[0].shape
-    rows = peer_ref.shape[0]
-    half = lax.axis_index("groups")
-    attended = jnp.concatenate(
-        [att_ref[:, columns(half, depth)], att_ref[:, columns(1 - half, depth)]], axis=1
-    )
-    for index in range(0, count, 2):
-        shards = range(index, min(index + 2, count))
+def project_pieces(attended, pieces, peer_ref, mine_ref):
+    rows, cols = peer_ref.shape[0], pieces[0].shape[1]
+    for index in range(0, len(pieces), 4):
         weight = jnp.concatenate(
             [
-                jnp.concatenate([pieces[2 * at][...], pieces[2 * at + 1][...]], axis=0)
-                for at in shards
+                jnp.concatenate([piece[...] for piece in pieces[at : at + 2]], axis=0)
+                for at in range(index, index + 4, 2)
             ],
             axis=1,
         )
         total = jnp.dot(attended, weight, preferred_element_type=jnp.float32)
         total = total.astype(peer_ref.dtype)
-        take = slice(index * cols, (index + len(shards)) * cols)
+        take = slice(index // 2 * cols, (index // 2 + 2) * cols)
         peer_ref[:, take] = total[:rows]
         mine_ref[:, take] = total[rows:]
+
+
+def project_first_kernel(heads, width, class_ref, spatial_ref, temporal_ref, *refs):
+    pieces, (peer_ref, mine_ref, attended_ref, att_ref) = refs[:-4], refs[-4:]
+    place_heads(heads, width, class_ref, spatial_ref, temporal_ref, att_ref)
+    depth = pieces[0].shape[0]
+    half = lax.axis_index("groups")
+    halves = (columns(half, depth), columns(1 - half, depth))
+    for at, side in enumerate(halves):
+        attended_ref[:, at * depth : (at + 1) * depth] = att_ref[:, side]
+    project_pieces(attended_ref[...], pieces, peer_ref, mine_ref)
+
+
+def project_last_kernel(attended_ref, *refs):
+    pieces, (peer_ref, mine_ref) = refs[:-2], refs[-2:]
+    project_pieces(attended_ref[...], pieces, peer_ref, mine_ref)
 
 
 def project_whole_kernel(
@@ -183,21 +191,33 @@
         ).astype(out_ref.dtype)
 
 
-def join_kernel(shards, *refs):
-    parts, out_ref = refs[:-1], refs[-1]
+def join_shards(shards, mine_ref, received_ref, out_ref, held_ref, sems):
     index = lax.axis_index("frame")
-    line, pair = index // 2, index % 2
-    cols = out_ref.shape[1] // 8
-    order = iter(shards)
-    for mine_ref, received_ref in zip(parts[0::2], parts[1::2]):
-        for at in range(mine_ref.shape[1] // cols):
-            step, crossed = next(order)
-            source = lax.rem(line - step + 4, 4) * 2 + (1 - pair if crossed else pair)
-            take = slice(at * cols, (at + 1) * cols)
-            total = mine_ref[:, take].astype(jnp.float32) + received_ref[:, take].astype(
-                jnp.float32
+    line, pair = index // 2, lax.rem(index, 2)
+    cols = mine_ref.shape[1] // len(shards)
+    copies = []
+    for at, (step, crossed) in enumerate(shards):
+        source = lax.rem(line - step + 4, 4) * 2 + (1 - pair if crossed else pair)
+        take = slice(at * cols, (at + 1) * cols)
+        held_ref[:, take] = (
+            mine_ref[:, take].astype(jnp.float32) + received_ref[:, take].astype(jnp.float32)
+        ).astype(out_ref.dtype)
+        copies.append(
+            pltpu.make_async_copy(
+                held_ref.at[:, take], out_ref.at[:, columns(source, cols)], sems.at[at]
             )
-            out_ref[:, columns(source, cols)] = total.astype(out_ref.dtype)
+        )
+        copies[-1].start()
+    for copy in copies:
+        copy.wait()
+
+
+def join_first_kernel(shards, *refs):
+    join_shards(shards, *refs)
+
+
+def join_last_kernel(shards, mine_ref, received_ref, joined_ref, *refs):
+    join_shards(shards, mine_ref, received_ref, *refs)
 
 
 def swap_pair(piece):
@@ -232,12 +252,13 @@
     groups = lax.axis_size("groups")
     model = out_weight.shape[1] * frames
     bf16 = functools.partial(jax.ShapeDtypeStruct, dtype=jnp.bfloat16)
-    def call(kernel, ins, outs, *operands, scratch=(), out_spec=VMEM):
+    def call(kernel, ins, outs, *operands, scratch=(), out_spec=VMEM, aliases={}):
         return pl.pallas_call(
             kernel,
             out_shape=outs,
             in_specs=ins,
             out_specs=jax.tree.map(lambda _: out_spec, outs),
+            input_output_aliases=aliases,
             scratch_shapes=scratch,
             compiler_params=PARAMS,
             cost_estimate=pl.CostEstimate(flops=next(v for k, v in COSTS.items() if k in str(kernel)) * 10**6, bytes_accessed=1000, transcendentals=0),
@@ -249,14 +270,7 @@
             split, "frame", split_axis=0, concat_axis=0, tiled=True
         ).reshape(rows.shape)
 
-    lists = call(
-        functools.partial(lists_kernel, heads, blocks),
-        [SMEM, SMEM],
-        jax.ShapeDtypeStruct((heads * blocks,), jnp.int32),
-        block_lists.reshape(heads, -1),
-        block_counts.reshape(heads, -1),
-        out_spec=SMEM,
-    )
+    lists = (block_lists.reshape(heads, -1), block_counts.reshape(heads, -1))
     packed = call(
         functools.partial(pack_kernel, heads, width),
         [SMEM, ANY, ANY, ANY],
@@ -271,10 +285,10 @@
     def spatial_heads():
         return call(
             functools.partial(spatial_kernel, heads, width, blocks),
-            [SMEM, SMEM, ANY, ANY, ANY],
+            [SMEM, SMEM, SMEM, ANY, ANY, ANY],
             bf16((pixels, half * width)),
             head_class,
-            lists,
+            *lists,
             head_queries,
             head_keys,
             head_values,
@@ -287,10 +301,10 @@
     def temporal_heads(arrived):
         return call(
             functools.partial(temporal_kernel, heads, width, blocks),
-            [SMEM, SMEM, VMEM],
+            [SMEM, SMEM, SMEM, VMEM],
             bf16((pixels, half * width)),
             head_class,
-            lists,
+            *lists,
             arrived,
         )
 
@@ -317,26 +331,29 @@
     own = lax.dynamic_slice_in_dim(out_weight, group * depth, depth, 0)
     rest = lax.dynamic_slice_in_dim(out_weight, (1 - group) * depth, depth, 0)
 
-    def project(pieces):
-        count = len(pieces) // 2
+    def join(kernel, shards, mine, received, joined=None):
         return call(
-            functools.partial(project_pieces_kernel, heads, width, count),
-            [SMEM] + [VMEM] * (2 + len(pieces)),
-            [bf16((pixels // 2, count * cols))] * 2,
-            head_class,
-            spatial,
-            returned,
-            *pieces,
-            scratch=att_scratch,
+            functools.partial(kernel, shards),
+            [VMEM, VMEM] + ([] if joined is None else [HBM]),
+            bf16((pixels // 2, model)),
+            mine,
+            received,
+            *([] if joined is None else [joined]),
+            scratch=[
+                pltpu.VMEM(mine.shape, jnp.bfloat16),
+                pltpu.SemaphoreType.DMA((len(shards),)),
+            ],
+            out_spec=HBM,
+            aliases={} if joined is None else {2: 0},
         )
 
     arrived = exchange(packed)
-    held_1, pair_0, lists = tied(next_line(own), swap_pair(own), lists)
+    held_1, pair_0 = tied(next_line(own), swap_pair(own))
     pair_1, rest_1, pair_rest_0, spatial = tied(
         swap_pair(held_1), swap_group(held_1), swap_group(pair_0), spatial_heads()
     )
     pair_rest_1 = swap_group(pair_1)
-    held_2, arrived = tied(next_line(held_1), arrived)
+    held_2 = next_line(held_1)
     returned = exchange(temporal_heads(arrived))
     held_3, pair_2, rest_2, pair_rest_1 = tied(
         next_line(held_2), swap_pair(held_2), swap_group(held_2), pair_rest_1
@@ -345,23 +362,34 @@
         swap_pair(held_3), swap_group(held_3), returned, pair_2
     )
     pair_rest_2, pair_rest_3 = swap_group(pair_2), swap_pair(rest_3)
-    peer, mine = project(
-        [own, rest, pair_0, pair_rest_0, held_1, rest_1, pair_1, pair_rest_1, held_2, rest_2]
-        + [held_3, rest_3]
+    pieces = [own, rest, pair_0, pair_rest_0, held_1, rest_1, pair_1, pair_rest_1]
+    pieces += [held_2, rest_2, held_3, rest_3]
+    peer, mine, attended = call(
+        functools.partial(project_first_kernel, heads, width),
+        [SMEM] + [VMEM] * (2 + len(pieces)),
+        [bf16((pixels // 2, 6 * cols))] * 2 + [bf16((pixels, heads * width))],
+        head_class,
+        spatial,
+        returned,
+        *pieces,
+        scratch=att_scratch,
     )
     received = swap_side(peer)
-    last_peer, last_mine = project([pair_2, pair_rest_2, pair_3, pair_rest_3])
+    last_peer, last_mine = call(
+        project_last_kernel,
+        [VMEM] * 5,
+        [bf16((pixels // 2, 2 * cols))] * 2,
+        attended,
+        pair_2,
+        pair_rest_2,
+        pair_3,
+        pair_rest_3,
+    )
     last_received = swap_side(last_peer)
-    order = ((0, 0), (0, 1), (1, 0), (1, 1), (2, 0), (3, 0), (2, 1), (3, 1))
-    return call(
-        functools.partial(join_kernel, order),
-        [VMEM] * 4,
-        bf16((pixels // 2, model)),
-        mine,
-        received,
-        last_mine,
-        last_received,
-    )
+    joined = join(
+        join_first_kernel, ((0, 0), (0, 1), (1, 0), (1, 1), (2, 0), (3, 0)), mine, received
+    )
+    return join(join_last_kernel, ((2, 1), (3, 1)), last_mine, last_received, joined)
 
 
 def solution(mesh):

time: 64.5 us -> 62.9 us (0.975)
  starting transfers between devices: 29.7 us -> 25.6 us
  waiting for transfers between devices: 18.7 us -> 22 us
  Pallas kernels: 11.8 us -> 10.3 us
  local copies, waits for them, and re-layouts: 3.73 us -> 4.46 us
    ppermute x6, waiting for transfers between devices: 3.3 us -> 14.7 us  [swap_group(): return lax.ppermute(piece, 'groups', [(0, 1), (1, 0)])]
    all_to_all x2, waiting for transfers between devices: 7.25 us -> 0.01 us  [exchange(): lax.all_to_all(split, 'frame', split_axis=0, concat_axis=0, tiled=True)]
    ppermute x3, starting transfers between devices: 5.91 us -> 2.89 us  [next_line(): return lax.ppermute(piece, 'frame', [(i, (i + 2) % 8) for i in range(8)])]
    ppermute x3, waiting for transfers between devices: 0.56 us -> 3.51 us  [next_line(): return lax.ppermute(piece, 'frame', [(i, (i + 2) % 8) for i in range(8)])]
    ppermute x5, waiting for transfers between devices: 6.2 us -> 3.33 us  [swap_pair(): return lax.ppermute(piece, 'frame', [(i, i ^ 1) for i in range(8)])]
    ppermute x5, starting transfers between devices: 8.23 us -> 6.01 us  [swap_pair(): return lax.ppermute(piece, 'frame', [(i, i ^ 1) for i in range(8)])]
    ppermute x6, starting transfers between devices: 6.26 us -> 8.15 us  [swap_group(): return lax.ppermute(piece, 'groups', [(0, 1), (1, 0)])]
    pallas_call x7, Pallas kernels: 11.8 us -> 10.3 us  [call(): pl.pallas_call(kernel, out_shape=outs, in_specs=ins, out_specs=jax.tree.m...]
  transfers between devices with their start and end apart: 18 -> 18, of which waited for: 9 -> 9; matrix products, arithmetic and copies ran while one was open for 0% -> 0% of each run, Pallas kernels for 17% -> 15%
where the time goes in v4:
time: 62.9 us; the launch traced here: 62.5 us
  starting transfers between devices  25.6 us (41%)
  waiting for transfers between devices  22 us (35%)
  Pallas kernels  10.3 us (16%)
  local copies, waits for them, and re-layouts  4.46 us (7%)
    ppermute x6, waiting for transfers between devices, swap_group(): return lax.ppermute(piece, 'groups', [(0, 1), (1, 0)])  14.7 us
    pallas_call x7, Pallas kernels, call(): pl.pallas_call(kernel, out_shape=outs, in_specs=ins, out_specs=jax.tree.m...  10.3 us
    all_to_all x2, starting transfers between devices, exchange(): lax.all_to_all(split, 'frame', split_axis=0, concat_axis=0, tiled=True)  8.44 us
    ppermute x6, starting transfers between devices, swap_group(): return lax.ppermute(piece, 'groups', [(0, 1), (1, 0)])  8.15 us
    ppermute x5, starting transfers between devices, swap_pair(): return lax.ppermute(piece, 'frame', [(i, i ^ 1) for i in range(8)])  6.01 us
    ppermute x3, waiting for transfers between devices, next_line(): return lax.ppermute(piece, 'frame', [(i, (i + 2) % 8) for i in range(8)])  3.51 us
    ppermute x5, waiting for transfers between devices, swap_pair(): return lax.ppermute(piece, 'frame', [(i, i ^ 1) for i in range(8)])  3.33 us
    unnamed x24, local copies, waits for them, and re-layouts  3.08 us
  transfers between devices with their start and end apart: 18, of which 9 were waited for; matrix products, arithmetic and copies ran while one was open for 0% of the time, Pallas kernels for 15%

profile of v4, /device:TPU:0, one launch (start us, length us, event | category | flops | bytes accessed | tf_op | source)
XLA Modules:
  0.0 62.5 jit_solution(18137392639435388385)
XLA Ops:
  0.0 1.2 %constant_dynamic-slice_fusion = (bf16[384,384]{1,0:T(8,128)(2,1)S(1)}, bf16[384,384]{1,0:T(8,128)(2,1)S(1)}) fusion(bf16[768,384]{1,0:T(8,128)(2,1)} %param.10, s32[]{:T(128)S(6)} %select_n.7, s32[]{:T(128)S(6)} %select_n.6), kind=kLoop, calls=%fused_computation | loop fusion | bytes 1179656 | tf_op jit(solution)/shard_map/dynamic_slice | solution.py:332
  1.2 3.0 %collective-permute-start.1 = (bf16[384,384]{1,0:T(8,128)(2,1)S(1)}, bf16[384,384]{1,0:T(8,128)(2,1)S(1)}, u32[]{:S(2)}, u32[]{:S(2)}) collective-permute-start(bf16[384,384]{1,0:T(8,128)(2,1)S(1)} %get-tuple-element.44.refs_0_), channel_id=1, source_target_pairs={{0,2},{2,0},{4,6},{6,4},{8,10},{10,8},{12,14},{14,12},{1,3},{3,1},... | collective-permute-start | bytes 884744 | tf_op jit(solution)/shard_map/ppermute | solution.py:224
  4.2 1.6 %collective-permute-start = (bf16[384,384]{1,0:T(8,128)(2,1)S(1)}, bf16[384,384]{1,0:T(8,128)(2,1)S(1)}, u32[]{:S(2)}, u32[]{:S(2)}) collective-permute-start(bf16[384,384]{1,0:T(8,128)(2,1)S(1)} %get-tuple-element.44.refs_0_), channel_id=1, source_target_pairs={{0,4},{2,6},{4,8},{6,10},{8,12},{10,14},{12,0},{14,2},{1,5},{3,7},... | collective-permute-start | bytes 884744 | tf_op jit(solution)/shard_map/ppermute | solution.py:232
  5.8 1.6 %shard_map.74 = bf16[256,1152]{1,0:T(8,128)(2,1)} custom-call(s32[6]{0:T(128)S(1)} %copy-done.7, bf16[256,768]{1,0:T(8,128)(2,1)S(1)} %copy-done, bf16[256,768]{1,0:T(8,128)(2,1)S(1)} %copy-done.1, bf16[256,768]{1,0:T(8,128)(2,1)S(1)} %copy-done.2), custom_call_target="tpu_custom_call" | custom-call | flops 5000000000 | bytes 1000 | tf_op jit(solution)/shard_map/pallas_call | solution.py:256
  7.4 3.9 %all-to-all-start = ((bf16[8,32,1152]{2,1,0:T(8,128)(2,1)}), bf16[8,32,1152]{2,1,0:T(8,128)(2,1)S(1)}, u32[]{:S(2)}, u32[]{:S(2)}) async-start(bf16[8,32,1152]{2,1,0:T(8,128)(2,1)} %bitcast.2), calls=%async_computation | async-start | bytes 1179648 | tf_op jit(solution)/shard_map/all_to_all | solution.py:269
  11.5 3.2 %collective-permute-done.refs_4_ = bf16[384,384]{1,0:T(8,128)(2,1)S(1)} collective-permute-done((bf16[384,384]{1,0:T(8,128)(2,1)S(1)}, bf16[384,384]{1,0:T(8,128)(2,1)S(1)}, u32[]{:S(2)}, u32[]{:S(2)}) %collective-permute-start) | collective-permute-done | bytes 294944 | tf_op jit(solution)/shard_map/ppermute | solution.py:232
  15.1 1.5 %collective-permute-start.3 = (bf16[384,384]{1,0:T(8,128)(2,1)S(1)}, bf16[384,384]{1,0:T(8,128)(2,1)S(1)}, u32[]{:S(2)}, u32[]{:S(2)}) collective-permute-start(bf16[384,384]{1,0:T(8,128)(2,1)S(1)} %collective-permute-done.refs_4_), channel_id=1, source_target_pairs={{0,16},{16,0},{1,17},{17,1},{2,18},{18,2},{3,19},{19,3},{4,20},{20... | collective-permute-start | bytes 884744 | tf_op jit(solution)/shard_map/ppermute | solution.py:228
  17.2 2.2 %shard_map.73.spatial_ref = bf16[256,384]{1,0:T(8,128)(2,1)S(1)} custom-call(s32[6]{0:T(128)S(1)} %copy-done.7, s32[6,8]{1,0:T(8,128)S(1)} %copy.9.lists_ref, s32[6,4]{1,0:T(8,128)S(1)} %copy.10.counts_ref, bf16[256,768]{1,0:T(8,128)(2,1)S(1)} %copy-done, bf16[256,768]{1,0:T(8,128)(2,1)S(1)} %copy-done.1, bf16[256,768]{1,0:T(8,128)(2,1)S(1)} %copy-done.2), custom_call_target="tpu_custom_call" | custom-call | flops 10000000000 | bytes 1000 | tf_op jit(solution)/shard_map/pallas_call | solution.py:256
  20.1 8.5 %collective-permute-done.4.refs_3_ = bf16[384,384]{1,0:T(8,128)(2,1)S(1)} collective-permute-done((bf16[384,384]{1,0:T(8,128)(2,1)S(1)}, bf16[384,384]{1,0:T(8,128)(2,1)S(1)}, u32[]{:S(2)}, u32[]{:S(2)}) %collective-permute-start.4) | collective-permute-done | bytes 294944 | tf_op jit(solution)/shard_map/ppermute | solution.py:228
  29.2 1.5 %collective-permute-start.9 = (bf16[384,384]{1,0:T(8,128)(2,1)}, bf16[384,384]{1,0:T(8,128)(2,1)S(1)}, u32[]{:S(2)}, u32[]{:S(2)}) collective-permute-start(bf16[384,384]{1,0:T(8,128)(2,1)} %collective-permute-done.2.refs_6_), channel_id=1, source_target_pairs={{0,16},{16,0},{1,17},{17,1},{2,18},{18,2},{3,19},{19,3},{4,20},{20... | collective-permute-start | bytes 884744 | tf_op jit(solution)/shard_map/ppermute | solution.py:228
  30.8 1.5 %collective-permute-start.8 = (bf16[384,384]{1,0:T(8,128)(2,1)S(1)}, bf16[384,384]{1,0:T(8,128)(2,1)S(1)}, u32[]{:S(2)}, u32[]{:S(2)}) collective-permute-start(bf16[384,384]{1,0:T(8,128)(2,1)S(1)} %collective-permute-done.5.refs_8_), channel_id=1, source_target_pairs={{0,16},{16,0},{1,17},{17,1},{2,18},{18,2},{3,19},{19,3},{4,20},{20... | collective-permute-start | bytes 884744 | tf_op jit(solution)/shard_map/ppermute | solution.py:228
  32.3 1.5 %collective-permute-start.7 = (bf16[384,384]{1,0:T(8,128)(2,1)S(1)}, bf16[384,384]{1,0:T(8,128)(2,1)S(1)}, u32[]{:S(2)}, u32[]{:S(2)}) collective-permute-start(bf16[384,384]{1,0:T(8,128)(2,1)S(1)} %collective-permute-done.5.refs_8_), channel_id=1, source_target_pairs={{0,2},{2,0},{4,6},{6,4},{8,10},{10,8},{12,14},{14,12},{1,3},{3,1},... | collective-permute-start | bytes 884744 | tf_op jit(solution)/shard_map/ppermute | solution.py:224
  34.7 2.1 %shard_map.75 = bf16[256,384]{1,0:T(8,128)(2,1)} custom-call(s32[6]{0:T(128)S(1)} %copy-done.7, s32[6,8]{1,0:T(8,128)S(1)} %copy.9.lists_ref, s32[6,4]{1,0:T(8,128)S(1)} %copy.10.counts_ref, bf16[256,1152]{1,0:T(8,128)(2,1)S(1)} %bitcast.6), custom_call_target="tpu_custom_call" | custom-call | flops 5000000000 | bytes 1000 | tf_op jit(solution)/shard_map/pallas_call | solution.py:256
  36.8 4.6 %all-to-all-start.1 = ((bf16[8,32,384]{2,1,0:T(8,128)(2,1)}), bf16[8,32,384]{2,1,0:T(8,128)(2,1)S(1)}, u32[]{:S(2)}, u32[]{:S(2)}) async-start(bf16[8,32,384]{2,1,0:T(8,128)(2,1)} %bitcast.4), calls=%async_computation.1 | async-start | bytes 393216 | tf_op jit(solution)/shard_map/all_to_all | solution.py:269
  42.4 1.9 %collective-permute-start.11 = (bf16[384,384]{1,0:T(8,128)(2,1)S(1)}, bf16[384,384]{1,0:T(8,128)(2,1)}, u32[]{:S(2)}, u32[]{:S(2)}) collective-permute-start(bf16[384,384]{1,0:T(8,128)(2,1)S(1)} %collective-permute-done.6.refs_10_), channel_id=1, source_target_pairs={{0,16},{16,0},{1,17},{17,1},{2,18},{18,2},{3,19},{19,3},{4,20},{20... | collective-permute-start | bytes 884744 | tf_op jit(solution)/shard_map/ppermute | solution.py:228
  44.6 4.6 %collective-permute-done.11.refs_11_ = bf16[384,384]{1,0:T(8,128)(2,1)} collective-permute-done((bf16[384,384]{1,0:T(8,128)(2,1)S(1)}, bf16[384,384]{1,0:T(8,128)(2,1)}, u32[]{:S(2)}, u32[]{:S(2)}) %collective-permute-start.11) | collective-permute-done | bytes 294944 | tf_op jit(solution)/shard_map/ppermute | solution.py:228
  49.2 2.0 %collective-permute-done.10.refs_2_ = bf16[384,384]{1,0:T(8,128)(2,1)S(1)} collective-permute-done((bf16[384,384]{1,0:T(8,128)(2,1)S(1)}, bf16[384,384]{1,0:T(8,128)(2,1)S(1)}, u32[]{:S(2)}, u32[]{:S(2)}) %collective-permute-start.10) | collective-permute-done | bytes 294944 | tf_op jit(solution)/shard_map/ppermute | solution.py:224
  52.0 1.1 %collective-permute-start.13 = (bf16[384,384]{1,0:T(8,128)(2,1)}, bf16[384,384]{1,0:T(8,128)(2,1)S(1)}, u32[]{:S(2)}, u32[]{:S(2)}) collective-permute-start(bf16[384,384]{1,0:T(8,128)(2,1)} %collective-permute-done.11.refs_11_), channel_id=1, source_target_pairs={{0,2},{2,0},{4,6},{6,4},{8,10},{10,8},{12,14},{14,12},{1,3},{3,1},... | collective-permute-start | bytes 884744 | tf_op jit(solution)/shard_map/ppermute | solution.py:224
  53.1 1.2 %collective-permute-start.12 = (bf16[384,384]{1,0:T(8,128)(2,1)S(1)}, bf16[384,384]{1,0:T(8,128)(2,1)S(1)}, u32[]{:S(2)}, u32[]{:S(2)}) collective-permute-start(bf16[384,384]{1,0:T(8,128)(2,1)S(1)} %collective-permute-done.7.refs_0_), channel_id=1, source_target_pairs={{0,16},{16,0},{1,17},{17,1},{2,18},{18,2},{3,19},{19,3},{4,20},{20... | collective-permute-start | bytes 884744 | tf_op jit(solution)/shard_map/ppermute | solution.py:228
  54.3 0.9 %copy-done.9 = bf16[256,384]{1,0:T(8,128)(2,1)S(1)} copy-done((bf16[256,384]{1,0:T(8,128)(2,1)S(1)}, bf16[256,384]{1,0:T(8,128)(2,1)}, u32[]{:S(2)}) %copy-start.9) | copy-done | bytes 196632
  55.2 2.3 %shard_map.76 = (bf16[128,2304]{1,0:T(8,128)(2,1)S(1)}, bf16[128,2304]{1,0:T(8,128)(2,1)S(1)}, bf16[256,768]{1,0:T(8,128)(2,1)S(1)}) custom-call(s32[6]{0:T(128)S(1)} %copy-done.7, bf16[256,384]{1,0:T(8,128)(2,1)S(1)} %copy-done.9, bf16[256,384]{1,0:T(8,128)(2,1)S(1)} %bitcast.7, bf16[384,384]{1,0:T(8,128)(2,1)S(1)} %get-tuple-element.44.refs_0_, ...), custom_call_target="tpu_custom_call" | custom-call | flops 3000000000 | bytes 1000 | tf_op jit(solution)/shard_map/pallas_call | solution.py:256
  57.6 1.3 %collective-permute-done.13.refs_3_ = bf16[384,384]{1,0:T(8,128)(2,1)S(1)} collective-permute-done((bf16[384,384]{1,0:T(8,128)(2,1)}, bf16[384,384]{1,0:T(8,128)(2,1)S(1)}, u32[]{:S(2)}, u32[]{:S(2)}) %collective-permute-start.13) | collective-permute-done | bytes 294944 | tf_op jit(solution)/shard_map/ppermute | solution.py:224
  58.9 0.9 %collective-permute-done.12.refs_1_ = bf16[384,384]{1,0:T(8,128)(2,1)S(1)} collective-permute-done((bf16[384,384]{1,0:T(8,128)(2,1)S(1)}, bf16[384,384]{1,0:T(8,128)(2,1)S(1)}, u32[]{:S(2)}, u32[]{:S(2)}) %collective-permute-start.12) | collective-permute-done | bytes 294944 | tf_op jit(solution)/shard_map/ppermute | solution.py:228
  60.4 0.9 %shard_map.78.joined_ref = bf16[128,3072]{1,0:T(8,128)(2,1)} custom-call(bf16[128,2304]{1,0:T(8,128)(2,1)S(1)} %get-tuple-element.41.refs_0_, bf16[128,2304]{1,0:T(8,128)(2,1)S(1)} %collective-permute-done.15.refs_1_), custom_call_target="tpu_custom_call" | custom-call | flops 1000000 | bytes 1000 | tf_op jit(solution)/shard_map/pallas_call | solution.py:256
  (46 shorter events, 7.4 us)
Async XLA Ops:
  0.0 5.8 %copy-start = (bf16[256,768]{1,0:T(8,128)(2,1)S(1)}, bf16[256,768]{1,0:T(8,128)(2,1)}, u32[]{:S(2)}) copy-start(bf16[256,768]{1,0:T(8,128)(2,1)} %q_ref.3) | copy-start | bytes 1179652
  0.0 5.8 %copy-start.1 = (bf16[256,768]{1,0:T(8,128)(2,1)S(1)}, bf16[256,768]{1,0:T(8,128)(2,1)}, u32[]{:S(2)}) copy-start(bf16[256,768]{1,0:T(8,128)(2,1)} %k_ref.3) | copy-start | bytes 1179652
  0.0 5.8 %copy-start.2 = (bf16[256,768]{1,0:T(8,128)(2,1)S(1)}, bf16[256,768]{1,0:T(8,128)(2,1)}, u32[]{:S(2)}) copy-start(bf16[256,768]{1,0:T(8,128)(2,1)} %v_ref.3) | copy-start | bytes 1179652
  1.2 4.6 %copy-start.7 = (s32[6]{0:T(128)S(1)}, s32[6]{0:T(128)}, u32[]{:S(2)}) copy-start(s32[6]{0:T(128)} %class_ref.7) | copy-start | bytes 76
  1.2 10.3 %collective-permute-start.1 = (bf16[384,384]{1,0:T(8,128)(2,1)S(1)}, bf16[384,384]{1,0:T(8,128)(2,1)S(1)}, u32[]{:S(2)}, u32[]{:S(2)}) collective-permute-start(bf16[384,384]{1,0:T(8,128)(2,1)S(1)} %get-tuple-element.44.refs_0_), channel_id=1, source_target_pairs={{0,2},{2,0},{4,6},{6,4},{8,10},{10,8},{12,14},{14,12},{1,3},{3,1},... | collective-permute-start | bytes 884744 | tf_op jit(solution)/shard_map/ppermute | solution.py:224
  4.2 10.4 %collective-permute-start = (bf16[384,384]{1,0:T(8,128)(2,1)S(1)}, bf16[384,384]{1,0:T(8,128)(2,1)S(1)}, u32[]{:S(2)}, u32[]{:S(2)}) collective-permute-start(bf16[384,384]{1,0:T(8,128)(2,1)S(1)} %get-tuple-element.44.refs_0_), channel_id=1, source_target_pairs={{0,4},{2,6},{4,8},{6,10},{8,12},{10,14},{12,0},{14,2},{1,5},{3,7},... | collective-permute-start | bytes 884744 | tf_op jit(solution)/shard_map/ppermute | solution.py:232
  7.4 27.2 %all-to-all-start = ((bf16[8,32,1152]{2,1,0:T(8,128)(2,1)}), bf16[8,32,1152]{2,1,0:T(8,128)(2,1)S(1)}, u32[]{:S(2)}, u32[]{:S(2)}) async-start(bf16[8,32,1152]{2,1,0:T(8,128)(2,1)} %bitcast.2), calls=%async_computation | async-start | bytes 1179648 | tf_op jit(solution)/shard_map/all_to_all | solution.py:269
  14.7 16.1 %collective-permute-start.5 = (bf16[384,384]{1,0:T(8,128)(2,1)S(1)}, bf16[384,384]{1,0:T(8,128)(2,1)S(1)}, u32[]{:S(2)}, u32[]{:S(2)}) collective-permute-start(bf16[384,384]{1,0:T(8,128)(2,1)S(1)} %collective-permute-done.refs_4_), channel_id=1, source_target_pairs={{0,4},{2,6},{4,8},{6,10},{8,12},{10,14},{12,0},{14,2},{1,5},{3,7},... | collective-permute-start | bytes 884744 | tf_op jit(solution)/shard_map/ppermute | solution.py:232
  15.1 14.1 %collective-permute-start.3 = (bf16[384,384]{1,0:T(8,128)(2,1)S(1)}, bf16[384,384]{1,0:T(8,128)(2,1)S(1)}, u32[]{:S(2)}, u32[]{:S(2)}) collective-permute-start(bf16[384,384]{1,0:T(8,128)(2,1)S(1)} %collective-permute-done.refs_4_), channel_id=1, source_target_pairs={{0,16},{16,0},{1,17},{17,1},{2,18},{18,2},{3,19},{19,3},{4,20},{20... | collective-permute-start | bytes 884744 | tf_op jit(solution)/shard_map/ppermute | solution.py:228
  16.6 12.6 %collective-permute-start.2 = (bf16[384,384]{1,0:T(8,128)(2,1)S(1)}, bf16[384,384]{1,0:T(8,128)(2,1)}, u32[]{:S(2)}, u32[]{:S(2)}) collective-permute-start(bf16[384,384]{1,0:T(8,128)(2,1)S(1)} %collective-permute-done.refs_4_), channel_id=1, source_target_pairs={{0,2},{2,0},{4,6},{6,4},{8,10},{10,8},{12,14},{14,12},{1,3},{3,1},... | collective-permute-start | bytes 884744 | tf_op jit(solution)/shard_map/ppermute | solution.py:224
  16.7 11.8 %collective-permute-start.4 = (bf16[384,384]{1,0:T(8,128)(2,1)S(1)}, bf16[384,384]{1,0:T(8,128)(2,1)S(1)}, u32[]{:S(2)}, u32[]{:S(2)}) collective-permute-start(bf16[384,384]{1,0:T(8,128)(2,1)S(1)} %collective-permute-done.1.refs_2_), channel_id=1, source_target_pairs={{0,16},{16,0},{1,17},{17,1},{2,18},{18,2},{3,19},{19,3},{4,20},{20... | collective-permute-start | bytes 884744 | tf_op jit(solution)/shard_map/ppermute | solution.py:228
  29.2 13.1 %collective-permute-start.9 = (bf16[384,384]{1,0:T(8,128)(2,1)}, bf16[384,384]{1,0:T(8,128)(2,1)S(1)}, u32[]{:S(2)}, u32[]{:S(2)}) collective-permute-start(bf16[384,384]{1,0:T(8,128)(2,1)} %collective-permute-done.2.refs_6_), channel_id=1, source_target_pairs={{0,16},{16,0},{1,17},{17,1},{2,18},{18,2},{3,19},{19,3},{4,20},{20... | collective-permute-start | bytes 884744 | tf_op jit(solution)/shard_map/ppermute | solution.py:228
  30.8 11.2 %collective-permute-start.8 = (bf16[384,384]{1,0:T(8,128)(2,1)S(1)}, bf16[384,384]{1,0:T(8,128)(2,1)S(1)}, u32[]{:S(2)}, u32[]{:S(2)}) collective-permute-start(bf16[384,384]{1,0:T(8,128)(2,1)S(1)} %collective-permute-done.5.refs_8_), channel_id=1, source_target_pairs={{0,16},{16,0},{1,17},{17,1},{2,18},{18,2},{3,19},{19,3},{4,20},{20... | collective-permute-start | bytes 884744 | tf_op jit(solution)/shard_map/ppermute | solution.py:228
  32.3 9.7 %collective-permute-start.7 = (bf16[384,384]{1,0:T(8,128)(2,1)S(1)}, bf16[384,384]{1,0:T(8,128)(2,1)S(1)}, u32[]{:S(2)}, u32[]{:S(2)}) collective-permute-start(bf16[384,384]{1,0:T(8,128)(2,1)S(1)} %collective-permute-done.5.refs_8_), channel_id=1, source_target_pairs={{0,2},{2,0},{4,6},{6,4},{8,10},{10,8},{12,14},{14,12},{1,3},{3,1},... | collective-permute-start | bytes 884744 | tf_op jit(solution)/shard_map/ppermute | solution.py:224
  33.8 8.5 %collective-permute-start.6 = (bf16[384,384]{1,0:T(8,128)(2,1)S(1)}, bf16[384,384]{1,0:T(8,128)(2,1)S(1)}, u32[]{:S(2)}, u32[]{:S(2)}) collective-permute-start(bf16[384,384]{1,0:T(8,128)(2,1)S(1)} %collective-permute-done.5.refs_8_), channel_id=1, source_target_pairs={{0,4},{2,6},{4,8},{6,10},{8,12},{10,14},{12,0},{14,2},{1,5},{3,7},... | collective-permute-start | bytes 884744 | tf_op jit(solution)/shard_map/ppermute | solution.py:232
  36.8 17.5 %copy-start.4 = (bf16[384,384]{1,0:T(8,128)(2,1)S(1)}, bf16[384,384]{1,0:T(8,128)(2,1)}, u32[]{:S(2)}) copy-start(bf16[384,384]{1,0:T(8,128)(2,1)} %copy-done.3) | copy-start | bytes 884740
  36.8 15.1 %all-to-all-start.1 = ((bf16[8,32,384]{2,1,0:T(8,128)(2,1)}), bf16[8,32,384]{2,1,0:T(8,128)(2,1)S(1)}, u32[]{:S(2)}, u32[]{:S(2)}) async-start(bf16[8,32,384]{2,1,0:T(8,128)(2,1)} %bitcast.4), calls=%async_computation.1 | async-start | bytes 393216 | tf_op jit(solution)/shard_map/all_to_all | solution.py:269
  42.4 6.8 %collective-permute-start.11 = (bf16[384,384]{1,0:T(8,128)(2,1)S(1)}, bf16[384,384]{1,0:T(8,128)(2,1)}, u32[]{:S(2)}, u32[]{:S(2)}) collective-permute-start(bf16[384,384]{1,0:T(8,128)(2,1)S(1)} %collective-permute-done.6.refs_10_), channel_id=1, source_target_pairs={{0,16},{16,0},{1,17},{17,1},{2,18},{18,2},{3,19},{19,3},{4,20},{20... | collective-permute-start | bytes 884744 | tf_op jit(solution)/shard_map/ppermute | solution.py:228
  44.2 7.0 %collective-permute-start.10 = (bf16[384,384]{1,0:T(8,128)(2,1)S(1)}, bf16[384,384]{1,0:T(8,128)(2,1)S(1)}, u32[]{:S(2)}, u32[]{:S(2)}) collective-permute-start(bf16[384,384]{1,0:T(8,128)(2,1)S(1)} %collective-permute-done.6.refs_10_), channel_id=1, source_target_pairs={{0,2},{2,0},{4,6},{6,4},{8,10},{10,8},{12,14},{14,12},{1,3},{3,1},... | collective-permute-start | bytes 884744 | tf_op jit(solution)/shard_map/ppermute | solution.py:224
  52.0 6.9 %collective-permute-start.13 = (bf16[384,384]{1,0:T(8,128)(2,1)}, bf16[384,384]{1,0:T(8,128)(2,1)S(1)}, u32[]{:S(2)}, u32[]{:S(2)}) collective-permute-start(bf16[384,384]{1,0:T(8,128)(2,1)} %collective-permute-done.11.refs_11_), channel_id=1, source_target_pairs={{0,2},{2,0},{4,6},{6,4},{8,10},{10,8},{12,14},{14,12},{1,3},{3,1},... | collective-permute-start | bytes 884744 | tf_op jit(solution)/shard_map/ppermute | solution.py:224
  53.1 6.7 %collective-permute-start.12 = (bf16[384,384]{1,0:T(8,128)(2,1)S(1)}, bf16[384,384]{1,0:T(8,128)(2,1)S(1)}, u32[]{:S(2)}, u32[]{:S(2)}) collective-permute-start(bf16[384,384]{1,0:T(8,128)(2,1)S(1)} %collective-permute-done.7.refs_0_), channel_id=1, source_target_pairs={{0,16},{16,0},{1,17},{17,1},{2,18},{18,2},{3,19},{19,3},{4,20},{20... | collective-permute-start | bytes 884744 | tf_op jit(solution)/shard_map/ppermute | solution.py:228
  55.2 4.6 %copy-start.6 = (bf16[384,384]{1,0:T(8,128)(2,1)S(1)}, bf16[384,384]{1,0:T(8,128)(2,1)}, u32[]{:S(2)}) copy-start(bf16[384,384]{1,0:T(8,128)(2,1)} %copy-done.5) | copy-start | bytes 884740
  57.5 2.9 %collective-permute-start.15 = (bf16[128,2304]{1,0:T(8,128)(2,1)S(1)}, bf16[128,2304]{1,0:T(8,128)(2,1)S(1)}, u32[]{:S(2)}, u32[]{:S(2)}) collective-permute-start(bf16[128,2304]{1,0:T(8,128)(2,1)S(1)} %get-tuple-element.42), channel_id=1, source_target_pairs={{0,1},{1,0},{2,3},{3,2},{4,5},{5,4},{6,7},{7,6},{8,9},{9,8},{10,11... | collective-permute-start | bytes 1769480 | tf_op jit(solution)/shard_map/ppermute | solution.py:236
  60.3 1.5 %collective-permute-start.14 = (bf16[128,768]{1,0:T(8,128)(2,1)S(1)}, bf16[128,768]{1,0:T(8,128)(2,1)S(1)}, u32[]{:S(2)}, u32[]{:S(2)}) collective-permute-start(bf16[128,768]{1,0:T(8,128)(2,1)S(1)} %get-tuple-element.40), channel_id=1, source_target_pairs={{0,1},{1,0},{2,3},{3,2},{4,5},{5,4},{6,7},{7,6},{8,9},{9,8},{10,11... | collective-permute-start | bytes 589832 | tf_op jit(solution)/shard_map/ppermute | solution.py:236
  (6 other events, 10.9 us)

commit v5 on v4

--- a/solution.py
+++ b/solution.py
@@ -11,7 +11,6 @@
 SMEM = pl.BlockSpec(memory_space=pltpu.SMEM)
 ANY = pl.BlockSpec(memory_space=pl.ANY)
 HBM = pl.BlockSpec(memory_space=pltpu.HBM)
-COSTS = {"pack": 5000, "spatial": 10000, "temporal": 5000, "join_first": 1, "join_last": 1, "project_first": 3000, "project_last": 5000, "project_whole": 20000}
 PARAMS = pltpu.CompilerParams(vmem_limit_bytes=16 * 1024 * 1024)
 
 
@@ -252,7 +251,7 @@
     groups = lax.axis_size("groups")
     model = out_weight.shape[1] * frames
     bf16 = functools.partial(jax.ShapeDtypeStruct, dtype=jnp.bfloat16)
-    def call(kernel, ins, outs, *operands, scratch=(), out_spec=VMEM, aliases={}):
+    def call(work, kernel, ins, outs, *operands, scratch=(), out_spec=VMEM, aliases={}):
         return pl.pallas_call(
             kernel,
             out_shape=outs,
@@ -261,7 +260,7 @@
             input_output_aliases=aliases,
             scratch_shapes=scratch,
             compiler_params=PARAMS,
-            cost_estimate=pl.CostEstimate(flops=next(v for k, v in COSTS.items() if k in str(kernel)) * 10**6, bytes_accessed=1000, transcendentals=0),
+            cost_estimate=pl.CostEstimate(flops=work * 10**6, bytes_accessed=1000, transcendentals=0),
         )(*operands)
 
     def exchange(rows):
@@ -272,6 +271,7 @@
 
     lists = (block_lists.reshape(heads, -1), block_counts.reshape(heads, -1))
     packed = call(
+        5000,
         functools.partial(pack_kernel, heads, width),
         [SMEM, ANY, ANY, ANY],
         bf16((pixels, 3 * half * width)),
@@ -284,6 +284,7 @@
 
     def spatial_heads():
         return call(
+            10000,
             functools.partial(spatial_kernel, heads, width, blocks),
             [SMEM, SMEM, SMEM, ANY, ANY, ANY],
             bf16((pixels, half * width)),
@@ -300,6 +301,7 @@
 
     def temporal_heads(arrived):
         return call(
+            5000,
             functools.partial(temporal_kernel, heads, width, blocks),
             [SMEM, SMEM, SMEM, VMEM],
             bf16((pixels, half * width)),
@@ -314,6 +316,7 @@
         returned = exchange(temporal_heads(exchange(packed)))
         weight = lax.all_gather(out_weight, "frame", axis=1, tiled=True)
         peer, mine = call(
+            20000,
             functools.partial(project_whole_kernel, heads, width),
             [SMEM, VMEM, VMEM, VMEM],
             [bf16((pixels // 2, model))] * 2,
@@ -333,6 +336,7 @@
 
     def join(kernel, shards, mine, received, joined=None):
         return call(
+            1,
             functools.partial(kernel, shards),
             [VMEM, VMEM] + ([] if joined is None else [HBM]),
             bf16((pixels // 2, model)),
@@ -348,7 +352,7 @@
         )
 
     arrived = exchange(packed)
-    held_1, pair_0 = tied(next_line(own), swap_pair(own))
+    pair_0, held_1 = tied(swap_pair(own), next_line(own))
     pair_1, rest_1, pair_rest_0, spatial = tied(
         swap_pair(held_1), swap_group(held_1), swap_group(pair_0), spatial_heads()
     )
@@ -365,6 +369,7 @@
     pieces = [own, rest, pair_0, pair_rest_0, held_1, rest_1, pair_1, pair_rest_1]
     pieces += [held_2, rest_2, held_3, rest_3]
     peer, mine, attended = call(
+        3000,
         functools.partial(project_first_kernel, heads, width),
         [SMEM] + [VMEM] * (2 + len(pieces)),
         [bf16((pixels // 2, 6 * cols))] * 2 + [bf16((pixels, heads * width))],
@@ -376,6 +381,7 @@
     )
     received = swap_side(peer)
     last_peer, last_mine = call(
+        5000,
         project_last_kernel,
         [VMEM] * 5,
         [bf16((pixels // 2, 2 * cols))] * 2,

time: 62.9 us -> 63.1 us (level)
  starting transfers between devices: 25.6 us -> 29.8 us
  waiting for transfers between devices: 22 us -> 17.8 us
    ppermute x3, starting transfers between devices: 2.89 us -> 6.29 us  [next_line(): return lax.ppermute(piece, 'frame', [(i, (i + 2) % 8) for i in range(8)])]
    ppermute x6, waiting for transfers between devices: 14.7 us -> 11.4 us  [swap_group(): return lax.ppermute(piece, 'groups', [(0, 1), (1, 0)])]
    ppermute x5, starting transfers between devices: 6.01 us -> 8.17 us  [swap_pair(): return lax.ppermute(piece, 'frame', [(i, i ^ 1) for i in range(8)])]
    ppermute x5, waiting for transfers between devices: 3.33 us -> 2.22 us  [swap_pair(): return lax.ppermute(piece, 'frame', [(i, i ^ 1) for i in range(8)])]
    ppermute x6, starting transfers between devices: 8.15 us -> 7.24 us  [swap_group(): return lax.ppermute(piece, 'groups', [(0, 1), (1, 0)])]
where the time goes in v5:
time: 63.1 us; the launch traced here: 62.4 us
  starting transfers between devices  29.8 us (47%)
  waiting for transfers between devices  17.8 us (28%)
  Pallas kernels  10.3 us (16%)
  local copies, waits for them, and re-layouts  4.46 us (7%)
    ppermute x6, waiting for transfers between devices, swap_group(): return lax.ppermute(piece, 'groups', [(0, 1), (1, 0)])  11.4 us
    pallas_call x7, Pallas kernels, call(): pl.pallas_call(kernel, out_shape=outs, in_specs=ins, out_specs=jax.tree.m...  10.3 us
    ppermute x5, starting transfers between devices, swap_pair(): return lax.ppermute(piece, 'frame', [(i, i ^ 1) for i in range(8)])  8.17 us
    all_to_all x2, starting transfers between devices, exchange(): lax.all_to_all(split, 'frame', split_axis=0, concat_axis=0, tiled=True)  7.94 us
    ppermute x6, starting transfers between devices, swap_group(): return lax.ppermute(piece, 'groups', [(0, 1), (1, 0)])  7.24 us
    ppermute x3, starting transfers between devices, next_line(): return lax.ppermute(piece, 'frame', [(i, (i + 2) % 8) for i in range(8)])  6.29 us
    ppermute x3, waiting for transfers between devices, next_line(): return lax.ppermute(piece, 'frame', [(i, (i + 2) % 8) for i in range(8)])  3.61 us
    unnamed x24, local copies, waits for them, and re-layouts  3.08 us
  transfers between devices with their start and end apart: 18, of which 9 were waited for; matrix products, arithmetic and copies ran while one was open for 0% of the time, Pallas kernels for 15%

profile of v5, /device:TPU:0, one launch (start us, length us, event | category | flops | bytes accessed | tf_op | source)
XLA Modules:
  0.0 62.4 jit_solution(14188798022613834290)
XLA Ops:
  0.0 1.2 %constant_dynamic-slice_fusion = (bf16[384,384]{1,0:T(8,128)(2,1)S(1)}, bf16[384,384]{1,0:T(8,128)(2,1)S(1)}) fusion(bf16[768,384]{1,0:T(8,128)(2,1)} %param.10, s32[]{:T(128)S(6)} %select_n.7, s32[]{:T(128)S(6)} %select_n.6), kind=kLoop, calls=%fused_computation | loop fusion | bytes 1179656 | tf_op jit(solution)/shard_map/dynamic_slice | solution.py:335
  1.2 3.1 %collective-permute-start.1 = (bf16[384,384]{1,0:T(8,128)(2,1)S(1)}, bf16[384,384]{1,0:T(8,128)(2,1)S(1)}, u32[]{:S(2)}, u32[]{:S(2)}) collective-permute-start(bf16[384,384]{1,0:T(8,128)(2,1)S(1)} %get-tuple-element.44.refs_0_), channel_id=1, source_target_pairs={{0,4},{2,6},{4,8},{6,10},{8,12},{10,14},{12,0},{14,2},{1,5},{3,7},... | collective-permute-start | bytes 884744 | tf_op jit(solution)/shard_map/ppermute | solution.py:231
  4.3 1.5 %collective-permute-start = (bf16[384,384]{1,0:T(8,128)(2,1)S(1)}, bf16[384,384]{1,0:T(8,128)(2,1)S(1)}, u32[]{:S(2)}, u32[]{:S(2)}) collective-permute-start(bf16[384,384]{1,0:T(8,128)(2,1)S(1)} %get-tuple-element.44.refs_0_), channel_id=1, source_target_pairs={{0,2},{2,0},{4,6},{6,4},{8,10},{10,8},{12,14},{14,12},{1,3},{3,1},... | collective-permute-start | bytes 884744 | tf_op jit(solution)/shard_map/ppermute | solution.py:223
  5.8 1.6 %shard_map.74 = bf16[256,1152]{1,0:T(8,128)(2,1)} custom-call(s32[6]{0:T(128)S(1)} %copy-done.7, bf16[256,768]{1,0:T(8,128)(2,1)S(1)} %copy-done, bf16[256,768]{1,0:T(8,128)(2,1)S(1)} %copy-done.1, bf16[256,768]{1,0:T(8,128)(2,1)S(1)} %copy-done.2), custom_call_target="tpu_custom_call" | custom-call | flops 5000000000 | bytes 1000 | tf_op jit(solution)/shard_map/pallas_call | solution.py:255
  7.4 3.9 %all-to-all-start = ((bf16[8,32,1152]{2,1,0:T(8,128)(2,1)}), bf16[8,32,1152]{2,1,0:T(8,128)(2,1)S(1)}, u32[]{:S(2)}, u32[]{:S(2)}) async-start(bf16[8,32,1152]{2,1,0:T(8,128)(2,1)} %bitcast.2), calls=%async_computation | async-start | bytes 1179648 | tf_op jit(solution)/shard_map/all_to_all | solution.py:268
  11.5 1.9 %collective-permute-done.1.refs_4_ = bf16[384,384]{1,0:T(8,128)(2,1)S(1)} collective-permute-done((bf16[384,384]{1,0:T(8,128)(2,1)S(1)}, bf16[384,384]{1,0:T(8,128)(2,1)S(1)}, u32[]{:S(2)}, u32[]{:S(2)}) %collective-permute-start.1) | collective-permute-done | bytes 294944 | tf_op jit(solution)/shard_map/ppermute | solution.py:231
  13.4 2.0 %collective-permute-start.5 = (bf16[384,384]{1,0:T(8,128)(2,1)S(1)}, bf16[384,384]{1,0:T(8,128)(2,1)S(1)}, u32[]{:S(2)}, u32[]{:S(2)}) collective-permute-start(bf16[384,384]{1,0:T(8,128)(2,1)S(1)} %collective-permute-done.1.refs_4_), channel_id=1, source_target_pairs={{0,4},{2,6},{4,8},{6,10},{8,12},{10,14},{12,0},{14,2},{1,5},{3,7},... | collective-permute-start | bytes 884744 | tf_op jit(solution)/shard_map/ppermute | solution.py:231
  15.4 1.5 %collective-permute-start.3 = (bf16[384,384]{1,0:T(8,128)(2,1)S(1)}, bf16[384,384]{1,0:T(8,128)(2,1)S(1)}, u32[]{:S(2)}, u32[]{:S(2)}) collective-permute-start(bf16[384,384]{1,0:T(8,128)(2,1)S(1)} %collective-permute-done.1.refs_4_), channel_id=1, source_target_pairs={{0,16},{16,0},{1,17},{17,1},{2,18},{18,2},{3,19},{19,3},{4,20},{20... | collective-permute-start | bytes 884744 | tf_op jit(solution)/shard_map/ppermute | solution.py:227
  16.9 2.6 %collective-permute-start.2 = (bf16[384,384]{1,0:T(8,128)(2,1)S(1)}, bf16[384,384]{1,0:T(8,128)(2,1)}, u32[]{:S(2)}, u32[]{:S(2)}) collective-permute-start(bf16[384,384]{1,0:T(8,128)(2,1)S(1)} %collective-permute-done.1.refs_4_), channel_id=1, source_target_pairs={{0,2},{2,0},{4,6},{6,4},{8,10},{10,8},{12,14},{14,12},{1,3},{3,1},... | collective-permute-start | bytes 884744 | tf_op jit(solution)/shard_map/ppermute | solution.py:223
  20.0 2.2 %shard_map.73.spatial_ref = bf16[256,384]{1,0:T(8,128)(2,1)S(1)} custom-call(s32[6]{0:T(128)S(1)} %copy-done.7, s32[6,8]{1,0:T(8,128)S(1)} %copy.9.lists_ref, s32[6,4]{1,0:T(8,128)S(1)} %copy.10.counts_ref, bf16[256,768]{1,0:T(8,128)(2,1)S(1)} %copy-done, bf16[256,768]{1,0:T(8,128)(2,1)S(1)} %copy-done.1, bf16[256,768]{1,0:T(8,128)(2,1)S(1)} %copy-done.2), custom_call_target="tpu_custom_call" | custom-call | flops 10000000000 | bytes 1000 | tf_op jit(solution)/shard_map/pallas_call | solution.py:255
  22.9 5.0 %collective-permute-done.4.refs_3_ = bf16[384,384]{1,0:T(8,128)(2,1)S(1)} collective-permute-done((bf16[384,384]{1,0:T(8,128)(2,1)S(1)}, bf16[384,384]{1,0:T(8,128)(2,1)S(1)}, u32[]{:S(2)}, u32[]{:S(2)}) %collective-permute-start.4) | collective-permute-done | bytes 294944 | tf_op jit(solution)/shard_map/ppermute | solution.py:227
  28.7 1.5 %collective-permute-start.9 = (bf16[384,384]{1,0:T(8,128)(2,1)}, bf16[384,384]{1,0:T(8,128)(2,1)S(1)}, u32[]{:S(2)}, u32[]{:S(2)}) collective-permute-start(bf16[384,384]{1,0:T(8,128)(2,1)} %collective-permute-done.2.refs_6_), channel_id=1, source_target_pairs={{0,16},{16,0},{1,17},{17,1},{2,18},{18,2},{3,19},{19,3},{4,20},{20... | collective-permute-start | bytes 884744 | tf_op jit(solution)/shard_map/ppermute | solution.py:227
  30.8 1.5 %collective-permute-start.8 = (bf16[384,384]{1,0:T(8,128)(2,1)S(1)}, bf16[384,384]{1,0:T(8,128)(2,1)S(1)}, u32[]{:S(2)}, u32[]{:S(2)}) collective-permute-start(bf16[384,384]{1,0:T(8,128)(2,1)S(1)} %collective-permute-done.5.refs_8_), channel_id=1, source_target_pairs={{0,16},{16,0},{1,17},{17,1},{2,18},{18,2},{3,19},{19,3},{4,20},{20... | collective-permute-start | bytes 884744 | tf_op jit(solution)/shard_map/ppermute | solution.py:227
  32.3 1.5 %collective-permute-start.7 = (bf16[384,384]{1,0:T(8,128)(2,1)S(1)}, bf16[384,384]{1,0:T(8,128)(2,1)S(1)}, u32[]{:S(2)}, u32[]{:S(2)}) collective-permute-start(bf16[384,384]{1,0:T(8,128)(2,1)S(1)} %collective-permute-done.5.refs_8_), channel_id=1, source_target_pairs={{0,2},{2,0},{4,6},{6,4},{8,10},{10,8},{12,14},{14,12},{1,3},{3,1},... | collective-permute-start | bytes 884744 | tf_op jit(solution)/shard_map/ppermute | solution.py:223
  33.8 1.2 %collective-permute-start.6 = (bf16[384,384]{1,0:T(8,128)(2,1)S(1)}, bf16[384,384]{1,0:T(8,128)(2,1)S(1)}, u32[]{:S(2)}, u32[]{:S(2)}) collective-permute-start(bf16[384,384]{1,0:T(8,128)(2,1)S(1)} %collective-permute-done.5.refs_8_), channel_id=1, source_target_pairs={{0,4},{2,6},{4,8},{6,10},{8,12},{10,14},{12,0},{14,2},{1,5},{3,7},... | collective-permute-start | bytes 884744 | tf_op jit(solution)/shard_map/ppermute | solution.py:231
  35.0 2.1 %shard_map.75 = bf16[256,384]{1,0:T(8,128)(2,1)} custom-call(s32[6]{0:T(128)S(1)} %copy-done.7, s32[6,8]{1,0:T(8,128)S(1)} %copy.9.lists_ref, s32[6,4]{1,0:T(8,128)S(1)} %copy.10.counts_ref, bf16[256,1152]{1,0:T(8,128)(2,1)S(1)} %bitcast.6), custom_call_target="tpu_custom_call" | custom-call | flops 5000000000 | bytes 1000 | tf_op jit(solution)/shard_map/pallas_call | solution.py:255
  37.1 4.1 %all-to-all-start.1 = ((bf16[8,32,384]{2,1,0:T(8,128)(2,1)}), bf16[8,32,384]{2,1,0:T(8,128)(2,1)S(1)}, u32[]{:S(2)}, u32[]{:S(2)}) async-start(bf16[8,32,384]{2,1,0:T(8,128)(2,1)} %bitcast.4), calls=%async_computation.1 | async-start | bytes 393216 | tf_op jit(solution)/shard_map/all_to_all | solution.py:268
  41.2 1.1 %collective-permute-done.6.refs_10_ = bf16[384,384]{1,0:T(8,128)(2,1)S(1)} collective-permute-done((bf16[384,384]{1,0:T(8,128)(2,1)S(1)}, bf16[384,384]{1,0:T(8,128)(2,1)S(1)}, u32[]{:S(2)}, u32[]{:S(2)}) %collective-permute-start.6) | collective-permute-done | bytes 294944 | tf_op jit(solution)/shard_map/ppermute | solution.py:231
  44.2 5.0 %collective-permute-done.11.refs_11_ = bf16[384,384]{1,0:T(8,128)(2,1)} collective-permute-done((bf16[384,384]{1,0:T(8,128)(2,1)S(1)}, bf16[384,384]{1,0:T(8,128)(2,1)}, u32[]{:S(2)}, u32[]{:S(2)}) %collective-permute-start.11) | collective-permute-done | bytes 294944 | tf_op jit(solution)/shard_map/ppermute | solution.py:227
  49.2 1.4 %collective-permute-done.10.refs_2_ = bf16[384,384]{1,0:T(8,128)(2,1)S(1)} collective-permute-done((bf16[384,384]{1,0:T(8,128)(2,1)S(1)}, bf16[384,384]{1,0:T(8,128)(2,1)S(1)}, u32[]{:S(2)}, u32[]{:S(2)}) %collective-permute-start.10) | collective-permute-done | bytes 294944 | tf_op jit(solution)/shard_map/ppermute | solution.py:223
  51.3 1.6 %collective-permute-start.13 = (bf16[384,384]{1,0:T(8,128)(2,1)}, bf16[384,384]{1,0:T(8,128)(2,1)S(1)}, u32[]{:S(2)}, u32[]{:S(2)}) collective-permute-start(bf16[384,384]{1,0:T(8,128)(2,1)} %collective-permute-done.11.refs_11_), channel_id=1, source_target_pairs={{0,2},{2,0},{4,6},{6,4},{8,10},{10,8},{12,14},{14,12},{1,3},{3,1},... | collective-permute-start | bytes 884744 | tf_op jit(solution)/shard_map/ppermute | solution.py:223
  52.9 1.3 %collective-permute-start.12 = (bf16[384,384]{1,0:T(8,128)(2,1)S(1)}, bf16[384,384]{1,0:T(8,128)(2,1)S(1)}, u32[]{:S(2)}, u32[]{:S(2)}) collective-permute-start(bf16[384,384]{1,0:T(8,128)(2,1)S(1)} %collective-permute-done.7.refs_0_), channel_id=1, source_target_pairs={{0,16},{16,0},{1,17},{17,1},{2,18},{18,2},{3,19},{19,3},{4,20},{20... | collective-permute-start | bytes 884744 | tf_op jit(solution)/shard_map/ppermute | solution.py:227
  55.1 2.3 %shard_map.76 = (bf16[128,2304]{1,0:T(8,128)(2,1)S(1)}, bf16[128,2304]{1,0:T(8,128)(2,1)S(1)}, bf16[256,768]{1,0:T(8,128)(2,1)S(1)}) custom-call(s32[6]{0:T(128)S(1)} %copy-done.7, bf16[256,384]{1,0:T(8,128)(2,1)S(1)} %copy-done.9, bf16[256,384]{1,0:T(8,128)(2,1)S(1)} %bitcast.7, bf16[384,384]{1,0:T(8,128)(2,1)S(1)} %get-tuple-element.44.refs_0_, ...), custom_call_target="tpu_custom_call" | custom-call | flops 3000000000 | bytes 1000 | tf_op jit(solution)/shard_map/pallas_call | solution.py:255
  58.3 1.4 %collective-permute-done.12.refs_1_ = bf16[384,384]{1,0:T(8,128)(2,1)S(1)} collective-permute-done((bf16[384,384]{1,0:T(8,128)(2,1)S(1)}, bf16[384,384]{1,0:T(8,128)(2,1)S(1)}, u32[]{:S(2)}, u32[]{:S(2)}) %collective-permute-start.12) | collective-permute-done | bytes 294944 | tf_op jit(solution)/shard_map/ppermute | solution.py:227
  (46 shorter events, 9.8 us)
Async XLA Ops:
  0.0 5.8 %copy-start = (bf16[256,768]{1,0:T(8,128)(2,1)S(1)}, bf16[256,768]{1,0:T(8,128)(2,1)}, u32[]{:S(2)}) copy-start(bf16[256,768]{1,0:T(8,128)(2,1)} %q_ref.3) | copy-start | bytes 1179652
  0.0 5.8 %copy-start.1 = (bf16[256,768]{1,0:T(8,128)(2,1)S(1)}, bf16[256,768]{1,0:T(8,128)(2,1)}, u32[]{:S(2)}) copy-start(bf16[256,768]{1,0:T(8,128)(2,1)} %k_ref.3) | copy-start | bytes 1179652
  0.0 5.8 %copy-start.2 = (bf16[256,768]{1,0:T(8,128)(2,1)S(1)}, bf16[256,768]{1,0:T(8,128)(2,1)}, u32[]{:S(2)}) copy-start(bf16[256,768]{1,0:T(8,128)(2,1)} %v_ref.3) | copy-start | bytes 1179652
  1.2 4.6 %copy-start.7 = (s32[6]{0:T(128)S(1)}, s32[6]{0:T(128)}, u32[]{:S(2)}) copy-start(s32[6]{0:T(128)} %class_ref.7) | copy-start | bytes 76
  1.2 12.1 %collective-permute-start.1 = (bf16[384,384]{1,0:T(8,128)(2,1)S(1)}, bf16[384,384]{1,0:T(8,128)(2,1)S(1)}, u32[]{:S(2)}, u32[]{:S(2)}) collective-permute-start(bf16[384,384]{1,0:T(8,128)(2,1)S(1)} %get-tuple-element.44.refs_0_), channel_id=1, source_target_pairs={{0,4},{2,6},{4,8},{6,10},{8,12},{10,14},{12,0},{14,2},{1,5},{3,7},... | collective-permute-start | bytes 884744 | tf_op jit(solution)/shard_map/ppermute | solution.py:231
  4.3 9.1 %collective-permute-start = (bf16[384,384]{1,0:T(8,128)(2,1)S(1)}, bf16[384,384]{1,0:T(8,128)(2,1)S(1)}, u32[]{:S(2)}, u32[]{:S(2)}) collective-permute-start(bf16[384,384]{1,0:T(8,128)(2,1)S(1)} %get-tuple-element.44.refs_0_), channel_id=1, source_target_pairs={{0,2},{2,0},{4,6},{6,4},{8,10},{10,8},{12,14},{14,12},{1,3},{3,1},... | collective-permute-start | bytes 884744 | tf_op jit(solution)/shard_map/ppermute | solution.py:223
  7.4 27.6 %all-to-all-start = ((bf16[8,32,1152]{2,1,0:T(8,128)(2,1)}), bf16[8,32,1152]{2,1,0:T(8,128)(2,1)S(1)}, u32[]{:S(2)}, u32[]{:S(2)}) async-start(bf16[8,32,1152]{2,1,0:T(8,128)(2,1)} %bitcast.2), calls=%async_computation | async-start | bytes 1179648 | tf_op jit(solution)/shard_map/all_to_all | solution.py:268
  13.4 17.4 %collective-permute-start.5 = (bf16[384,384]{1,0:T(8,128)(2,1)S(1)}, bf16[384,384]{1,0:T(8,128)(2,1)S(1)}, u32[]{:S(2)}, u32[]{:S(2)}) collective-permute-start(bf16[384,384]{1,0:T(8,128)(2,1)S(1)} %collective-permute-done.1.refs_4_), channel_id=1, source_target_pairs={{0,4},{2,6},{4,8},{6,10},{8,12},{10,14},{12,0},{14,2},{1,5},{3,7},... | collective-permute-start | bytes 884744 | tf_op jit(solution)/shard_map/ppermute | solution.py:231
  15.4 13.3 %collective-permute-start.3 = (bf16[384,384]{1,0:T(8,128)(2,1)S(1)}, bf16[384,384]{1,0:T(8,128)(2,1)S(1)}, u32[]{:S(2)}, u32[]{:S(2)}) collective-permute-start(bf16[384,384]{1,0:T(8,128)(2,1)S(1)} %collective-permute-done.1.refs_4_), channel_id=1, source_target_pairs={{0,16},{16,0},{1,17},{17,1},{2,18},{18,2},{3,19},{19,3},{4,20},{20... | collective-permute-start | bytes 884744 | tf_op jit(solution)/shard_map/ppermute | solution.py:227
  16.9 11.8 %collective-permute-start.2 = (bf16[384,384]{1,0:T(8,128)(2,1)S(1)}, bf16[384,384]{1,0:T(8,128)(2,1)}, u32[]{:S(2)}, u32[]{:S(2)}) collective-permute-start(bf16[384,384]{1,0:T(8,128)(2,1)S(1)} %collective-permute-done.1.refs_4_), channel_id=1, source_target_pairs={{0,2},{2,0},{4,6},{6,4},{8,10},{10,8},{12,14},{14,12},{1,3},{3,1},... | collective-permute-start | bytes 884744 | tf_op jit(solution)/shard_map/ppermute | solution.py:223
  19.5 8.4 %collective-permute-start.4 = (bf16[384,384]{1,0:T(8,128)(2,1)S(1)}, bf16[384,384]{1,0:T(8,128)(2,1)S(1)}, u32[]{:S(2)}, u32[]{:S(2)}) collective-permute-start(bf16[384,384]{1,0:T(8,128)(2,1)S(1)} %collective-permute-done.refs_2_), channel_id=1, source_target_pairs={{0,16},{16,0},{1,17},{17,1},{2,18},{18,2},{3,19},{19,3},{4,20},{20... | collective-permute-start | bytes 884744 | tf_op jit(solution)/shard_map/ppermute | solution.py:227
  28.7 13.7 %collective-permute-start.9 = (bf16[384,384]{1,0:T(8,128)(2,1)}, bf16[384,384]{1,0:T(8,128)(2,1)S(1)}, u32[]{:S(2)}, u32[]{:S(2)}) collective-permute-start(bf16[384,384]{1,0:T(8,128)(2,1)} %collective-permute-done.2.refs_6_), channel_id=1, source_target_pairs={{0,16},{16,0},{1,17},{17,1},{2,18},{18,2},{3,19},{19,3},{4,20},{20... | collective-permute-start | bytes 884744 | tf_op jit(solution)/shard_map/ppermute | solution.py:227
  30.8 10.4 %collective-permute-start.8 = (bf16[384,384]{1,0:T(8,128)(2,1)S(1)}, bf16[384,384]{1,0:T(8,128)(2,1)S(1)}, u32[]{:S(2)}, u32[]{:S(2)}) collective-permute-start(bf16[384,384]{1,0:T(8,128)(2,1)S(1)} %collective-permute-done.5.refs_8_), channel_id=1, source_target_pairs={{0,16},{16,0},{1,17},{17,1},{2,18},{18,2},{3,19},{19,3},{4,20},{20... | collective-permute-start | bytes 884744 | tf_op jit(solution)/shard_map/ppermute | solution.py:227
  32.3 8.9 %collective-permute-start.7 = (bf16[384,384]{1,0:T(8,128)(2,1)S(1)}, bf16[384,384]{1,0:T(8,128)(2,1)S(1)}, u32[]{:S(2)}, u32[]{:S(2)}) collective-permute-start(bf16[384,384]{1,0:T(8,128)(2,1)S(1)} %collective-permute-done.5.refs_8_), channel_id=1, source_target_pairs={{0,2},{2,0},{4,6},{6,4},{8,10},{10,8},{12,14},{14,12},{1,3},{3,1},... | collective-permute-start | bytes 884744 | tf_op jit(solution)/shard_map/ppermute | solution.py:223
  33.8 8.5 %collective-permute-start.6 = (bf16[384,384]{1,0:T(8,128)(2,1)S(1)}, bf16[384,384]{1,0:T(8,128)(2,1)S(1)}, u32[]{:S(2)}, u32[]{:S(2)}) collective-permute-start(bf16[384,384]{1,0:T(8,128)(2,1)S(1)} %collective-permute-done.5.refs_8_), channel_id=1, source_target_pairs={{0,4},{2,6},{4,8},{6,10},{8,12},{10,14},{12,0},{14,2},{1,5},{3,7},... | collective-permute-start | bytes 884744 | tf_op jit(solution)/shard_map/ppermute | solution.py:231
  37.1 17.1 %copy-start.4 = (bf16[384,384]{1,0:T(8,128)(2,1)S(1)}, bf16[384,384]{1,0:T(8,128)(2,1)}, u32[]{:S(2)}) copy-start(bf16[384,384]{1,0:T(8,128)(2,1)} %copy-done.3) | copy-start | bytes 884740
  37.1 14.2 %all-to-all-start.1 = ((bf16[8,32,384]{2,1,0:T(8,128)(2,1)}), bf16[8,32,384]{2,1,0:T(8,128)(2,1)S(1)}, u32[]{:S(2)}, u32[]{:S(2)}) async-start(bf16[8,32,384]{2,1,0:T(8,128)(2,1)} %bitcast.4), calls=%async_computation.1 | async-start | bytes 393216 | tf_op jit(solution)/shard_map/all_to_all | solution.py:268
  42.4 6.8 %collective-permute-start.11 = (bf16[384,384]{1,0:T(8,128)(2,1)S(1)}, bf16[384,384]{1,0:T(8,128)(2,1)}, u32[]{:S(2)}, u32[]{:S(2)}) collective-permute-start(bf16[384,384]{1,0:T(8,128)(2,1)S(1)} %collective-permute-done.6.refs_10_), channel_id=1, source_target_pairs={{0,16},{16,0},{1,17},{17,1},{2,18},{18,2},{3,19},{19,3},{4,20},{20... | collective-permute-start | bytes 884744 | tf_op jit(solution)/shard_map/ppermute | solution.py:227
  43.3 7.4 %collective-permute-start.10 = (bf16[384,384]{1,0:T(8,128)(2,1)S(1)}, bf16[384,384]{1,0:T(8,128)(2,1)S(1)}, u32[]{:S(2)}, u32[]{:S(2)}) collective-permute-start(bf16[384,384]{1,0:T(8,128)(2,1)S(1)} %collective-permute-done.6.refs_10_), channel_id=1, source_target_pairs={{0,2},{2,0},{4,6},{6,4},{8,10},{10,8},{12,14},{14,12},{1,3},{3,1},... | collective-permute-start | bytes 884744 | tf_op jit(solution)/shard_map/ppermute | solution.py:223
  51.3 6.9 %collective-permute-start.13 = (bf16[384,384]{1,0:T(8,128)(2,1)}, bf16[384,384]{1,0:T(8,128)(2,1)S(1)}, u32[]{:S(2)}, u32[]{:S(2)}) collective-permute-start(bf16[384,384]{1,0:T(8,128)(2,1)} %collective-permute-done.11.refs_11_), channel_id=1, source_target_pairs={{0,2},{2,0},{4,6},{6,4},{8,10},{10,8},{12,14},{14,12},{1,3},{3,1},... | collective-permute-start | bytes 884744 | tf_op jit(solution)/shard_map/ppermute | solution.py:223
  52.9 6.7 %collective-permute-start.12 = (bf16[384,384]{1,0:T(8,128)(2,1)S(1)}, bf16[384,384]{1,0:T(8,128)(2,1)S(1)}, u32[]{:S(2)}, u32[]{:S(2)}) collective-permute-start(bf16[384,384]{1,0:T(8,128)(2,1)S(1)} %collective-permute-done.7.refs_0_), channel_id=1, source_target_pairs={{0,16},{16,0},{1,17},{17,1},{2,18},{18,2},{3,19},{19,3},{4,20},{20... | collective-permute-start | bytes 884744 | tf_op jit(solution)/shard_map/ppermute | solution.py:227
  55.1 4.5 %copy-start.6 = (bf16[384,384]{1,0:T(8,128)(2,1)S(1)}, bf16[384,384]{1,0:T(8,128)(2,1)}, u32[]{:S(2)}) copy-start(bf16[384,384]{1,0:T(8,128)(2,1)} %copy-done.5) | copy-start | bytes 884740
  57.4 2.8 %collective-permute-start.15 = (bf16[128,2304]{1,0:T(8,128)(2,1)S(1)}, bf16[128,2304]{1,0:T(8,128)(2,1)S(1)}, u32[]{:S(2)}, u32[]{:S(2)}) collective-permute-start(bf16[128,2304]{1,0:T(8,128)(2,1)S(1)} %get-tuple-element.42), channel_id=1, source_target_pairs={{0,1},{1,0},{2,3},{3,2},{4,5},{5,4},{6,7},{7,6},{8,9},{9,8},{10,11... | collective-permute-start | bytes 1769480 | tf_op jit(solution)/shard_map/ppermute | solution.py:235
  60.2 1.5 %collective-permute-start.14 = (bf16[128,768]{1,0:T(8,128)(2,1)S(1)}, bf16[128,768]{1,0:T(8,128)(2,1)S(1)}, u32[]{:S(2)}, u32[]{:S(2)}) collective-permute-start(bf16[128,768]{1,0:T(8,128)(2,1)S(1)} %get-tuple-element.40), channel_id=1, source_target_pairs={{0,1},{1,0},{2,3},{3,2},{4,5},{5,4},{6,7},{7,6},{8,9},{9,8},{10,11... | collective-permute-start | bytes 589832 | tf_op jit(solution)/shard_map/ppermute | solution.py:235
  (6 other events, 10.9 us)

commit v6 on v4

--- a/solution.py
+++ b/solution.py
@@ -12,7 +12,7 @@
 ANY = pl.BlockSpec(memory_space=pl.ANY)
 HBM = pl.BlockSpec(memory_space=pltpu.HBM)
 COSTS = {"pack": 5000, "spatial": 10000, "temporal": 5000, "join_first": 1, "join_last": 1, "project_first": 3000, "project_last": 5000, "project_whole": 20000}
-PARAMS = pltpu.CompilerParams(vmem_limit_bytes=16 * 1024 * 1024)
+PARAMS = pltpu.CompilerParams(vmem_limit_bytes=10 * 1024 * 1024)
 
 
 def head_of_rank(class_ref, kind, rank, heads):
@@ -77,7 +77,7 @@
     total = jnp.dot(
         weights.astype(jnp.bfloat16), values, preferred_element_type=jnp.float32
     )
-    return (total / denominator).astype(jnp.bfloat16)
+    return (total * (1.0 / denominator)).astype(jnp.bfloat16)
 
 
 def spatial_kernel(

time: 62.9 us -> 62.9 us (level)
  no operation moved by 1% of the time
where the time goes in v6:
time: 62.9 us; the launch traced here: 62.5 us
  starting transfers between devices  25.6 us (41%)
  waiting for transfers between devices  22 us (35%)
  Pallas kernels  10.3 us (16%)
  local copies, waits for them, and re-layouts  4.46 us (7%)
    ppermute x6, waiting for transfers between devices, swap_group(): return lax.ppermute(piece, 'groups', [(0, 1), (1, 0)])  14.7 us
    pallas_call x7, Pallas kernels, call(): pl.pallas_call(kernel, out_shape=outs, in_specs=ins, out_specs=jax.tree.m...  10.3 us
    all_to_all x2, starting transfers between devices, exchange(): lax.all_to_all(split, 'frame', split_axis=0, concat_axis=0, tiled=True)  8.44 us
    ppermute x6, starting transfers between devices, swap_group(): return lax.ppermute(piece, 'groups', [(0, 1), (1, 0)])  8.15 us
    ppermute x5, starting transfers between devices, swap_pair(): return lax.ppermute(piece, 'frame', [(i, i ^ 1) for i in range(8)])  6.01 us
    ppermute x3, waiting for transfers between devices, next_line(): return lax.ppermute(piece, 'frame', [(i, (i + 2) % 8) for i in range(8)])  3.51 us
    ppermute x5, waiting for transfers between devices, swap_pair(): return lax.ppermute(piece, 'frame', [(i, i ^ 1) for i in range(8)])  3.33 us
    unnamed x24, local copies, waits for them, and re-layouts  3.08 us
  transfers between devices with their start and end apart: 18, of which 9 were waited for; matrix products, arithmetic and copies ran while one was open for 0% of the time, Pallas kernels for 15%

profile of v6, /device:TPU:0, one launch (start us, length us, event | category | flops | bytes accessed | tf_op | source)
XLA Modules:
  0.0 62.5 jit_solution(8441753477523723356)
XLA Ops:
  0.0 1.2 %constant_dynamic-slice_fusion = (bf16[384,384]{1,0:T(8,128)(2,1)S(1)}, bf16[384,384]{1,0:T(8,128)(2,1)S(1)}) fusion(bf16[768,384]{1,0:T(8,128)(2,1)} %param.10, s32[]{:T(128)S(6)} %select_n.7, s32[]{:T(128)S(6)} %select_n.6), kind=kLoop, calls=%fused_computation | loop fusion | bytes 1179656 | tf_op jit(solution)/shard_map/dynamic_slice | solution.py:332
  1.2 3.0 %collective-permute-start.1 = (bf16[384,384]{1,0:T(8,128)(2,1)S(1)}, bf16[384,384]{1,0:T(8,128)(2,1)S(1)}, u32[]{:S(2)}, u32[]{:S(2)}) collective-permute-start(bf16[384,384]{1,0:T(8,128)(2,1)S(1)} %get-tuple-element.44.refs_0_), channel_id=1, source_target_pairs={{0,2},{2,0},{4,6},{6,4},{8,10},{10,8},{12,14},{14,12},{1,3},{3,1},... | collective-permute-start | bytes 884744 | tf_op jit(solution)/shard_map/ppermute | solution.py:224
  4.2 1.6 %collective-permute-start = (bf16[384,384]{1,0:T(8,128)(2,1)S(1)}, bf16[384,384]{1,0:T(8,128)(2,1)S(1)}, u32[]{:S(2)}, u32[]{:S(2)}) collective-permute-start(bf16[384,384]{1,0:T(8,128)(2,1)S(1)} %get-tuple-element.44.refs_0_), channel_id=1, source_target_pairs={{0,4},{2,6},{4,8},{6,10},{8,12},{10,14},{12,0},{14,2},{1,5},{3,7},... | collective-permute-start | bytes 884744 | tf_op jit(solution)/shard_map/ppermute | solution.py:232
  5.8 1.6 %shard_map.74 = bf16[256,1152]{1,0:T(8,128)(2,1)} custom-call(s32[6]{0:T(128)S(1)} %copy-done.7, bf16[256,768]{1,0:T(8,128)(2,1)S(1)} %copy-done, bf16[256,768]{1,0:T(8,128)(2,1)S(1)} %copy-done.1, bf16[256,768]{1,0:T(8,128)(2,1)S(1)} %copy-done.2), custom_call_target="tpu_custom_call" | custom-call | flops 5000000000 | bytes 1000 | tf_op jit(solution)/shard_map/pallas_call | solution.py:256
  7.4 3.9 %all-to-all-start = ((bf16[8,32,1152]{2,1,0:T(8,128)(2,1)}), bf16[8,32,1152]{2,1,0:T(8,128)(2,1)S(1)}, u32[]{:S(2)}, u32[]{:S(2)}) async-start(bf16[8,32,1152]{2,1,0:T(8,128)(2,1)} %bitcast.2), calls=%async_computation | async-start | bytes 1179648 | tf_op jit(solution)/shard_map/all_to_all | solution.py:269
  11.5 3.2 %collective-permute-done.refs_4_ = bf16[384,384]{1,0:T(8,128)(2,1)S(1)} collective-permute-done((bf16[384,384]{1,0:T(8,128)(2,1)S(1)}, bf16[384,384]{1,0:T(8,128)(2,1)S(1)}, u32[]{:S(2)}, u32[]{:S(2)}) %collective-permute-start) | collective-permute-done | bytes 294944 | tf_op jit(solution)/shard_map/ppermute | solution.py:232
  15.1 1.5 %collective-permute-start.3 = (bf16[384,384]{1,0:T(8,128)(2,1)S(1)}, bf16[384,384]{1,0:T(8,128)(2,1)S(1)}, u32[]{:S(2)}, u32[]{:S(2)}) collective-permute-start(bf16[384,384]{1,0:T(8,128)(2,1)S(1)} %collective-permute-done.refs_4_), channel_id=1, source_target_pairs={{0,16},{16,0},{1,17},{17,1},{2,18},{18,2},{3,19},{19,3},{4,20},{20... | collective-permute-start | bytes 884744 | tf_op jit(solution)/shard_map/ppermute | solution.py:228
  17.2 2.2 %shard_map.73.spatial_ref = bf16[256,384]{1,0:T(8,128)(2,1)S(1)} custom-call(s32[6]{0:T(128)S(1)} %copy-done.7, s32[6,8]{1,0:T(8,128)S(1)} %copy.9.lists_ref, s32[6,4]{1,0:T(8,128)S(1)} %copy.10.counts_ref, bf16[256,768]{1,0:T(8,128)(2,1)S(1)} %copy-done, bf16[256,768]{1,0:T(8,128)(2,1)S(1)} %copy-done.1, bf16[256,768]{1,0:T(8,128)(2,1)S(1)} %copy-done.2), custom_call_target="tpu_custom_call" | custom-call | flops 10000000000 | bytes 1000 | tf_op jit(solution)/shard_map/pallas_call | solution.py:256
  20.1 8.5 %collective-permute-done.4.refs_3_ = bf16[384,384]{1,0:T(8,128)(2,1)S(1)} collective-permute-done((bf16[384,384]{1,0:T(8,128)(2,1)S(1)}, bf16[384,384]{1,0:T(8,128)(2,1)S(1)}, u32[]{:S(2)}, u32[]{:S(2)}) %collective-permute-start.4) | collective-permute-done | bytes 294944 | tf_op jit(solution)/shard_map/ppermute | solution.py:228
  29.2 1.5 %collective-permute-start.9 = (bf16[384,384]{1,0:T(8,128)(2,1)}, bf16[384,384]{1,0:T(8,128)(2,1)S(1)}, u32[]{:S(2)}, u32[]{:S(2)}) collective-permute-start(bf16[384,384]{1,0:T(8,128)(2,1)} %collective-permute-done.2.refs_6_), channel_id=1, source_target_pairs={{0,16},{16,0},{1,17},{17,1},{2,18},{18,2},{3,19},{19,3},{4,20},{20... | collective-permute-start | bytes 884744 | tf_op jit(solution)/shard_map/ppermute | solution.py:228
  30.8 1.5 %collective-permute-start.8 = (bf16[384,384]{1,0:T(8,128)(2,1)S(1)}, bf16[384,384]{1,0:T(8,128)(2,1)S(1)}, u32[]{:S(2)}, u32[]{:S(2)}) collective-permute-start(bf16[384,384]{1,0:T(8,128)(2,1)S(1)} %collective-permute-done.5.refs_8_), channel_id=1, source_target_pairs={{0,16},{16,0},{1,17},{17,1},{2,18},{18,2},{3,19},{19,3},{4,20},{20... | collective-permute-start | bytes 884744 | tf_op jit(solution)/shard_map/ppermute | solution.py:228
  32.3 1.5 %collective-permute-start.7 = (bf16[384,384]{1,0:T(8,128)(2,1)S(1)}, bf16[384,384]{1,0:T(8,128)(2,1)S(1)}, u32[]{:S(2)}, u32[]{:S(2)}) collective-permute-start(bf16[384,384]{1,0:T(8,128)(2,1)S(1)} %collective-permute-done.5.refs_8_), channel_id=1, source_target_pairs={{0,2},{2,0},{4,6},{6,4},{8,10},{10,8},{12,14},{14,12},{1,3},{3,1},... | collective-permute-start | bytes 884744 | tf_op jit(solution)/shard_map/ppermute | solution.py:224
  34.7 2.1 %shard_map.75 = bf16[256,384]{1,0:T(8,128)(2,1)} custom-call(s32[6]{0:T(128)S(1)} %copy-done.7, s32[6,8]{1,0:T(8,128)S(1)} %copy.9.lists_ref, s32[6,4]{1,0:T(8,128)S(1)} %copy.10.counts_ref, bf16[256,1152]{1,0:T(8,128)(2,1)S(1)} %bitcast.6), custom_call_target="tpu_custom_call" | custom-call | flops 5000000000 | bytes 1000 | tf_op jit(solution)/shard_map/pallas_call | solution.py:256
  36.8 4.6 %all-to-all-start.1 = ((bf16[8,32,384]{2,1,0:T(8,128)(2,1)}), bf16[8,32,384]{2,1,0:T(8,128)(2,1)S(1)}, u32[]{:S(2)}, u32[]{:S(2)}) async-start(bf16[8,32,384]{2,1,0:T(8,128)(2,1)} %bitcast.4), calls=%async_computation.1 | async-start | bytes 393216 | tf_op jit(solution)/shard_map/all_to_all | solution.py:269
  42.4 1.9 %collective-permute-start.11 = (bf16[384,384]{1,0:T(8,128)(2,1)S(1)}, bf16[384,384]{1,0:T(8,128)(2,1)}, u32[]{:S(2)}, u32[]{:S(2)}) collective-permute-start(bf16[384,384]{1,0:T(8,128)(2,1)S(1)} %collective-permute-done.6.refs_10_), channel_id=1, source_target_pairs={{0,16},{16,0},{1,17},{17,1},{2,18},{18,2},{3,19},{19,3},{4,20},{20... | collective-permute-start | bytes 884744 | tf_op jit(solution)/shard_map/ppermute | solution.py:228
  44.6 4.6 %collective-permute-done.11.refs_11_ = bf16[384,384]{1,0:T(8,128)(2,1)} collective-permute-done((bf16[384,384]{1,0:T(8,128)(2,1)S(1)}, bf16[384,384]{1,0:T(8,128)(2,1)}, u32[]{:S(2)}, u32[]{:S(2)}) %collective-permute-start.11) | collective-permute-done | bytes 294944 | tf_op jit(solution)/shard_map/ppermute | solution.py:228
  49.2 2.0 %collective-permute-done.10.refs_2_ = bf16[384,384]{1,0:T(8,128)(2,1)S(1)} collective-permute-done((bf16[384,384]{1,0:T(8,128)(2,1)S(1)}, bf16[384,384]{1,0:T(8,128)(2,1)S(1)}, u32[]{:S(2)}, u32[]{:S(2)}) %collective-permute-start.10) | collective-permute-done | bytes 294944 | tf_op jit(solution)/shard_map/ppermute | solution.py:224
  52.0 1.1 %collective-permute-start.13 = (bf16[384,384]{1,0:T(8,128)(2,1)}, bf16[384,384]{1,0:T(8,128)(2,1)S(1)}, u32[]{:S(2)}, u32[]{:S(2)}) collective-permute-start(bf16[384,384]{1,0:T(8,128)(2,1)} %collective-permute-done.11.refs_11_), channel_id=1, source_target_pairs={{0,2},{2,0},{4,6},{6,4},{8,10},{10,8},{12,14},{14,12},{1,3},{3,1},... | collective-permute-start | bytes 884744 | tf_op jit(solution)/shard_map/ppermute | solution.py:224
  53.1 1.2 %collective-permute-start.12 = (bf16[384,384]{1,0:T(8,128)(2,1)S(1)}, bf16[384,384]{1,0:T(8,128)(2,1)S(1)}, u32[]{:S(2)}, u32[]{:S(2)}) collective-permute-start(bf16[384,384]{1,0:T(8,128)(2,1)S(1)} %collective-permute-done.7.refs_0_), channel_id=1, source_target_pairs={{0,16},{16,0},{1,17},{17,1},{2,18},{18,2},{3,19},{19,3},{4,20},{20... | collective-permute-start | bytes 884744 | tf_op jit(solution)/shard_map/ppermute | solution.py:228
  54.3 0.9 %copy-done.9 = bf16[256,384]{1,0:T(8,128)(2,1)S(1)} copy-done((bf16[256,384]{1,0:T(8,128)(2,1)S(1)}, bf16[256,384]{1,0:T(8,128)(2,1)}, u32[]{:S(2)}) %copy-start.9) | copy-done | bytes 196632
  55.2 2.3 %shard_map.76 = (bf16[128,2304]{1,0:T(8,128)(2,1)S(1)}, bf16[128,2304]{1,0:T(8,128)(2,1)S(1)}, bf16[256,768]{1,0:T(8,128)(2,1)S(1)}) custom-call(s32[6]{0:T(128)S(1)} %copy-done.7, bf16[256,384]{1,0:T(8,128)(2,1)S(1)} %copy-done.9, bf16[256,384]{1,0:T(8,128)(2,1)S(1)} %bitcast.7, bf16[384,384]{1,0:T(8,128)(2,1)S(1)} %get-tuple-element.44.refs_0_, ...), custom_call_target="tpu_custom_call" | custom-call | flops 3000000000 | bytes 1000 | tf_op jit(solution)/shard_map/pallas_call | solution.py:256
  57.6 1.3 %collective-permute-done.13.refs_3_ = bf16[384,384]{1,0:T(8,128)(2,1)S(1)} collective-permute-done((bf16[384,384]{1,0:T(8,128)(2,1)}, bf16[384,384]{1,0:T(8,128)(2,1)S(1)}, u32[]{:S(2)}, u32[]{:S(2)}) %collective-permute-start.13) | collective-permute-done | bytes 294944 | tf_op jit(solution)/shard_map/ppermute | solution.py:224
  58.9 0.9 %collective-permute-done.12.refs_1_ = bf16[384,384]{1,0:T(8,128)(2,1)S(1)} collective-permute-done((bf16[384,384]{1,0:T(8,128)(2,1)S(1)}, bf16[384,384]{1,0:T(8,128)(2,1)S(1)}, u32[]{:S(2)}, u32[]{:S(2)}) %collective-permute-start.12) | collective-permute-done | bytes 294944 | tf_op jit(solution)/shard_map/ppermute | solution.py:228
  60.4 0.9 %shard_map.78.joined_ref = bf16[128,3072]{1,0:T(8,128)(2,1)} custom-call(bf16[128,2304]{1,0:T(8,128)(2,1)S(1)} %get-tuple-element.41.refs_0_, bf16[128,2304]{1,0:T(8,128)(2,1)S(1)} %collective-permute-done.15.refs_1_), custom_call_target="tpu_custom_call" | custom-call | flops 1000000 | bytes 1000 | tf_op jit(solution)/shard_map/pallas_call | solution.py:256
  (46 shorter events, 7.4 us)
Async XLA Ops:
  0.0 5.8 %copy-start = (bf16[256,768]{1,0:T(8,128)(2,1)S(1)}, bf16[256,768]{1,0:T(8,128)(2,1)}, u32[]{:S(2)}) copy-start(bf16[256,768]{1,0:T(8,128)(2,1)} %q_ref.3) | copy-start | bytes 1179652
  0.0 5.8 %copy-start.1 = (bf16[256,768]{1,0:T(8,128)(2,1)S(1)}, bf16[256,768]{1,0:T(8,128)(2,1)}, u32[]{:S(2)}) copy-start(bf16[256,768]{1,0:T(8,128)(2,1)} %k_ref.3) | copy-start | bytes 1179652
  0.0 5.8 %copy-start.2 = (bf16[256,768]{1,0:T(8,128)(2,1)S(1)}, bf16[256,768]{1,0:T(8,128)(2,1)}, u32[]{:S(2)}) copy-start(bf16[256,768]{1,0:T(8,128)(2,1)} %v_ref.3) | copy-start | bytes 1179652
  1.2 4.6 %copy-start.7 = (s32[6]{0:T(128)S(1)}, s32[6]{0:T(128)}, u32[]{:S(2)}) copy-start(s32[6]{0:T(128)} %class_ref.7) | copy-start | bytes 76
  1.2 10.3 %collective-permute-start.1 = (bf16[384,384]{1,0:T(8,128)(2,1)S(1)}, bf16[384,384]{1,0:T(8,128)(2,1)S(1)}, u32[]{:S(2)}, u32[]{:S(2)}) collective-permute-start(bf16[384,384]{1,0:T(8,128)(2,1)S(1)} %get-tuple-element.44.refs_0_), channel_id=1, source_target_pairs={{0,2},{2,0},{4,6},{6,4},{8,10},{10,8},{12,14},{14,12},{1,3},{3,1},... | collective-permute-start | bytes 884744 | tf_op jit(solution)/shard_map/ppermute | solution.py:224
  4.2 10.4 %collective-permute-start = (bf16[384,384]{1,0:T(8,128)(2,1)S(1)}, bf16[384,384]{1,0:T(8,128)(2,1)S(1)}, u32[]{:S(2)}, u32[]{:S(2)}) collective-permute-start(bf16[384,384]{1,0:T(8,128)(2,1)S(1)} %get-tuple-element.44.refs_0_), channel_id=1, source_target_pairs={{0,4},{2,6},{4,8},{6,10},{8,12},{10,14},{12,0},{14,2},{1,5},{3,7},... | collective-permute-start | bytes 884744 | tf_op jit(solution)/shard_map/ppermute | solution.py:232
  7.4 27.2 %all-to-all-start = ((bf16[8,32,1152]{2,1,0:T(8,128)(2,1)}), bf16[8,32,1152]{2,1,0:T(8,128)(2,1)S(1)}, u32[]{:S(2)}, u32[]{:S(2)}) async-start(bf16[8,32,1152]{2,1,0:T(8,128)(2,1)} %bitcast.2), calls=%async_computation | async-start | bytes 1179648 | tf_op jit(solution)/shard_map/all_to_all | solution.py:269
  14.7 16.1 %collective-permute-start.5 = (bf16[384,384]{1,0:T(8,128)(2,1)S(1)}, bf16[384,384]{1,0:T(8,128)(2,1)S(1)}, u32[]{:S(2)}, u32[]{:S(2)}) collective-permute-start(bf16[384,384]{1,0:T(8,128)(2,1)S(1)} %collective-permute-done.refs_4_), channel_id=1, source_target_pairs={{0,4},{2,6},{4,8},{6,10},{8,12},{10,14},{12,0},{14,2},{1,5},{3,7},... | collective-permute-start | bytes 884744 | tf_op jit(solution)/shard_map/ppermute | solution.py:232
  15.1 14.1 %collective-permute-start.3 = (bf16[384,384]{1,0:T(8,128)(2,1)S(1)}, bf16[384,384]{1,0:T(8,128)(2,1)S(1)}, u32[]{:S(2)}, u32[]{:S(2)}) collective-permute-start(bf16[384,384]{1,0:T(8,128)(2,1)S(1)} %collective-permute-done.refs_4_), channel_id=1, source_target_pairs={{0,16},{16,0},{1,17},{17,1},{2,18},{18,2},{3,19},{19,3},{4,20},{20... | collective-permute-start | bytes 884744 | tf_op jit(solution)/shard_map/ppermute | solution.py:228
  16.6 12.6 %collective-permute-start.2 = (bf16[384,384]{1,0:T(8,128)(2,1)S(1)}, bf16[384,384]{1,0:T(8,128)(2,1)}, u32[]{:S(2)}, u32[]{:S(2)}) collective-permute-start(bf16[384,384]{1,0:T(8,128)(2,1)S(1)} %collective-permute-done.refs_4_), channel_id=1, source_target_pairs={{0,2},{2,0},{4,6},{6,4},{8,10},{10,8},{12,14},{14,12},{1,3},{3,1},... | collective-permute-start | bytes 884744 | tf_op jit(solution)/shard_map/ppermute | solution.py:224
  16.7 11.8 %collective-permute-start.4 = (bf16[384,384]{1,0:T(8,128)(2,1)S(1)}, bf16[384,384]{1,0:T(8,128)(2,1)S(1)}, u32[]{:S(2)}, u32[]{:S(2)}) collective-permute-start(bf16[384,384]{1,0:T(8,128)(2,1)S(1)} %collective-permute-done.1.refs_2_), channel_id=1, source_target_pairs={{0,16},{16,0},{1,17},{17,1},{2,18},{18,2},{3,19},{19,3},{4,20},{20... | collective-permute-start | bytes 884744 | tf_op jit(solution)/shard_map/ppermute | solution.py:228
  29.2 13.1 %collective-permute-start.9 = (bf16[384,384]{1,0:T(8,128)(2,1)}, bf16[384,384]{1,0:T(8,128)(2,1)S(1)}, u32[]{:S(2)}, u32[]{:S(2)}) collective-permute-start(bf16[384,384]{1,0:T(8,128)(2,1)} %collective-permute-done.2.refs_6_), channel_id=1, source_target_pairs={{0,16},{16,0},{1,17},{17,1},{2,18},{18,2},{3,19},{19,3},{4,20},{20... | collective-permute-start | bytes 884744 | tf_op jit(solution)/shard_map/ppermute | solution.py:228
  30.8 11.2 %collective-permute-start.8 = (bf16[384,384]{1,0:T(8,128)(2,1)S(1)}, bf16[384,384]{1,0:T(8,128)(2,1)S(1)}, u32[]{:S(2)}, u32[]{:S(2)}) collective-permute-start(bf16[384,384]{1,0:T(8,128)(2,1)S(1)} %collective-permute-done.5.refs_8_), channel_id=1, source_target_pairs={{0,16},{16,0},{1,17},{17,1},{2,18},{18,2},{3,19},{19,3},{4,20},{20... | collective-permute-start | bytes 884744 | tf_op jit(solution)/shard_map/ppermute | solution.py:228
  32.3 9.7 %collective-permute-start.7 = (bf16[384,384]{1,0:T(8,128)(2,1)S(1)}, bf16[384,384]{1,0:T(8,128)(2,1)S(1)}, u32[]{:S(2)}, u32[]{:S(2)}) collective-permute-start(bf16[384,384]{1,0:T(8,128)(2,1)S(1)} %collective-permute-done.5.refs_8_), channel_id=1, source_target_pairs={{0,2},{2,0},{4,6},{6,4},{8,10},{10,8},{12,14},{14,12},{1,3},{3,1},... | collective-permute-start | bytes 884744 | tf_op jit(solution)/shard_map/ppermute | solution.py:224
  33.8 8.5 %collective-permute-start.6 = (bf16[384,384]{1,0:T(8,128)(2,1)S(1)}, bf16[384,384]{1,0:T(8,128)(2,1)S(1)}, u32[]{:S(2)}, u32[]{:S(2)}) collective-permute-start(bf16[384,384]{1,0:T(8,128)(2,1)S(1)} %collective-permute-done.5.refs_8_), channel_id=1, source_target_pairs={{0,4},{2,6},{4,8},{6,10},{8,12},{10,14},{12,0},{14,2},{1,5},{3,7},... | collective-permute-start | bytes 884744 | tf_op jit(solution)/shard_map/ppermute | solution.py:232
  36.8 17.5 %copy-start.4 = (bf16[384,384]{1,0:T(8,128)(2,1)S(1)}, bf16[384,384]{1,0:T(8,128)(2,1)}, u32[]{:S(2)}) copy-start(bf16[384,384]{1,0:T(8,128)(2,1)} %copy-done.3) | copy-start | bytes 884740
  36.8 15.1 %all-to-all-start.1 = ((bf16[8,32,384]{2,1,0:T(8,128)(2,1)}), bf16[8,32,384]{2,1,0:T(8,128)(2,1)S(1)}, u32[]{:S(2)}, u32[]{:S(2)}) async-start(bf16[8,32,384]{2,1,0:T(8,128)(2,1)} %bitcast.4), calls=%async_computation.1 | async-start | bytes 393216 | tf_op jit(solution)/shard_map/all_to_all | solution.py:269
  42.4 6.8 %collective-permute-start.11 = (bf16[384,384]{1,0:T(8,128)(2,1)S(1)}, bf16[384,384]{1,0:T(8,128)(2,1)}, u32[]{:S(2)}, u32[]{:S(2)}) collective-permute-start(bf16[384,384]{1,0:T(8,128)(2,1)S(1)} %collective-permute-done.6.refs_10_), channel_id=1, source_target_pairs={{0,16},{16,0},{1,17},{17,1},{2,18},{18,2},{3,19},{19,3},{4,20},{20... | collective-permute-start | bytes 884744 | tf_op jit(solution)/shard_map/ppermute | solution.py:228
  44.2 7.0 %collective-permute-start.10 = (bf16[384,384]{1,0:T(8,128)(2,1)S(1)}, bf16[384,384]{1,0:T(8,128)(2,1)S(1)}, u32[]{:S(2)}, u32[]{:S(2)}) collective-permute-start(bf16[384,384]{1,0:T(8,128)(2,1)S(1)} %collective-permute-done.6.refs_10_), channel_id=1, source_target_pairs={{0,2},{2,0},{4,6},{6,4},{8,10},{10,8},{12,14},{14,12},{1,3},{3,1},... | collective-permute-start | bytes 884744 | tf_op jit(solution)/shard_map/ppermute | solution.py:224
  52.0 6.9 %collective-permute-start.13 = (bf16[384,384]{1,0:T(8,128)(2,1)}, bf16[384,384]{1,0:T(8,128)(2,1)S(1)}, u32[]{:S(2)}, u32[]{:S(2)}) collective-permute-start(bf16[384,384]{1,0:T(8,128)(2,1)} %collective-permute-done.11.refs_11_), channel_id=1, source_target_pairs={{0,2},{2,0},{4,6},{6,4},{8,10},{10,8},{12,14},{14,12},{1,3},{3,1},... | collective-permute-start | bytes 884744 | tf_op jit(solution)/shard_map/ppermute | solution.py:224
  53.1 6.7 %collective-permute-start.12 = (bf16[384,384]{1,0:T(8,128)(2,1)S(1)}, bf16[384,384]{1,0:T(8,128)(2,1)S(1)}, u32[]{:S(2)}, u32[]{:S(2)}) collective-permute-start(bf16[384,384]{1,0:T(8,128)(2,1)S(1)} %collective-permute-done.7.refs_0_), channel_id=1, source_target_pairs={{0,16},{16,0},{1,17},{17,1},{2,18},{18,2},{3,19},{19,3},{4,20},{20... | collective-permute-start | bytes 884744 | tf_op jit(solution)/shard_map/ppermute | solution.py:228
  55.2 4.6 %copy-start.6 = (bf16[384,384]{1,0:T(8,128)(2,1)S(1)}, bf16[384,384]{1,0:T(8,128)(2,1)}, u32[]{:S(2)}) copy-start(bf16[384,384]{1,0:T(8,128)(2,1)} %copy-done.5) | copy-start | bytes 884740
  57.5 2.9 %collective-permute-start.15 = (bf16[128,2304]{1,0:T(8,128)(2,1)S(1)}, bf16[128,2304]{1,0:T(8,128)(2,1)S(1)}, u32[]{:S(2)}, u32[]{:S(2)}) collective-permute-start(bf16[128,2304]{1,0:T(8,128)(2,1)S(1)} %get-tuple-element.42), channel_id=1, source_target_pairs={{0,1},{1,0},{2,3},{3,2},{4,5},{5,4},{6,7},{7,6},{8,9},{9,8},{10,11... | collective-permute-start | bytes 1769480 | tf_op jit(solution)/shard_map/ppermute | solution.py:236
  60.3 1.5 %collective-permute-start.14 = (bf16[128,768]{1,0:T(8,128)(2,1)S(1)}, bf16[128,768]{1,0:T(8,128)(2,1)S(1)}, u32[]{:S(2)}, u32[]{:S(2)}) collective-permute-start(bf16[128,768]{1,0:T(8,128)(2,1)S(1)} %get-tuple-element.40), channel_id=1, source_target_pairs={{0,1},{1,0},{2,3},{3,2},{4,5},{5,4},{6,7},{7,6},{8,9},{9,8},{10,11... | collective-permute-start | bytes 589832 | tf_op jit(solution)/shard_map/ppermute | solution.py:236
  (6 other events, 10.9 us)
